TPU v7x, 32 devices: a whole 2x2x4 slice. The times are simulated.
32 devices in a mesh: fsdp: 2 (over y), ctx: 4 (over z), tp: 4 (over x, core).
Axes of the slice: x: 2, y: 2, z: 4, core: 2. Of those that a mesh axis runs over, the one named last changes fastest.
Arguments:
- tokens: bfloat16 [4, 512, 768], P('fsdp', 'ctx'), may hold values from -10 to 10
- lengths: int32 [4, 6], P('fsdp'), may hold values from 1 to 320, 512 in all within a row
- qkv_weight: bfloat16 [3, 768, 768], P(None, ('fsdp', 'ctx'), 'tp')
- qv_bias: bfloat16 [2, 12, 64], P(None, 'tp', ('fsdp', 'ctx')), may hold values from -3 to 3
- out_weight: bfloat16 [768, 768], P('tp', ('fsdp', 'ctx')), may hold values from -0.875 to 0.875
- out_bias: bfloat16 [768], P(('fsdp', 'ctx')), may hold values from -3 to 3
- norm1_gain: bfloat16 [768], P(('fsdp', 'ctx')), may hold values from 0.099609375 to 1.8984375
- norm1_bias: bfloat16 [768], P(('fsdp', 'ctx')), may hold values from -3 to 3
- up_weight: bfloat16 [768, 3072], P(('fsdp', 'ctx'), 'tp'), may hold values from -0.21875 to 0.21875
- up_bias: bfloat16 [48, 64], P('tp', ('fsdp', 'ctx')), may hold values from -3 to 3
- down_weight: bfloat16 [3072, 768], P('tp', ('fsdp', 'ctx')), may hold values from -0.109375 to 0.109375
- down_bias: bfloat16 [768], P(('fsdp', 'ctx')), may hold values from -3 to 3
- norm2_gain: bfloat16 [768], P(('fsdp', 'ctx')), may hold values from 0.099609375 to 1.8984375
- norm2_bias: bfloat16 [768], P(('fsdp', 'ctx')), may hold values from -3 to 3
- cotangent: bfloat16 [4, 512, 768], P('fsdp', 'ctx'), may hold values from -6 to 6
Outputs:
- output: bfloat16 [4, 512, 768], P('fsdp', 'ctx')
- tokens_grad: bfloat16 [4, 512, 768], P('fsdp', 'ctx')
- qkv_weight_grad: float32 [3, 768, 768], P(None, ('fsdp', 'ctx'), 'tp')
- qv_bias_grad: float32 [2, 12, 64], P(None, 'tp', ('fsdp', 'ctx'))
- out_weight_grad: float32 [768, 768], P('tp', ('fsdp', 'ctx'))
- out_bias_grad: float32 [768], P(('fsdp', 'ctx'))
- norm1_gain_grad: float32 [768], P(('fsdp', 'ctx'))
- norm1_bias_grad: float32 [768], P(('fsdp', 'ctx'))
- up_weight_grad: float32 [768, 3072], P(('fsdp', 'ctx'), 'tp')
- up_bias_grad: float32 [48, 64], P('tp', ('fsdp', 'ctx'))
- down_weight_grad: float32 [3072, 768], P('tp', ('fsdp', 'ctx'))
- down_bias_grad: float32 [768], P(('fsdp', 'ctx'))
- norm2_gain_grad: float32 [768], P(('fsdp', 'ctx'))
- norm2_bias_grad: float32 [768], P(('fsdp', 'ctx'))
Inputs may be any that keep to these rules, and one draw needn't show every extreme that they name: The lengths of each sequence sum to 512, and the longest document of every sequence has exactly 320 tokens.
All inputs are finite; a program needn't handle non-finite values.
Results may differ from a plain program's by a relative error of at most 0.038.
Values may be sent and summed in bfloat16 or wider, within the bound.
No kernel may reach another device: no remote copies, remote signals or barrier semaphores. Data moves between devices by JAX's collectives and lax.ppermute only.
A program may use at most 64 MiB of HBM per device.

v0:
```python
import functools
import math

import jax
import jax.numpy as jnp
from jax import lax
from jax.experimental import pallas as pl
from jax.experimental.pallas import tpu as pltpu
from jax.sharding import PartitionSpec as P


EPSILON = 1e-12
BF = jnp.bfloat16
F32 = jnp.float32
TAIL = 8


def norm_rows(hidden):
    center = hidden - jnp.mean(hidden, axis=-1, keepdims=True)
    inverse = lax.rsqrt(jnp.mean(center * center, axis=-1, keepdims=True) + EPSILON)
    return (center * inverse, inverse)


def norm_back(grad_norm, normed, inverse):
    first_mean = jnp.mean(grad_norm, axis=-1, keepdims=True)
    second_mean = jnp.mean(grad_norm * normed, axis=-1, keepdims=True)
    return inverse * (grad_norm - first_mean - normed * second_mean)


def gelu_parts(pre_act):
    cdf_part = 0.5 * (1.0 + lax.erf(pre_act * (1.0 / math.sqrt(2.0))))
    density = jnp.exp(-0.5 * pre_act * pre_act) * (1.0 / math.sqrt(2.0 * math.pi))
    return (pre_act * cdf_part, cdf_part + pre_act * density)


def dot(left, right, over_left, over_right):
    return lax.dot_general(
        left, right, (((over_left,), (over_right,)), ((), ())), preferred_element_type=F32
    )


def ring(value, axis, step):
    size = lax.axis_size(axis)
    return lax.ppermute(value, axis, [(i, (i + step) % size) for i in range(size)])


def flip(value, axis, bit):
    size = lax.axis_size(axis)
    return lax.ppermute(value, axis, [(i, i ^ bit) for i in range(size)])


def near_first(size):
    return sorted(range(1, size), key=lambda k: min(k, size - k))


def call(kernel, outs, args, smem=(), scratch=(), flops=0):
    size = sum(math.prod(s) * jnp.dtype(t).itemsize for s, t in outs)
    size += sum(a.size * a.dtype.itemsize for a in args)
    vmem = pl.BlockSpec(memory_space=pltpu.VMEM)
    table = pl.BlockSpec(memory_space=pltpu.SMEM)
    return pallas(kernel, outs, args, smem, scratch, flops, size, vmem, table)


def pallas(kernel, outs, args, smem, scratch, flops, size, vmem, table):
    return pl.pallas_call(
        kernel,
        out_shape=tuple(jax.ShapeDtypeStruct(s, t) for s, t in outs),
        in_specs=[table] * len(smem) + [vmem] * len(args),
        out_specs=tuple(vmem for _ in outs),
        scratch_shapes=list(scratch),
        cost_estimate=pl.CostEstimate(flops=flops, bytes_accessed=size, transcendentals=0),
    )(*smem, *args)


def lanes(low, high, width):
    at = lax.broadcasted_iota(jnp.int32, (1, width), 1)
    return (at >= low) & (at < high)


def aligned(start, size):
    return pl.ds(pl.multiple_of(start, size), size)


class Sizes:
    def __init__(self, tokens, qv_bias, up_weight):
        self.seqs, self.local, self.width = tokens.shape
        self.rows = self.seqs * self.local
        self.fsdp, self.ctx, self.tp = (lax.axis_size(a) for a in ("fsdp", "ctx", "tp"))
        self.blocks = self.fsdp * self.ctx
        self.shard = self.width // self.blocks
        self.heads, self.piece = qv_bias.shape[1:]
        self.head = self.piece * self.blocks
        self.inner = self.heads * self.head
        self.pair = 2 * self.inner
        self.hidden = up_weight.shape[1]
        self.total = self.local * self.ctx
        self.half = self.rows // 2
        self.scale = 1.0 / math.sqrt(self.head)
        self.direct = self.fsdp == 2 and self.shard % 16 == 0


def attention_kernel(z, order, masks, *refs):
    (meta, lengths), refs = refs[:2], refs[2:]
    count = z.blocks if z.direct else 1
    blocks, refs = refs[:count], refs[count:]
    own, refs = refs[0], refs[1:]
    pieces, refs = refs[: len(masks)], refs[len(masks) :]
    mixed, small, every, keys, query, probs, att, kept, sent = refs[:9]
    part = refs[9]
    row, col, lane = meta[0], meta[1], meta[2]
    if z.direct:
        places = block_places(z, order, row, col)
        total = jnp.zeros((TAIL, z.width), F32)
        for block, place in zip(blocks, places):
            mixed[aligned(place * z.shard, z.shard), :] = block[: z.shard, :]
            total = total + block[z.shard :, :].astype(F32)
        small[...] = total
    else:
        mixed[...] = blocks[0][: z.width, :]
        small[...] = blocks[0][z.width :, :].astype(F32)
    every[col] = own[...]
    share = z.rows // z.tp
    for at, step in enumerate(order):
        source = lax.rem(col - step + z.ctx, z.ctx)
        for which, mask in enumerate(masks):
            spot = jnp.bitwise_xor(lane, mask) * share
            every[source, aligned(spot, share), :] = pieces[which][at]
    b_q = jnp.where(lanes(0, z.inner, z.pair), small[7:8, : z.pair], 0.0)
    b_kv = jnp.where(lanes(z.inner, z.pair, z.pair), small[7:8, : z.pair], 0.0)

    @pl.loop(0, z.ctx)
    def _(at):
        both = dot(every[at], mixed[:, z.pair :], 1, 0) + b_kv
        both = both.astype(BF)
        for seq in range(z.seqs):
            piece = both[seq * z.local : (seq + 1) * z.local]
            keys[seq, aligned(at * z.local, z.local), :] = piece

    flat = dot(own[...], mixed[:, : z.pair], 1, 0) + b_q
    query[...] = jnp.where(lanes(0, z.inner, z.pair), flat, 0.0).astype(BF)
    docs = lengths.shape[1]
    key_at = lax.broadcasted_iota(jnp.int32, (1, z.total), 1)
    query_at = lax.broadcasted_iota(jnp.int32, (z.local, 1), 0) + col * z.local
    for seq in range(z.seqs):
        key_label = jnp.zeros((1, z.total), jnp.int32)
        query_label = jnp.zeros((z.local, 1), jnp.int32)
        end = 0
        for doc in range(docs):
            end = end + lengths[seq, doc]
            key_label = key_label + jnp.where(key_at >= end, 1, 0)
            query_label = query_label + jnp.where(query_at >= end, 1, 0)
        same = query_label == key_label
        flat = query[seq * z.local : (seq + 1) * z.local, :]
        result = jnp.zeros((z.local, z.pair), F32)
        for head in range(z.heads):
            low = head * z.head
            chosen = jnp.where(lanes(low, low + z.head, z.pair), flat, jnp.zeros_like(flat))
            scores = dot(chosen, keys[seq], 1, 1) * z.scale
            scores = jnp.where(same, scores, -1e30)
            weights = jnp.exp(scores - jnp.max(scores, axis=1, keepdims=True))
            chance = weights * (1.0 / jnp.sum(weights, axis=1, keepdims=True))
            chance = chance.astype(BF)
            probs[seq * z.heads + head] = chance
            low = low + z.inner
            found = dot(chance, keys[seq], 1, 0)
            result = jnp.where(lanes(low, low + z.head, z.pair), found, result)
        att[seq * z.local : (seq + 1) * z.local, :] = result.astype(BF)
    part[...] = dot(att[...], mixed[:, : z.pair], 1, 1)
    split_halves(z, lane, part, kept, sent)


def block_places(z, order, row, col):
    places = []
    for step in [0] + order:
        source = lax.rem(col - step + z.ctx, z.ctx)
        places.append(row * z.ctx + source)
        places.append((1 - row) * z.ctx + source)
    return places


def split_halves(z, lane, part, kept, sent):
    parity = jnp.bitwise_and(lane, 1)
    kept[...] = part[aligned(parity * z.half, z.half), :]
    sent[...] = part[aligned((1 - parity) * z.half, z.half), :].astype(sent.dtype)


def place_halves(z, lane, own, other, whole):
    parity = jnp.bitwise_and(lane, 1)
    whole[aligned(parity * z.half, z.half), :] = own[...].astype(F32)
    whole[aligned((1 - parity) * z.half, z.half), :] = other[...].astype(F32)


def forward_kernel(z, order, *refs):
    meta, own, other, rows, small = refs[:5]
    count = z.blocks if z.direct else 1
    blocks, refs = refs[5 : 5 + count], refs[5 + count :]
    up, down, normed_one, inverse_one, middle_b, slope, active, kept, sent = refs[:9]
    work = refs[9]
    row, col, lane = meta[0], meta[1], meta[2]
    if z.direct:
        for block, place in zip(blocks, block_places(z, order, row, col)):
            up[aligned(place * z.shard, z.shard), :] = block[: z.shard, :]
            down[aligned(place * z.shard, z.shard), :] = block[z.shard :, :]
    else:
        up[...] = blocks[0][: z.width, :]
        down[...] = blocks[0][z.width :, :]
    place_halves(z, lane, own, other, work)
    hidden = rows[...].astype(F32) + work[...] + small[0:1, :]
    normed, inverse = norm_rows(hidden)
    normed_one[...] = normed
    inverse_one[...] = inverse
    middle_b[...] = (normed * small[1:2, :] + small[2:3, :]).astype(BF)
    pre = dot(middle_b[...], up[...], 1, 0) + small[6:7, :]
    activated, gradient = gelu_parts(pre)
    slope[...] = gradient
    active[...] = activated.astype(BF)
    work[...] = dot(active[...], down[...], 1, 1)
    split_halves(z, lane, work, kept, sent)


def middle_kernel(z, *refs):
    meta, own, other, normed_one, small, cotangent, up, down, slope = refs[:9]
    output, d_two, d_two_b, d_pre_b, kept, sent, sums, work = refs[9:]
    lane = meta[2]
    place_halves(z, lane, own, other, work)
    middle = normed_one[...] * small[1:2, :] + small[2:3, :]
    normed, inverse = norm_rows(middle + work[...] + small[3:4, :])
    output[...] = (normed * small[4:5, :] + small[5:6, :]).astype(BF)
    grad_in = cotangent[...].astype(F32)
    sums[...] = jnp.zeros_like(sums)
    sums[4:5, :] = jnp.sum(grad_in * normed, axis=0, keepdims=True)
    sums[5:6, :] = jnp.sum(grad_in, axis=0, keepdims=True)
    d_res = norm_back(grad_in * small[4:5, :], normed, inverse)
    sums[3:4, :] = jnp.sum(d_res, axis=0, keepdims=True)
    d_two[...] = d_res
    d_two_b[...] = d_res.astype(BF)
    d_pre = dot(d_two_b[...], down[...], 1, 0) * slope[...]
    sums[6:7, :] = jnp.sum(d_pre, axis=0, keepdims=True)
    d_pre_b[...] = d_pre.astype(BF)
    work[...] = dot(d_pre_b[...], up[...], 1, 1)
    split_halves(z, lane, work, kept, sent)


def second_grad_kernel(z, *refs):
    meta, middle_b, d_pre_b, d_two_b, active = refs[:5]
    kept, sent, work = refs[5:]
    pairs = ((middle_b, d_pre_b), (d_two_b, active))
    for at, (left, right) in enumerate(pairs):
        work[...] = dot(left[...], right[...], 0, 0).astype(BF)
        part = z.width // 2
        kept[at] = work[aligned(meta[0] * part, part), :]
        sent[at] = work[aligned((1 - meta[0]) * part, part), :]


def second_grad_whole_kernel(*refs):
    _, middle_b, d_pre_b, d_two_b, active, out = refs
    out[0] = dot(middle_b[...], d_pre_b[...], 0, 0).astype(BF)
    out[1] = dot(d_two_b[...], active[...], 0, 0).astype(BF)


def backward_kernel(z, order, *refs):
    (meta, own, other, d_two, normed_one, inverse_one, small, mixed, att, query, keys), refs = (
        refs[:11],
        refs[11:],
    )
    (probs, sums_in), refs = refs[:2], refs[2:]
    d_one, d_one_b, d_query, d_keys, sums = refs[:5]
    sends, refs = refs[5 : 4 + z.ctx], refs[4 + z.ctx :]
    work, grads = refs
    col, lane = meta[1], meta[2]
    place_halves(z, lane, own, other, work)
    d_middle = d_two[...] + work[...]
    normed = normed_one[...]
    sums[...] = sums_in[...]
    sums[1:2, :] = jnp.sum(d_middle * normed, axis=0, keepdims=True)
    sums[2:3, :] = jnp.sum(d_middle, axis=0, keepdims=True)
    d_res = norm_back(d_middle * small[1:2, :], normed, inverse_one[...])
    sums[0:1, :] = jnp.sum(d_res, axis=0, keepdims=True)
    d_one[...] = d_res
    d_one_b[...] = d_res.astype(BF)
    upper = lanes(z.inner, z.pair, z.pair)
    d_att = jnp.where(upper, dot(d_one_b[...], mixed[:, : z.pair], 1, 0), 0.0).astype(BF)
    qv_sum = jnp.zeros((1, z.pair), F32)
    for seq in range(z.seqs):
        span = slice(seq * z.local, (seq + 1) * z.local)
        d_here, a_here, q_here = d_att[span], att[span, :], query[span, :]
        product = d_here.astype(F32) * a_here.astype(F32)
        d_q = jnp.zeros((z.local, z.pair), F32)
        for head in range(z.heads):
            low = head * z.head
            near = lanes(low, low + z.head, z.pair)
            far = lanes(low + z.inner, low + z.inner + z.head, z.pair)
            q_head = jnp.where(near, q_here, jnp.zeros_like(q_here))
            d_head = jnp.where(far, d_here, jnp.zeros_like(d_here))
            delta = jnp.sum(jnp.where(far, product, 0.0), axis=1, keepdims=True)
            chance = probs[seq * z.heads + head]
            d_chance = dot(d_head, keys[seq], 1, 1)
            d_scores = (chance.astype(F32) * (d_chance - delta)).astype(BF)
            d_q = jnp.where(near, dot(d_scores, keys[seq], 1, 0), d_q)
            d_kv = dot(d_scores, q_head, 0, 0) * z.scale + dot(chance, d_head, 0, 0)
            if head == 0:
                grads[...] = d_kv
            else:
                grads[...] += d_kv
        d_q = d_q * z.scale
        qv_sum = qv_sum + jnp.sum(d_q, axis=0, keepdims=True)
        qv_sum = qv_sum + jnp.where(upper, jnp.sum(grads[...], axis=0, keepdims=True), 0.0)
        d_query[span, :] = d_q.astype(BF)
        for at in range(z.ctx):
            d_keys[at, span, :] = grads[at * z.local : (at + 1) * z.local, :].astype(BF)
    sums[7:8, : z.pair] = qv_sum
    for step, send in zip(order, sends):
        send[...] = d_keys[lax.rem(col + step, z.ctx)]


def first_grad_kernel(z, *refs):
    meta, rows, every, d_query, d_keys, d_one_b, att, sums = refs[:8]
    outs, work = refs[8:-1], refs[-1]
    near = dot(rows[...], d_query[...], 0, 0) + dot(d_one_b[...], att[...], 0, 0)
    work[:, : z.pair] = near.astype(BF)
    far = dot(every[0], d_keys[0], 0, 0)
    for at in range(1, z.ctx):
        far = far + dot(every[at], d_keys[at], 0, 0)
    work[:, z.pair :] = far.astype(BF)
    if len(outs) == 1:
        outs[0][...] = work[...]
        return
    part = z.width // 2
    for out, start in zip(outs, (meta[0] * part, (1 - meta[0]) * part)):
        out[:part, :] = work[aligned(start, part), :]
        out[part:, :] = sums[...].astype(BF)


def back_kernel(z, *refs):
    meta, d_keys, d_query, mixed = refs[:4]
    got, refs = refs[4 : 3 + z.ctx], refs[3 + z.ctx :]
    kept, sent, work = refs
    total = d_keys[meta[1]].astype(F32)
    for piece in got:
        total = total + piece[...].astype(F32)
    work[...] = dot(d_query[...], mixed[:, : z.pair], 1, 1)
    work[...] += dot(total.astype(BF), mixed[:, z.pair :], 1, 1)
    split_halves(z, meta[2], work, kept, sent)


def token_kernel(z, meta, own, other, d_one, out, work):
    place_halves(z, meta[2], own, other, work)
    out[...] = (d_one[...] + work[...]).astype(BF)


def where_equal(shape, left, right):
    rows = lax.broadcasted_iota(jnp.int32, shape, 0)
    cols = lax.broadcasted_iota(jnp.int32, shape, 1)
    return jnp.where(left(rows) == right(cols), 1.0, 0.0).astype(BF)


def same_head(z, heads, width):
    rows = lax.broadcasted_iota(jnp.int32, (heads, width), 0)
    cols = lax.broadcasted_iota(jnp.int32, (heads, width), 1)
    return (cols >= rows * z.head) & (cols < (rows + 1) * z.head)


def qv_lanes(z, head):
    start = lax.broadcasted_iota(jnp.int32, (2, z.width), 0) * z.inner + head * z.head
    cols = lax.broadcasted_iota(jnp.int32, (2, z.width), 1)
    return (cols >= start) & (cols < start + z.head)


def pack_kernel(z, *refs):
    meta, qkv, out, up_bias, qv_bias, rows = refs[:6]
    vectors, (pack, share) = refs[6:-2], refs[-2:]
    place = meta[0] * z.ctx + meta[1]
    inner = z.inner

    def spread(at):
        return where_equal((inner, z.width), lambda r: r + at * inner, lambda c: c)

    total = dot(qkv[0], spread(0), 1, 0) + dot(out[...], spread(1), 0, 0)
    total = total + dot(qkv[1], spread(2), 1, 0) + dot(qkv[2], spread(3), 1, 0)
    pack[: z.shard, :] = total.astype(BF)
    at = place * z.shard
    chosen = where_equal((z.shard, z.width), lambda r: r + at, lambda c: c)
    lines = [dot(vector[...], chosen, 1, 0) for vector in vectors]
    at = place * z.piece
    chosen = where_equal(
        (z.piece, z.width), lambda r: r + at, lambda c: jnp.bitwise_and(c, z.head - 1)
    )
    heads = up_bias.shape[1]
    wide = jnp.where(same_head(z, heads, z.width), dot(up_bias[...], chosen, 0, 0), 0.0)
    lines.append(jnp.sum(wide, axis=0, keepdims=True))
    line = jnp.zeros((1, z.width), F32)
    for head in range(z.heads):
        wide = jnp.where(qv_lanes(z, head), dot(qv_bias[head], chosen, 1, 0), 0.0)
        line = line + jnp.sum(wide, axis=0, keepdims=True)
    lines.append(line)
    pack[z.shard :, :] = jnp.concatenate(lines, axis=0).astype(BF)
    size = z.rows // z.tp
    share[...] = rows[aligned(meta[2] * size, size), :]


def pack_plain(z, place, qkv_weight, out_weight, vectors, up_bias, qv_bias):
    vectors = lax.dynamic_update_slice(jnp.zeros((6, z.width), BF), vectors, (0, place * z.shard))
    up_row = lax.dynamic_update_slice(
        jnp.zeros((up_bias.shape[0], z.head), BF), up_bias, (0, place * z.piece)
    ).reshape(1, z.hidden)
    qv_row = lax.dynamic_update_slice(
        jnp.zeros((2, z.heads, z.head), BF), qv_bias, (0, 0, place * z.piece)
    ).reshape(1, z.pair)
    qv_row = jnp.pad(qv_row, ((0, 0), (0, z.width - z.pair)))
    tail = jnp.concatenate([vectors, up_row, qv_row], axis=0)
    mixed = jnp.concatenate([qkv_weight[0], out_weight.T, qkv_weight[1], qkv_weight[2]], axis=1)
    return mixed, tail


def terms(value):
    high = value.astype(BF)
    rest = value - high.astype(F32)
    middle = rest.astype(BF)
    return high, middle, (rest - middle.astype(F32)).astype(BF)


def exact_dot(left, right, over_left, over_right):
    if left.dtype == F32:
        return sum(dot(term, right, over_left, over_right) for term in terms(left))
    return sum(dot(left, term, over_left, over_right) for term in terms(right))


def finish_first_kernel(z, meta, *refs):
    blocks, refs = refs[: z.ctx], refs[z.ctx :]
    (g_qkv, g_out, g_up_bias, g_qv), g_vectors = refs[:4], refs[4:]
    total = blocks[0][...].astype(F32)
    for block in blocks[1:]:
        total = total + block[...].astype(F32)
    inner = z.inner
    for at, start in enumerate((0, 2 * inner, 3 * inner)):
        g_qkv[at] = total[: z.shard, start : start + inner]
    eye = where_equal((z.shard, z.shard), lambda r: r, lambda c: c)
    g_out[...] = exact_dot(total[: z.shard, inner : 2 * inner], eye, 0, 0)
    small = total[z.shard :]
    place = meta[0] * z.ctx + meta[1]
    at = place * z.shard
    chosen = where_equal((z.width, z.shard), lambda r: r, lambda c: c + at)
    for line, vector in enumerate(g_vectors):
        vector[...] = exact_dot(small[line : line + 1], chosen, 1, 0)
    at = place * z.piece
    chosen = where_equal(
        (z.width, z.piece), lambda r: jnp.bitwise_and(r, z.head - 1), lambda c: c + at
    )
    heads = g_up_bias.shape[1]
    wide = jnp.where(same_head(z, heads, z.width), small[6:7], 0.0)
    g_up_bias[...] = exact_dot(chosen, wide, 0, 1)
    for head in range(z.heads):
        wide = jnp.where(qv_lanes(z, head), small[7:8], 0.0)
        g_qv[head] = exact_dot(wide, chosen, 1, 0)


def finish_second_kernel(z, *refs):
    blocks, (g_up, g_down_t) = refs[: z.ctx], refs[z.ctx :]
    up, down = blocks[0][0].astype(F32), blocks[0][1].astype(F32)
    for block in blocks[1:]:
        up = up + block[0].astype(F32)
        down = down + block[1].astype(F32)
    g_up[...] = up
    g_down_t[...] = down


def share_kernel(z, order, *refs):
    meta, kept, got = refs[:3]
    own, sends, work = refs[3], refs[4:-1], refs[-1]
    work[...] = (kept[...].astype(F32) + got[...].astype(F32)).astype(BF)
    for step, out in zip([0] + order, (own,) + tuple(sends)):
        start = lax.rem(meta[1] + step, z.ctx) * z.shard
        if len(work.shape) == 3:
            for at in range(work.shape[0]):
                out[at] = work[at, aligned(start, z.shard), :]
        else:
            out[: z.shard, :] = work[aligned(start, z.shard), :]
            out[z.shard :, :] = work[z.ctx * z.shard :, :]


def gather_blocks(order, shard):
    found = []
    for step in [0] + order:
        block = ring(shard, "ctx", step) if step else shard
        found += [block, ring(block, "fsdp", 1)]
    return found


def sum_rows(z, kept, sent):
    total = kept + flip(sent, "tp", 1).astype(F32)
    bit = 2
    while bit < z.tp:
        mine = total.astype(BF)
        total = mine.astype(F32) + flip(mine, "tp", bit).astype(F32)
        bit *= 2
    total = total.astype(BF)
    return total, flip(total, "tp", 1)


def reduce_shared(z, order, meta, kept, sent):
    got = ring(sent, "fsdp", 1)
    shape = kept.shape[:-2] + (kept.shape[-2] - (z.ctx - 1) * z.shard, kept.shape[-1])
    if len(shape) == 3:
        shape = (shape[0], z.shard, shape[2])
    pieces = call(
        functools.partial(share_kernel, z, order),
        [(shape, BF)] * z.ctx,
        (kept, got),
        smem=(meta,),
        scratch=[pltpu.VMEM(kept.shape, BF)],
    )
    got = [ring(piece, "ctx", step) for step, piece in zip(order, pieces[1:])]
    return [pieces[0]] + got


def body(
    tokens,
    lengths,
    qkv_weight,
    qv_bias,
    out_weight,
    out_bias,
    norm1_gain,
    norm1_bias,
    up_weight,
    up_bias,
    down_weight,
    down_bias,
    norm2_gain,
    norm2_bias,
    cotangent,
):
    z = Sizes(tokens, qv_bias, up_weight)
    rows = tokens.reshape(-1, z.width)
    row, col, lane = (lax.axis_index(a).astype(jnp.int32) for a in ("fsdp", "ctx", "tp"))
    meta = jnp.stack([row, col, lane])
    place = row * z.ctx + col
    order = near_first(z.ctx)
    full = (z.rows, z.width)
    half = (z.half, z.width)
    square = (z.width, z.width)

    vectors = (out_bias, norm1_gain, norm1_bias, down_bias, norm2_gain, norm2_bias)
    if z.direct:
        first_pack, token_share = call(
            functools.partial(pack_kernel, z),
            [((z.shard + TAIL, z.width), BF), ((z.rows // z.tp, z.width), BF)],
            (
                qkv_weight,
                out_weight,
                up_bias.T,
                qv_bias.transpose(1, 0, 2),
                rows,
                *(vector.reshape(1, z.shard) for vector in vectors),
            ),
            smem=(meta,),
        )
    else:
        mixed_shard, tail = pack_plain(
            z, place, qkv_weight, out_weight, jnp.stack(vectors), up_bias, qv_bias
        )
        share = z.rows // z.tp
        token_share = lax.dynamic_slice_in_dim(rows, lane * share, share, 0)
    got = jnp.stack([ring(token_share, "ctx", step) for step in order])
    pieces, masks = [got], [0]
    bit = z.tp // 2
    while bit:
        pieces = pieces + [flip(piece, "tp", bit) for piece in pieces]
        masks = masks + [mask ^ bit for mask in masks]
        bit //= 2
    second_pack = jnp.concatenate([up_weight, down_weight.T], axis=0)
    if z.direct:
        first_blocks = gather_blocks(order, first_pack)
        second_blocks = gather_blocks(order, second_pack)
    else:
        split = ("fsdp", "ctx")
        mixed_all = lax.all_gather(mixed_shard, split, axis=0, tiled=True)
        tail_all = jnp.sum(lax.all_gather(tail, split, axis=0).astype(F32), axis=0).astype(BF)
        first_blocks = [jnp.concatenate([mixed_all, tail_all], axis=0)]
        second_all = lax.all_gather(second_pack, split, axis=0)
        second_all = second_all.reshape(z.blocks, 2, z.shard, z.hidden).transpose(1, 0, 2, 3)
        second_blocks = [second_all.reshape(2 * z.width, z.hidden)]

    mixed, small, every, keys, query, probs, att, kept, sent = call(
        functools.partial(attention_kernel, z, order, masks),
        [
            (square, BF),
            ((TAIL, z.width), F32),
            ((z.ctx,) + full, BF),
            ((z.seqs, z.total, z.pair), BF),
            ((z.rows, z.pair), BF),
            ((z.seqs * z.heads, z.local, z.total), BF),
            ((z.rows, z.pair), BF),
            (half, F32),
            (half, BF),
        ],
        (*first_blocks, rows, *pieces),
        smem=(meta, lengths),
        scratch=[pltpu.VMEM(full, F32)],
        flops=4 * z.rows * z.ctx * z.width * z.pair,
    )
    own, other = sum_rows(z, kept, sent)
    up, down, normed_one, inverse_one, middle_b, slope, active, kept, sent = call(
        functools.partial(forward_kernel, z, order),
        [
            (square, BF),
            (square, BF),
            (full, F32),
            ((z.rows, 1), F32),
            (full, BF),
            (full, F32),
            (full, BF),
            (half, F32),
            (half, BF),
        ],
        (own, other, rows, small, *second_blocks),
        smem=(meta,),
        scratch=[pltpu.VMEM(full, F32)],
        flops=4 * z.rows * z.width * z.hidden,
    )
    own, other = sum_rows(z, kept, sent)
    output, d_two, d_two_b, d_pre_b, kept, sent, sums = call(
        functools.partial(middle_kernel, z),
        [
            (full, BF),
            (full, F32),
            (full, BF),
            (full, BF),
            (half, F32),
            (half, BF),
            ((TAIL, z.width), F32),
        ],
        (own, other, normed_one, small, cotangent.reshape(full), up, down, slope),
        smem=(meta,),
        scratch=[pltpu.VMEM(full, F32)],
        flops=4 * z.rows * z.width * z.hidden,
    )
    grad_args = (middle_b, d_pre_b, d_two_b, active)
    grad_flops = 4 * z.rows * z.width * z.hidden
    if z.direct:
        part = (2, z.width // 2, z.hidden)
        kept_two, sent_two = call(
            functools.partial(second_grad_kernel, z),
            [(part, BF), (part, BF)],
            grad_args,
            smem=(meta,),
            scratch=[pltpu.VMEM(square, BF)],
            flops=grad_flops,
        )
    else:
        (second_grads,) = call(
            second_grad_whole_kernel,
            [((2,) + square, BF)],
            grad_args,
            smem=(meta,),
            flops=grad_flops,
        )
    own, other = sum_rows(z, kept, sent)
    d_one, d_one_b, d_query, d_keys, sums, *sends = call(
        functools.partial(backward_kernel, z, order),
        [
            (full, F32),
            (full, BF),
            ((z.rows, z.pair), BF),
            ((z.ctx, z.rows, z.pair), BF),
            ((TAIL, z.width), F32),
        ]
        + [((z.rows, z.pair), BF)] * (z.ctx - 1),
        (own, other, d_two, normed_one, inverse_one, small, mixed, att, query, keys, probs, sums),
        smem=(meta,),
        scratch=[pltpu.VMEM(full, F32), pltpu.VMEM((z.total, z.pair), F32)],
        flops=10 * z.rows * z.heads * z.total * z.pair,
    )
    got = [ring(piece, "ctx", step) for step, piece in zip(order, sends)]
    if z.direct:
        part = (z.width // 2 + TAIL, z.width)
        grad_outs = [(part, BF), (part, BF)]
    else:
        grad_outs = [(square, BF)]
    first_parts = call(
        functools.partial(first_grad_kernel, z),
        grad_outs,
        (rows, every, d_query, d_keys, d_one_b, att, sums),
        smem=(meta,),
        scratch=[pltpu.VMEM(square, BF)],
        flops=2 * z.rows * (z.ctx + 2) * z.width * z.pair,
    )
    kept, sent = call(
        functools.partial(back_kernel, z),
        [(half, F32), (half, BF)],
        (d_keys, d_query, mixed, *got),
        smem=(meta,),
        scratch=[pltpu.VMEM(full, F32)],
        flops=4 * z.rows * z.width * z.pair,
    )
    own, other = sum_rows(z, kept, sent)
    (token_grad,) = call(
        functools.partial(token_kernel, z),
        [(full, BF)],
        (own, other, d_one),
        smem=(meta,),
        scratch=[pltpu.VMEM(full, F32)],
    )

    if z.direct:
        second = reduce_shared(z, order, meta, kept_two, sent_two)
        first = reduce_shared(z, order, meta, *first_parts)
        g_up, g_down_t = call(
            functools.partial(finish_second_kernel, z),
            [(up_weight.shape, F32), (up_weight.shape, F32)],
            second,
        )
        g_down = g_down_t.T
        g_qkv, g_out, g_up_bias, g_qv, *g_vectors = call(
            functools.partial(finish_first_kernel, z),
            [
                (qkv_weight.shape, F32),
                (out_weight.shape, F32),
                (up_bias.shape[::-1], F32),
                ((z.heads, 2, z.piece), F32),
            ]
            + [((1, z.shard), F32)] * 6,
            first,
            smem=(meta,),
        )
        g_up_bias = g_up_bias.T
        g_qv = g_qv.transpose(1, 0, 2)
        g_vectors = [vector.reshape(z.shard) for vector in g_vectors]
    else:
        split = ("fsdp", "ctx")
        second = lax.psum_scatter(
            second_grads.astype(F32), split, scatter_dimension=1, tiled=True
        )
        g_up, g_down = second[0], second[1].T
        g_mixed = lax.psum_scatter(
            first_parts[0].astype(F32), split, scatter_dimension=0, tiled=True
        )
        g_small = lax.psum(sums, split)
        inner = z.inner
        starts = (0, 2 * inner, 3 * inner)
        g_qkv = jnp.stack([g_mixed[:, start : start + inner] for start in starts])
        g_out = g_mixed[:, inner : 2 * inner].T
        g_vectors = lax.dynamic_slice(g_small, (0, place * z.shard), (6, z.shard))
        g_up_bias = lax.dynamic_slice(
            g_small[6].reshape(up_bias.shape[0], z.head), (0, place * z.piece), up_bias.shape
        )
        g_qv = lax.dynamic_slice(
            g_small[7, : z.pair].reshape(2, z.heads, z.head),
            (0, 0, place * z.piece),
            qv_bias.shape,
        )
    return (
        output.reshape(tokens.shape),
        token_grad.reshape(tokens.shape),
        g_qkv,
        g_qv,
        g_out,
        g_vectors[0],
        g_vectors[1],
        g_vectors[2],
        g_up,
        g_up_bias,
        g_down,
        g_vectors[3],
        g_vectors[4],
        g_vectors[5],
    )


def solution(mesh):
    split = ("fsdp", "ctx")
    vector = P(split)
    rows = P("fsdp", "ctx", None)
    weights = (
        P(None, split, "tp"),
        P(None, "tp", split),
        P("tp", split),
        vector,
        vector,
        vector,
        P(split, "tp"),
        P("tp", split),
        P("tp", split),
        vector,
        vector,
        vector,
    )

    return jax.shard_map(
        body,
        mesh=mesh,
        in_specs=(rows, P("fsdp", None)) + weights + (rows,),
        out_specs=(rows, rows) + weights,
        check_vma=False,
    )
```

profile of v0, /device:TPU:0, one launch (start us, length us, event | category | flops | bytes accessed | tf_op | source)
XLA Modules:
  0.0 232.9 jit_solution(10170278390966666644)
XLA Ops:
  1.3 2.3 %shard_map.254 = (bf16[104,768]{1,0:T(8,128)(2,1)}, bf16[64,768]{1,0:T(8,128)(2,1)}) custom-call(s32[3]{0:T(128)} %pad_add_fusion.refs_0_.meta, bf16[3,96,192]{2,1,0:T(8,128)(2,1)} %refs_1_.2, bf16[192,96]{1,0:T(8,128)(2,1)} %refs_2_.1, bf16[8,12]{1,0:T(8,128)(2,1)} %bitcast.38, bf16[3,2,8]{2,1,0:T(2,128)(2,1)} %bitcast.39, bf16[256,768]{1,0:T(8,128)(2,1)} %bitcast.28, ...), custom_call_target="tpu_custom_call" | custom-call | bytes 800160 | tf_op jit(solution)/shard_map/pallas_call | solution.py:65
  3.7 4.1 %collective-permute-start.9 = (bf16[64,768]{1,0:T(8,128)(2,1)}, bf16[64,768]{1,0:T(8,128)(2,1)S(1)}, u32[]{:S(2)}, u32[]{:S(2)}) collective-permute-start(bf16[64,768]{1,0:T(8,128)(2,1)} %get-tuple-element.76), channel_id=1, source_target_pairs={{0,8},{4,12},{8,0},{12,4},{1,9},{5,13},{9,1},{13,5},{2,10},{6,14},... | collective-permute-start | bytes 294920 | tf_op jit(solution)/shard_map/ppermute | solution.py:44
  9.8 4.6 %collective-permute-done.9 = bf16[64,768]{1,0:T(8,128)(2,1)S(1)} collective-permute-done((bf16[64,768]{1,0:T(8,128)(2,1)}, bf16[64,768]{1,0:T(8,128)(2,1)S(1)}, u32[]{:S(2)}, u32[]{:S(2)}) %collective-permute-start.9) | collective-permute-done | bytes 98336 | tf_op jit(solution)/shard_map/ppermute | solution.py:44
  14.4 1.7 collective-permute-done.7
  17.6 3.7 %collective-permute-start.5 = (bf16[104,768]{1,0:T(8,128)(2,1)}, bf16[104,768]{1,0:T(8,128)(2,1)S(1)}, u32[]{:S(2)}, u32[]{:S(2)}) collective-permute-start(bf16[104,768]{1,0:T(8,128)(2,1)} %get-tuple-element.75.refs_2_), channel_id=1, source_target_pairs={{0,8},{4,12},{8,0},{12,4},{1,9},{5,13},{9,1},{13,5},{2,10},{6,14},... | collective-permute-start | bytes 479240 | tf_op jit(solution)/shard_map/ppermute | solution.py:44
  23.3 1.5 collective-permute-start
  24.8 5.7 %collective-permute-done.5.refs_8_ = bf16[104,768]{1,0:T(8,128)(2,1)S(1)} collective-permute-done((bf16[104,768]{1,0:T(8,128)(2,1)}, bf16[104,768]{1,0:T(8,128)(2,1)S(1)}, u32[]{:S(2)}, u32[]{:S(2)}) %collective-permute-start.5) | collective-permute-done | bytes 159776 | tf_op jit(solution)/shard_map/ppermute | solution.py:44
  31.1 2.4 %collective-permute-done.3.refs_6_ = bf16[104,768]{1,0:T(8,128)(2,1)S(1)} collective-permute-done((bf16[104,768]{1,0:T(8,128)(2,1)}, bf16[104,768]{1,0:T(8,128)(2,1)S(1)}, u32[]{:S(2)}, u32[]{:S(2)}) %collective-permute-start.3) | collective-permute-done | bytes 159776 | tf_op jit(solution)/shard_map/ppermute | solution.py:44
  33.5 1.5 collective-permute-start.6
  35.5 1.5 collective-permute-start.2
  37.0 3.4 %collective-permute-done.6.refs_9_ = bf16[104,768]{1,0:T(8,128)(2,1)S(1)} collective-permute-done((bf16[104,768]{1,0:T(8,128)(2,1)S(1)}, bf16[104,768]{1,0:T(8,128)(2,1)S(1)}, u32[]{:S(2)}, u32[]{:S(2)}) %collective-permute-start.6) | collective-permute-done | bytes 159776 | tf_op jit(solution)/shard_map/ppermute | solution.py:44
  40.5 1.9 collective-permute-done.4.refs_7_
  42.3 1.7 collective-permute-done.2.refs_5_
  45.5 7.9 %shard_map.255 = (bf16[768,768]{1,0:T(8,128)(2,1)}, f32[8,768]{1,0:T(8,128)}, bf16[4,256,768]{2,1,0:T(8,128)(2,1)}, bf16[2,512,384]{2,1,0:T(8,128)(2,1)}, bf16[2...) custom-call(s32[3]{0:T(128)} %pad_add_fusion.refs_0_.meta, ...), custom_call_target="tpu_custom_call" | custom-call | flops 1207959552 | bytes 8183808 | tf_op jit(solution)/shard_map/pallas_call | solution.py:65
  53.5 4.1 %collective-permute-start.21 = (bf16[192,768]{1,0:T(8,128)(2,1)S(1)}, bf16[192,768]{1,0:T(8,128)(2,1)S(1)}, u32[]{:S(2)}, u32[]{:S(2)}) collective-permute-start(bf16[192,768]{1,0:T(8,128)(2,1)S(1)} %pad_maximum_fusion.1.refs_5_), channel_id=1, source_target_pairs={{0,8},{4,12},{8,0},{12,4},{1,9},{5,13},{9,1},{13,5},{2,10},{6,14},... | collective-permute-start | bytes 884744 | tf_op jit(solution)/shard_map/ppermute | solution.py:44
  57.6 3.3 %collective-permute-start.19 = (bf16[192,768]{1,0:T(8,128)(2,1)S(1)}, bf16[192,768]{1,0:T(8,128)(2,1)S(1)}, u32[]{:S(2)}, u32[]{:S(2)}) collective-permute-start(bf16[192,768]{1,0:T(8,128)(2,1)S(1)} %pad_maximum_fusion.1.refs_5_), channel_id=1, source_target_pairs={{0,12},{4,0},{8,4},{12,8},{1,13},{5,1},{9,5},{13,9},{2,14},{6,2},{... | collective-permute-start | bytes 884744 | tf_op jit(solution)/shard_map/ppermute | solution.py:44
  62.5 1.5 collective-permute-start.16
  64.0 7.7 %collective-permute-done.21.refs_11_ = bf16[192,768]{1,0:T(8,128)(2,1)S(1)} collective-permute-done((bf16[192,768]{1,0:T(8,128)(2,1)S(1)}, bf16[192,768]{1,0:T(8,128)(2,1)S(1)}, u32[]{:S(2)}, u32[]{:S(2)}) %collective-permute-start.21) | collective-permute-done | bytes 294944 | tf_op jit(solution)/shard_map/ppermute | solution.py:44
  71.8 1.5 collective-permute-start.22
  73.8 7.2 %collective-permute-done.17.refs_7_ = bf16[192,768]{1,0:T(8,128)(2,1)S(1)} collective-permute-done((bf16[192,768]{1,0:T(8,128)(2,1)S(1)}, bf16[192,768]{1,0:T(8,128)(2,1)S(1)}, u32[]{:S(2)}, u32[]{:S(2)}) %collective-permute-start.17) | collective-permute-done | bytes 294944 | tf_op jit(solution)/shard_map/ppermute | solution.py:44
  81.0 1.5 collective-permute-start.18
  82.7 5.2 %collective-permute-done.20.refs_10_ = bf16[192,768]{1,0:T(8,128)(2,1)S(1)} collective-permute-done((bf16[192,768]{1,0:T(8,128)(2,1)S(1)}, bf16[192,768]{1,0:T(8,128)(2,1)S(1)}, u32[]{:S(2)}, u32[]{:S(2)}) %collective-permute-start.20) | collective-permute-done | bytes 294944 | tf_op jit(solution)/shard_map/ppermute | solution.py:44
  88.0 5.1 %collective-permute-done.18.refs_8_ = bf16[192,768]{1,0:T(8,128)(2,1)S(1)} collective-permute-done((bf16[192,768]{1,0:T(8,128)(2,1)S(1)}, bf16[192,768]{1,0:T(8,128)(2,1)S(1)}, u32[]{:S(2)}, u32[]{:S(2)}) %collective-permute-start.18) | collective-permute-done | bytes 294944 | tf_op jit(solution)/shard_map/ppermute | solution.py:44
  93.8 4.8 %shard_map.256 = (bf16[768,768]{1,0:T(8,128)(2,1)}, bf16[768,768]{1,0:T(8,128)(2,1)}, f32[256,768]{1,0:T(8,128)}, f32[256,1]{1,0:T(8,128)}, bf16[256,768]{1,0:T(...) custom-call(s32[3]{0:T(128)} %pad_add_fusion.refs_0_.meta, ...), custom_call_target="tpu_custom_call" | custom-call | flops 603979776 | bytes 8479744 | tf_op jit(solution)/shard_map/pallas_call | solution.py:65
  98.6 1.6 collective-permute-done.23
  101.9 6.4 %collective-permute-done.24 = bf16[128,768]{1,0:T(8,128)(2,1)S(1)} collective-permute-done((bf16[128,768]{1,0:T(8,128)(2,1)S(1)}, bf16[128,768]{1,0:T(8,128)(2,1)S(1)}, u32[]{:S(2)}, u32[]{:S(2)}) %collective-permute-start.24) | collective-permute-done | bytes 196640 | tf_op jit(solution)/shard_map/ppermute | solution.py:49
  110.5 5.0 %shard_map.257 = (bf16[256,768]{1,0:T(8,128)(2,1)}, f32[256,768]{1,0:T(8,128)}, bf16[256,768]{1,0:T(8,128)(2,1)}, bf16[256,768]{1,0:T(8,128)(2,1)}, f32[128,768]...) custom-call(s32[3]{0:T(128)} %pad_add_fusion.refs_0_.meta, bf16[128,768]{1,0:T(8,128)(2,1)} %copy-done.2, ...), custom_call_target="tpu_custom_call" | custom-call | flops 603979776 | bytes 7323648 | tf_op jit(solution)/shard_map/pallas_call | solution.py:65
  118.8 6.4 %collective-permute-done.27 = bf16[128,768]{1,0:T(8,128)(2,1)S(1)} collective-permute-done((bf16[128,768]{1,0:T(8,128)(2,1)S(1)}, bf16[128,768]{1,0:T(8,128)(2,1)S(1)}, u32[]{:S(2)}, u32[]{:S(2)}) %collective-permute-start.27) | collective-permute-done | bytes 196640 | tf_op jit(solution)/shard_map/ppermute | solution.py:49
  125.4 3.7 %shard_map.264 = (bf16[2,384,768]{2,1,0:T(8,128)(2,1)}, bf16[2,384,768]{2,1,0:T(8,128)(2,1)}) custom-call(s32[3]{0:T(128)} %pad_add_fusion.refs_0_.meta, bf16[256,768]{1,0:T(8,128)(2,1)} %get-tuple-element.120.refs_1_, bf16[256,768]{1,0:T(8,128)(2,1)} %get-tuple-element.121.refs_2_, bf16[256,768]{1,0:T(8,128)(2,1)} %get-tuple-element.122.refs_3_, ...), custom_call_target="tpu_custom_call" | custom-call | flops 603979776 | bytes 3932160 | tf_op jit(solution)/shard_map/pallas_call | solution.py:65
  131.3 7.3 %shard_map.258 = (f32[256,768]{1,0:T(8,128)}, bf16[256,768]{1,0:T(8,128)(2,1)}, bf16[256,384]{1,0:T(8,128)(2,1)}, bf16[4,256,384]{2,1,0:T(8,128)(2,1)}, f32[8,76...) custom-call(s32[3]{0:T(128)} %pad_add_fusion.refs_0_.meta, ...), custom_call_target="tpu_custom_call" | custom-call | flops 1509949440 | bytes 7939072 | tf_op jit(solution)/shard_map/pallas_call | solution.py:65
  138.6 6.9 %collective-permute-start.29 = (bf16[256,384]{1,0:T(8,128)(2,1)}, bf16[256,384]{1,0:T(8,128)(2,1)S(1)}, u32[]{:S(2)}, u32[]{:S(2)}) collective-permute-start(bf16[256,384]{1,0:T(8,128)(2,1)} %get-tuple-element.99), channel_id=1, source_target_pairs={{0,4},{4,8},{8,12},{12,0},{1,5},{5,9},{9,13},{13,1},{2,6},{6,10},{... | collective-permute-start | bytes 589832 | tf_op jit(solution)/shard_map/ppermute | solution.py:44
  145.6 2.8 %collective-permute-start.30 = (bf16[256,384]{1,0:T(8,128)(2,1)}, bf16[256,384]{1,0:T(8,128)(2,1)S(1)}, u32[]{:S(2)}, u32[]{:S(2)}) collective-permute-start(bf16[256,384]{1,0:T(8,128)(2,1)} %get-tuple-element.100), channel_id=1, source_target_pairs={{0,12},{4,0},{8,4},{12,8},{1,13},{5,1},{9,5},{13,9},{2,14},{6,2},{... | collective-permute-start | bytes 589832 | tf_op jit(solution)/shard_map/ppermute | solution.py:44
  148.8 5.4 %collective-permute-done.29.refs_4_ = bf16[256,384]{1,0:T(8,128)(2,1)S(1)} collective-permute-done((bf16[256,384]{1,0:T(8,128)(2,1)}, bf16[256,384]{1,0:T(8,128)(2,1)S(1)}, u32[]{:S(2)}, u32[]{:S(2)}) %collective-permute-start.29) | collective-permute-done | bytes 196640 | tf_op jit(solution)/shard_map/ppermute | solution.py:44
  154.3 2.5 %collective-permute-done.30.refs_5_ = bf16[256,384]{1,0:T(8,128)(2,1)S(1)} collective-permute-done((bf16[256,384]{1,0:T(8,128)(2,1)}, bf16[256,384]{1,0:T(8,128)(2,1)S(1)}, u32[]{:S(2)}, u32[]{:S(2)}) %collective-permute-start.30) | collective-permute-done | bytes 196640 | tf_op jit(solution)/shard_map/ppermute | solution.py:44
  156.7 9.7 %collective-permute-done.31.refs_6_ = bf16[256,384]{1,0:T(8,128)(2,1)S(1)} collective-permute-done((bf16[256,384]{1,0:T(8,128)(2,1)}, bf16[256,384]{1,0:T(8,128)(2,1)S(1)}, u32[]{:S(2)}, u32[]{:S(2)}) %collective-permute-start.31) | collective-permute-done | bytes 196640 | tf_op jit(solution)/shard_map/ppermute | solution.py:44
  167.1 3.3 %shard_map.259 = (f32[128,768]{1,0:T(8,128)}, bf16[128,768]{1,0:T(8,128)(2,1)}) custom-call(s32[3]{0:T(128)} %pad_add_fusion.refs_0_.meta, bf16[4,256,384]{2,1,0:T(8,128)(2,1)} %get-tuple-element.97.refs_1_.refs_4_, bf16[256,384]{1,0:T(8,128)(2,1)} %get-tuple-element.98.refs_2_.refs_3_, bf16[768,768]{1,0:T(8,128)(2,1)} %get-tuple-element.91.refs_7_.refs_3_, ...), custom_call_target="tpu_custom_call" | custom-call | flops 301989888 | bytes 3342336 | tf_op jit(solution)/shard_map/pallas_call | solution.py:65
  170.4 4.5 %shard_map.261 = (bf16[392,768]{1,0:T(8,128)(2,1)}, bf16[392,768]{1,0:T(8,128)(2,1)}) custom-call(s32[3]{0:T(128)} %pad_add_fusion.refs_0_.meta, bf16[256,768]{1,0:T(8,128)(2,1)} %bitcast.31, bf16[4,256,768]{2,1,0:T(8,128)(2,1)} %get-tuple-element.105.refs_2_, bf16[256,384]{1,0:T(8,128)(2,1)} %get-tuple-element.98.refs_2_.refs_3_, ...), custom_call_target="tpu_custom_call" | custom-call | flops 905969664 | bytes 4767744 | tf_op jit(solution)/shard_map/pallas_call | solution.py:65
  177.1 3.3 %shard_map.265 = (bf16[2,96,768]{2,1,0:T(8,128)(2,1)}, bf16[2,96,768]{2,1,0:T(8,128)(2,1)}, bf16[2,96,768]{2,1,0:T(8,128)(2,1)}, bf16[2,96,768]{2,1,0:T(8,128)(2,1)}) custom-call(s32[3]{0:T(128)} %pad_add_fusion.refs_0_.meta, bf16[2,384,768]{2,1,0:T(8,128)(2,1)} %get-tuple-element.124.refs_1_, bf16[2,384,768]{2,1,0:T(8,128)(2,1)} %copy-done), custom_call_target="tpu_custom_call" | custom-call | bytes 3538944 | tf_op jit(solution)/shard_map/pallas_call | solution.py:65
  180.4 3.8 %collective-permute-start.41 = (bf16[2,96,768]{2,1,0:T(8,128)(2,1)}, bf16[2,96,768]{2,1,0:T(8,128)(2,1)S(1)}, u32[]{:S(2)}, u32[]{:S(2)}) collective-permute-start(bf16[2,96,768]{2,1,0:T(8,128)(2,1)} %get-tuple-element.128), channel_id=1, source_target_pairs={{0,12},{4,0},{8,4},{12,8},{1,13},{5,1},{9,5},{13,9},{2,14},{6,2},{... | collective-permute-start | bytes 884744 | tf_op jit(solution)/shard_map/ppermute | solution.py:44
  184.2 6.8 %collective-permute-done.35.refs_2_ = bf16[392,768]{1,0:T(8,128)(2,1)S(1)} collective-permute-done((bf16[392,768]{1,0:T(8,128)(2,1)}, bf16[392,768]{1,0:T(8,128)(2,1)S(1)}, u32[]{:S(2)}, u32[]{:S(2)}) %collective-permute-start.35) | collective-permute-done | bytes 602144 | tf_op jit(solution)/shard_map/ppermute | solution.py:44
  191.9 2.4 %shard_map.262 = (bf16[104,768]{1,0:T(8,128)(2,1)}, bf16[104,768]{1,0:T(8,128)(2,1)}, bf16[104,768]{1,0:T(8,128)(2,1)}, bf16[104,768]{1,0:T(8,128)(2,1)}) custom-call(s32[3]{0:T(128)} %pad_add_fusion.refs_0_.meta, bf16[392,768]{1,0:T(8,128)(2,1)} %get-tuple-element.108.refs_1_, bf16[392,768]{1,0:T(8,128)(2,1)} %copy-done.5), custom_call_target="tpu_custom_call" | custom-call | bytes 1843200 | tf_op jit(solution)/shard_map/pallas_call | solution.py:65
  194.3 3.8 %collective-permute-start.37 = (bf16[104,768]{1,0:T(8,128)(2,1)}, bf16[104,768]{1,0:T(8,128)(2,1)S(1)}, u32[]{:S(2)}, u32[]{:S(2)}) collective-permute-start(bf16[104,768]{1,0:T(8,128)(2,1)} %get-tuple-element.112), channel_id=1, source_target_pairs={{0,12},{4,0},{8,4},{12,8},{1,13},{5,1},{9,5},{13,9},{2,14},{6,2},{... | collective-permute-start | bytes 479240 | tf_op jit(solution)/shard_map/ppermute | solution.py:44
  198.2 10.2 %collective-permute-done.36.refs_1_ = bf16[104,768]{1,0:T(8,128)(2,1)S(1)} collective-permute-done((bf16[104,768]{1,0:T(8,128)(2,1)}, bf16[104,768]{1,0:T(8,128)(2,1)S(1)}, u32[]{:S(2)}, u32[]{:S(2)}) %collective-permute-start.36) | collective-permute-done | bytes 159776 | tf_op jit(solution)/shard_map/ppermute | solution.py:44
  208.4 6.5 %collective-permute-start.38 = (bf16[104,768]{1,0:T(8,128)(2,1)}, bf16[104,768]{1,0:T(8,128)(2,1)S(1)}, u32[]{:S(2)}, u32[]{:S(2)}) collective-permute-start(bf16[104,768]{1,0:T(8,128)(2,1)} %get-tuple-element.113), channel_id=1, source_target_pairs={{0,8},{4,12},{8,0},{12,4},{1,9},{5,13},{9,1},{13,5},{2,10},{6,14},... | collective-permute-start | bytes 479240 | tf_op jit(solution)/shard_map/ppermute | solution.py:44
  215.0 8.3 %collective-permute-done.38.refs_3_ = bf16[104,768]{1,0:T(8,128)(2,1)S(1)} collective-permute-done((bf16[104,768]{1,0:T(8,128)(2,1)}, bf16[104,768]{1,0:T(8,128)(2,1)S(1)}, u32[]{:S(2)}, u32[]{:S(2)}) %collective-permute-start.38) | collective-permute-done | bytes 159776 | tf_op jit(solution)/shard_map/ppermute | solution.py:44
  224.0 2.9 %shard_map.263 = (f32[3,96,192]{2,1,0:T(8,128)}, f32[192,96]{1,0:T(8,128)}, f32[8,12]{1,0:T(8,128)}, f32[3,2,8]{2,1,0:T(2,128)}, f32[1,96]{1,0:T(1,128)}, /*inde...) custom-call(s32[3]{0:T(128)} %pad_add_fusion.refs_0_.meta, ...), custom_call_target="tpu_custom_call" | custom-call | bytes 936768 | tf_op jit(solution)/shard_map/pallas_call | solution.py:65
  227.6 2.2 shard_map.260
  230.8 2.1 shard_map.266
  (144 shorter events, 27.8 us)
Async XLA Ops:
  3.7 10.7 %collective-permute-start.9 = (bf16[64,768]{1,0:T(8,128)(2,1)}, bf16[64,768]{1,0:T(8,128)(2,1)S(1)}, u32[]{:S(2)}, u32[]{:S(2)}) collective-permute-start(bf16[64,768]{1,0:T(8,128)(2,1)} %get-tuple-element.76), channel_id=1, source_target_pairs={{0,8},{4,12},{8,0},{12,4},{1,9},{5,13},{9,1},{13,5},{2,10},{6,14},... | collective-permute-start | bytes 294920 | tf_op jit(solution)/shard_map/ppermute | solution.py:44
  7.7 6.6 %collective-permute-start.8 = (bf16[64,768]{1,0:T(8,128)(2,1)}, bf16[64,768]{1,0:T(8,128)(2,1)S(1)}, u32[]{:S(2)}, u32[]{:S(2)}) collective-permute-start(bf16[64,768]{1,0:T(8,128)(2,1)} %get-tuple-element.76), channel_id=1, source_target_pairs={{0,12},{4,0},{8,4},{12,8},{1,13},{5,1},{9,5},{13,9},{2,14},{6,2},{... | collective-permute-start | bytes 294920 | tf_op jit(solution)/shard_map/ppermute | solution.py:44
  9.1 7.0 %collective-permute-start.7 = (bf16[64,768]{1,0:T(8,128)(2,1)}, bf16[64,768]{1,0:T(8,128)(2,1)S(1)}, u32[]{:S(2)}, u32[]{:S(2)}) collective-permute-start(bf16[64,768]{1,0:T(8,128)(2,1)} %get-tuple-element.76), channel_id=1, source_target_pairs={{0,4},{4,8},{8,12},{12,0},{1,5},{5,9},{9,13},{13,1},{2,6},{6,10},{... | collective-permute-start | bytes 294920 | tf_op jit(solution)/shard_map/ppermute | solution.py:44
  16.1 28.0 %copy-start.7 = (bf16[3,64,768]{2,1,0:T(8,128)(2,1)}, bf16[3,64,768]{2,1,0:T(8,128)(2,1)S(1)}, u32[]{:S(2)}) copy-start(bf16[3,64,768]{2,1,0:T(8,128)(2,1)S(1)} %pad_maximum_fusion.refs_11_) | copy-start | bytes 884740
  16.1 14.5 %collective-permute-start.10 = (bf16[3,64,768]{2,1,0:T(8,128)(2,1)S(1)}, bf16[3,64,768]{2,1,0:T(8,128)(2,1)S(1)}, u32[]{:S(2)}, u32[]{:S(2)}) collective-permute-start(bf16[3,64,768]{2,1,0:T(8,128)(2,1)S(1)} %pad_maximum_fusion.refs_11_), channel_id=1, source_target_pairs={{0,2},{1,3},{2,0},{3,1},{4,6},{5,7},{6,4},{7,5},{8,10},{9,11},{10,... | collective-permute-start | bytes 884744 | tf_op jit(solution)/shard_map/ppermute | solution.py:49
  17.6 35.8 %copy-start.28 = (bf16[768,96]{0,1:T(8,128)(2,1)S(1)}, bf16[768,96]{0,1:T(8,128)(2,1)}, u32[]{:S(2)}) copy-start(bf16[768,96]{0,1:T(8,128)(2,1)} %param.25) | copy-start | bytes 442372
  17.6 35.8 %copy-start.29 = (bf16[96,768]{1,0:T(8,128)(2,1)S(1)}, bf16[96,768]{1,0:T(8,128)(2,1)}, u32[]{:S(2)}) copy-start(bf16[96,768]{1,0:T(8,128)(2,1)} %param.23) | copy-start | bytes 442372
  17.6 12.9 %collective-permute-start.5 = (bf16[104,768]{1,0:T(8,128)(2,1)}, bf16[104,768]{1,0:T(8,128)(2,1)S(1)}, u32[]{:S(2)}, u32[]{:S(2)}) collective-permute-start(bf16[104,768]{1,0:T(8,128)(2,1)} %get-tuple-element.75.refs_2_), channel_id=1, source_target_pairs={{0,8},{4,12},{8,0},{12,4},{1,9},{5,13},{9,1},{13,5},{2,10},{6,14},... | collective-permute-start | bytes 479240 | tf_op jit(solution)/shard_map/ppermute | solution.py:44
  21.3 12.2 %collective-permute-start.3 = (bf16[104,768]{1,0:T(8,128)(2,1)}, bf16[104,768]{1,0:T(8,128)(2,1)S(1)}, u32[]{:S(2)}, u32[]{:S(2)}) collective-permute-start(bf16[104,768]{1,0:T(8,128)(2,1)} %get-tuple-element.75.refs_2_), channel_id=1, source_target_pairs={{0,12},{4,0},{8,4},{12,8},{1,13},{5,1},{9,5},{13,9},{2,14},{6,2},{... | collective-permute-start | bytes 479240 | tf_op jit(solution)/shard_map/ppermute | solution.py:44
  21.9 13.1 %collective-permute-start.1 = (bf16[104,768]{1,0:T(8,128)(2,1)}, bf16[104,768]{1,0:T(8,128)(2,1)S(1)}, u32[]{:S(2)}, u32[]{:S(2)}) collective-permute-start(bf16[104,768]{1,0:T(8,128)(2,1)} %get-tuple-element.75.refs_2_), channel_id=1, source_target_pairs={{0,4},{4,8},{8,12},{12,0},{1,5},{5,9},{9,13},{13,1},{2,6},{6,10},{... | collective-permute-start | bytes 479240 | tf_op jit(solution)/shard_map/ppermute | solution.py:44
  23.3 12.2 %collective-permute-start = (bf16[104,768]{1,0:T(8,128)(2,1)}, bf16[104,768]{1,0:T(8,128)(2,1)S(1)}, u32[]{:S(2)}, u32[]{:S(2)}) collective-permute-start(bf16[104,768]{1,0:T(8,128)(2,1)} %get-tuple-element.75.refs_2_), channel_id=1, source_target_pairs={{0,16},{16,0},{1,17},{17,1},{2,18},{18,2},{3,19},{19,3},{4,20},{20... | collective-permute-start | bytes 479240 | tf_op jit(solution)/shard_map/ppermute | solution.py:44
  30.6 13.5 %collective-permute-start.11 = (bf16[3,64,768]{2,1,0:T(8,128)(2,1)S(1)}, bf16[3,64,768]{2,1,0:T(8,128)(2,1)S(1)}, u32[]{:S(2)}, u32[]{:S(2)}) collective-permute-start(bf16[3,64,768]{2,1,0:T(8,128)(2,1)S(1)} %pad_maximum_fusion.refs_11_), channel_id=1, source_target_pairs={{0,1},{1,0},{2,3},{3,2},{4,5},{5,4},{6,7},{7,6},{8,9},{9,8},{10,11... | collective-permute-start | bytes 884744 | tf_op jit(solution)/shard_map/ppermute | solution.py:49
  30.6 13.5 %collective-permute-start.12 = (bf16[3,64,768]{2,1,0:T(8,128)(2,1)S(1)}, bf16[3,64,768]{2,1,0:T(8,128)(2,1)S(1)}, u32[]{:S(2)}, u32[]{:S(2)}) collective-permute-start(bf16[3,64,768]{2,1,0:T(8,128)(2,1)S(1)} %collective-permute-done.10.refs_12_), channel_id=1, source_target_pairs={{0,1},{1,0},{2,3},{3,2},{4,5},{5,4},{6,7},{7,6},{8,9},{9,8},{10,11... | collective-permute-start | bytes 884744 | tf_op jit(solution)/shard_map/ppermute | solution.py:49
  33.5 7.0 %collective-permute-start.6 = (bf16[104,768]{1,0:T(8,128)(2,1)S(1)}, bf16[104,768]{1,0:T(8,128)(2,1)S(1)}, u32[]{:S(2)}, u32[]{:S(2)}) collective-permute-start(bf16[104,768]{1,0:T(8,128)(2,1)S(1)} %collective-permute-done.5.refs_8_), channel_id=1, source_target_pairs={{0,16},{16,0},{1,17},{17,1},{2,18},{18,2},{3,19},{19,3},{4,20},{20... | collective-permute-start | bytes 479240 | tf_op jit(solution)/shard_map/ppermute | solution.py:44
  35.0 7.3 %collective-permute-start.4 = (bf16[104,768]{1,0:T(8,128)(2,1)S(1)}, bf16[104,768]{1,0:T(8,128)(2,1)S(1)}, u32[]{:S(2)}, u32[]{:S(2)}) collective-permute-start(bf16[104,768]{1,0:T(8,128)(2,1)S(1)} %collective-permute-done.3.refs_6_), channel_id=1, source_target_pairs={{0,16},{16,0},{1,17},{17,1},{2,18},{18,2},{3,19},{19,3},{4,20},{20... | collective-permute-start | bytes 479240 | tf_op jit(solution)/shard_map/ppermute | solution.py:44
  35.5 8.5 %collective-permute-start.2 = (bf16[104,768]{1,0:T(8,128)(2,1)S(1)}, bf16[104,768]{1,0:T(8,128)(2,1)S(1)}, u32[]{:S(2)}, u32[]{:S(2)}) collective-permute-start(bf16[104,768]{1,0:T(8,128)(2,1)S(1)} %collective-permute-done.1.refs_4_), channel_id=1, source_target_pairs={{0,16},{16,0},{1,17},{17,1},{2,18},{18,2},{3,19},{19,3},{4,20},{20... | collective-permute-start | bytes 479240 | tf_op jit(solution)/shard_map/ppermute | solution.py:44
  53.4 7.5 %collective-permute-start.13 = (bf16[128,768]{1,0:T(8,128)(2,1)}, bf16[128,768]{1,0:T(8,128)(2,1)S(1)}, u32[]{:S(2)}, u32[]{:S(2)}) collective-permute-start(bf16[128,768]{1,0:T(8,128)(2,1)} %get-tuple-element.78), channel_id=1, source_target_pairs={{0,1},{1,0},{2,3},{3,2},{4,5},{5,4},{6,7},{7,6},{8,9},{9,8},{10,11... | collective-permute-start | bytes 589832 | tf_op jit(solution)/shard_map/ppermute | solution.py:49
  53.4 39.6 %copy-start.1 = (bf16[192,768]{1,0:T(8,128)(2,1)}, bf16[192,768]{1,0:T(8,128)(2,1)S(1)}, u32[]{:S(2)}) copy-start(bf16[192,768]{1,0:T(8,128)(2,1)S(1)} %pad_maximum_fusion.1.refs_5_) | copy-start | bytes 884740
  53.5 18.3 %collective-permute-start.21 = (bf16[192,768]{1,0:T(8,128)(2,1)S(1)}, bf16[192,768]{1,0:T(8,128)(2,1)S(1)}, u32[]{:S(2)}, u32[]{:S(2)}) collective-permute-start(bf16[192,768]{1,0:T(8,128)(2,1)S(1)} %pad_maximum_fusion.1.refs_5_), channel_id=1, source_target_pairs={{0,8},{4,12},{8,0},{12,4},{1,9},{5,13},{9,1},{13,5},{2,10},{6,14},... | collective-permute-start | bytes 884744 | tf_op jit(solution)/shard_map/ppermute | solution.py:44
  57.6 15.7 %collective-permute-start.19 = (bf16[192,768]{1,0:T(8,128)(2,1)S(1)}, bf16[192,768]{1,0:T(8,128)(2,1)S(1)}, u32[]{:S(2)}, u32[]{:S(2)}) collective-permute-start(bf16[192,768]{1,0:T(8,128)(2,1)S(1)} %pad_maximum_fusion.1.refs_5_), channel_id=1, source_target_pairs={{0,12},{4,0},{8,4},{12,8},{1,13},{5,1},{9,5},{13,9},{2,14},{6,2},{... | collective-permute-start | bytes 884744 | tf_op jit(solution)/shard_map/ppermute | solution.py:44
  60.9 20.2 %collective-permute-start.17 = (bf16[192,768]{1,0:T(8,128)(2,1)S(1)}, bf16[192,768]{1,0:T(8,128)(2,1)S(1)}, u32[]{:S(2)}, u32[]{:S(2)}) collective-permute-start(bf16[192,768]{1,0:T(8,128)(2,1)S(1)} %pad_maximum_fusion.1.refs_5_), channel_id=1, source_target_pairs={{0,4},{4,8},{8,12},{12,0},{1,5},{5,9},{9,13},{13,1},{2,6},{6,10},{... | collective-permute-start | bytes 884744 | tf_op jit(solution)/shard_map/ppermute | solution.py:44
  61.9 20.6 %collective-permute-start.14 = (bf16[128,768]{1,0:T(8,128)(2,1)S(1)}, bf16[128,768]{1,0:T(8,128)(2,1)S(1)}, u32[]{:S(2)}, u32[]{:S(2)}) collective-permute-start(bf16[128,768]{1,0:T(8,128)(2,1)S(1)} %add_convert_fusion.7), channel_id=1, source_target_pairs={{0,2},{1,3},{2,0},{3,1},{4,6},{5,7},{6,4},{7,5},{8,10},{9,11},{10,... | collective-permute-start | bytes 589832 | tf_op jit(solution)/shard_map/ppermute | solution.py:49
  62.5 20.2 %collective-permute-start.16 = (bf16[192,768]{1,0:T(8,128)(2,1)S(1)}, bf16[192,768]{1,0:T(8,128)(2,1)S(1)}, u32[]{:S(2)}, u32[]{:S(2)}) collective-permute-start(bf16[192,768]{1,0:T(8,128)(2,1)S(1)} %pad_maximum_fusion.1.refs_5_), channel_id=1, source_target_pairs={{0,16},{16,0},{1,17},{17,1},{2,18},{18,2},{3,19},{19,3},{4,20},{20... | collective-permute-start | bytes 884744 | tf_op jit(solution)/shard_map/ppermute | solution.py:44
  71.8 10.9 %collective-permute-start.22 = (bf16[192,768]{1,0:T(8,128)(2,1)S(1)}, bf16[192,768]{1,0:T(8,128)(2,1)S(1)}, u32[]{:S(2)}, u32[]{:S(2)}) collective-permute-start(bf16[192,768]{1,0:T(8,128)(2,1)S(1)} %collective-permute-done.21.refs_11_), channel_id=1, source_target_pairs={{0,16},{16,0},{1,17},{17,1},{2,18},{18,2},{3,19},{19,3},{4,20},{20... | collective-permute-start | bytes 884744 | tf_op jit(solution)/shard_map/ppermute | solution.py:44
  73.3 14.7 %collective-permute-start.20 = (bf16[192,768]{1,0:T(8,128)(2,1)S(1)}, bf16[192,768]{1,0:T(8,128)(2,1)S(1)}, u32[]{:S(2)}, u32[]{:S(2)}) collective-permute-start(bf16[192,768]{1,0:T(8,128)(2,1)S(1)} %collective-permute-done.19.refs_9_), channel_id=1, source_target_pairs={{0,16},{16,0},{1,17},{17,1},{2,18},{18,2},{3,19},{19,3},{4,20},{20... | collective-permute-start | bytes 884744 | tf_op jit(solution)/shard_map/ppermute | solution.py:44
  81.0 12.0 %collective-permute-start.18 = (bf16[192,768]{1,0:T(8,128)(2,1)S(1)}, bf16[192,768]{1,0:T(8,128)(2,1)S(1)}, u32[]{:S(2)}, u32[]{:S(2)}) collective-permute-start(bf16[192,768]{1,0:T(8,128)(2,1)S(1)} %collective-permute-done.17.refs_7_), channel_id=1, source_target_pairs={{0,16},{16,0},{1,17},{17,1},{2,18},{18,2},{3,19},{19,3},{4,20},{20... | collective-permute-start | bytes 884744 | tf_op jit(solution)/shard_map/ppermute | solution.py:44
  82.6 10.4 %collective-permute-start.15 = (bf16[128,768]{1,0:T(8,128)(2,1)S(1)}, bf16[128,768]{1,0:T(8,128)(2,1)S(1)}, u32[]{:S(2)}, u32[]{:S(2)}) collective-permute-start(bf16[128,768]{1,0:T(8,128)(2,1)S(1)} %add_convert_fusion.6.refs_1_), channel_id=1, source_target_pairs={{0,1},{1,0},{2,3},{3,2},{4,5},{5,4},{6,7},{7,6},{8,9},{9,8},{10,11... | collective-permute-start | bytes 589832 | tf_op jit(solution)/shard_map/ppermute | solution.py:49
  98.6 1.7 collective-permute-start.23
  101.3 7.0 %collective-permute-start.24 = (bf16[128,768]{1,0:T(8,128)(2,1)S(1)}, bf16[128,768]{1,0:T(8,128)(2,1)S(1)}, u32[]{:S(2)}, u32[]{:S(2)}) collective-permute-start(bf16[128,768]{1,0:T(8,128)(2,1)S(1)} %add_convert_fusion.5), channel_id=1, source_target_pairs={{0,2},{1,3},{2,0},{3,1},{4,6},{5,7},{6,4},{7,5},{8,10},{9,11},{10,... | collective-permute-start | bytes 589832 | tf_op jit(solution)/shard_map/ppermute | solution.py:49
  108.4 1.5 collective-permute-start.25
  115.5 1.7 collective-permute-start.26
  118.2 7.0 %collective-permute-start.27 = (bf16[128,768]{1,0:T(8,128)(2,1)S(1)}, bf16[128,768]{1,0:T(8,128)(2,1)S(1)}, u32[]{:S(2)}, u32[]{:S(2)}) collective-permute-start(bf16[128,768]{1,0:T(8,128)(2,1)S(1)} %add_convert_fusion.3), channel_id=1, source_target_pairs={{0,2},{1,3},{2,0},{3,1},{4,6},{5,7},{6,4},{7,5},{8,10},{9,11},{10,... | collective-permute-start | bytes 589832 | tf_op jit(solution)/shard_map/ppermute | solution.py:49
  125.3 5.3 %collective-permute-start.28 = (bf16[128,768]{1,0:T(8,128)(2,1)S(1)}, bf16[128,768]{1,0:T(8,128)(2,1)S(1)}, u32[]{:S(2)}, u32[]{:S(2)}) collective-permute-start(bf16[128,768]{1,0:T(8,128)(2,1)S(1)} %add_convert_fusion.2.refs_1_), channel_id=1, source_target_pairs={{0,1},{1,0},{2,3},{3,2},{4,5},{5,4},{6,7},{7,6},{8,9},{9,8},{10,11... | collective-permute-start | bytes 589832 | tf_op jit(solution)/shard_map/ppermute | solution.py:49
  129.1 46.9 %collective-permute-start.39 = (bf16[2,384,768]{2,1,0:T(8,128)(2,1)}, bf16[2,384,768]{2,1,0:T(8,128)(2,1)S(1)}, u32[]{:S(2)}, u32[]{:S(2)}) collective-permute-start(bf16[2,384,768]{2,1,0:T(8,128)(2,1)} %get-tuple-element.125), channel_id=1, source_target_pairs={{0,16},{16,0},{1,17},{17,1},{2,18},{18,2},{3,19},{19,3},{4,20},{20... | collective-permute-start | bytes 3538952 | tf_op jit(solution)/shard_map/ppermute | solution.py:44
  138.6 15.6 %collective-permute-start.29 = (bf16[256,384]{1,0:T(8,128)(2,1)}, bf16[256,384]{1,0:T(8,128)(2,1)S(1)}, u32[]{:S(2)}, u32[]{:S(2)}) collective-permute-start(bf16[256,384]{1,0:T(8,128)(2,1)} %get-tuple-element.99), channel_id=1, source_target_pairs={{0,4},{4,8},{8,12},{12,0},{1,5},{5,9},{9,13},{13,1},{2,6},{6,10},{... | collective-permute-start | bytes 589832 | tf_op jit(solution)/shard_map/ppermute | solution.py:44
  145.6 11.2 %collective-permute-start.30 = (bf16[256,384]{1,0:T(8,128)(2,1)}, bf16[256,384]{1,0:T(8,128)(2,1)S(1)}, u32[]{:S(2)}, u32[]{:S(2)}) collective-permute-start(bf16[256,384]{1,0:T(8,128)(2,1)} %get-tuple-element.100), channel_id=1, source_target_pairs={{0,12},{4,0},{8,4},{12,8},{1,13},{5,1},{9,5},{13,9},{2,14},{6,2},{... | collective-permute-start | bytes 589832 | tf_op jit(solution)/shard_map/ppermute | solution.py:44
  148.3 18.1 %collective-permute-start.31 = (bf16[256,384]{1,0:T(8,128)(2,1)}, bf16[256,384]{1,0:T(8,128)(2,1)S(1)}, u32[]{:S(2)}, u32[]{:S(2)}) collective-permute-start(bf16[256,384]{1,0:T(8,128)(2,1)} %get-tuple-element.101), channel_id=1, source_target_pairs={{0,8},{4,12},{8,0},{12,4},{1,9},{5,13},{9,1},{13,5},{2,10},{6,14},... | collective-permute-start | bytes 589832 | tf_op jit(solution)/shard_map/ppermute | solution.py:44
  170.3 5.0 %collective-permute-start.32 = (bf16[128,768]{1,0:T(8,128)(2,1)}, bf16[128,768]{1,0:T(8,128)(2,1)S(1)}, u32[]{:S(2)}, u32[]{:S(2)}) collective-permute-start(bf16[128,768]{1,0:T(8,128)(2,1)} %get-tuple-element.103), channel_id=1, source_target_pairs={{0,1},{1,0},{2,3},{3,2},{4,5},{5,4},{6,7},{7,6},{8,9},{9,8},{10,11... | collective-permute-start | bytes 589832 | tf_op jit(solution)/shard_map/ppermute | solution.py:49
  174.9 16.2 %collective-permute-start.35 = (bf16[392,768]{1,0:T(8,128)(2,1)}, bf16[392,768]{1,0:T(8,128)(2,1)S(1)}, u32[]{:S(2)}, u32[]{:S(2)}) collective-permute-start(bf16[392,768]{1,0:T(8,128)(2,1)} %get-tuple-element.109), channel_id=1, source_target_pairs={{0,16},{16,0},{1,17},{17,1},{2,18},{18,2},{3,19},{19,3},{4,20},{20... | collective-permute-start | bytes 1806344 | tf_op jit(solution)/shard_map/ppermute | solution.py:44
  175.4 18.8 %collective-permute-start.33 = (bf16[128,768]{1,0:T(8,128)(2,1)S(1)}, bf16[128,768]{1,0:T(8,128)(2,1)S(1)}, u32[]{:S(2)}, u32[]{:S(2)}) collective-permute-start(bf16[128,768]{1,0:T(8,128)(2,1)S(1)} %add_convert_fusion.1), channel_id=1, source_target_pairs={{0,2},{1,3},{2,0},{3,1},{4,6},{5,7},{6,4},{7,5},{8,10},{9,11},{10,... | collective-permute-start | bytes 589832 | tf_op jit(solution)/shard_map/ppermute | solution.py:49
  180.4 49.4 %collective-permute-start.40 = (bf16[2,96,768]{2,1,0:T(8,128)(2,1)}, bf16[2,96,768]{2,1,0:T(8,128)(2,1)S(1)}, u32[]{:S(2)}, u32[]{:S(2)}) collective-permute-start(bf16[2,96,768]{2,1,0:T(8,128)(2,1)} %get-tuple-element.127), channel_id=1, source_target_pairs={{0,4},{4,8},{8,12},{12,0},{1,5},{5,9},{9,13},{13,1},{2,6},{6,10},{... | collective-permute-start | bytes 884744 | tf_op jit(solution)/shard_map/ppermute | solution.py:44
  180.4 49.4 %collective-permute-start.41 = (bf16[2,96,768]{2,1,0:T(8,128)(2,1)}, bf16[2,96,768]{2,1,0:T(8,128)(2,1)S(1)}, u32[]{:S(2)}, u32[]{:S(2)}) collective-permute-start(bf16[2,96,768]{2,1,0:T(8,128)(2,1)} %get-tuple-element.128), channel_id=1, source_target_pairs={{0,12},{4,0},{8,4},{12,8},{1,13},{5,1},{9,5},{13,9},{2,14},{6,2},{... | collective-permute-start | bytes 884744 | tf_op jit(solution)/shard_map/ppermute | solution.py:44
  184.2 45.6 %collective-permute-start.42 = (bf16[2,96,768]{2,1,0:T(8,128)(2,1)}, bf16[2,96,768]{2,1,0:T(8,128)(2,1)S(1)}, u32[]{:S(2)}, u32[]{:S(2)}) collective-permute-start(bf16[2,96,768]{2,1,0:T(8,128)(2,1)} %get-tuple-element.129), channel_id=1, source_target_pairs={{0,8},{4,12},{8,0},{12,4},{1,9},{5,13},{9,1},{13,5},{2,10},{6,14},... | collective-permute-start | bytes 884744 | tf_op jit(solution)/shard_map/ppermute | solution.py:44
  194.3 14.1 %collective-permute-start.36 = (bf16[104,768]{1,0:T(8,128)(2,1)}, bf16[104,768]{1,0:T(8,128)(2,1)S(1)}, u32[]{:S(2)}, u32[]{:S(2)}) collective-permute-start(bf16[104,768]{1,0:T(8,128)(2,1)} %get-tuple-element.111), channel_id=1, source_target_pairs={{0,4},{4,8},{8,12},{12,0},{1,5},{5,9},{9,13},{13,1},{2,6},{6,10},{... | collective-permute-start | bytes 479240 | tf_op jit(solution)/shard_map/ppermute | solution.py:44
  194.3 14.1 %collective-permute-start.37 = (bf16[104,768]{1,0:T(8,128)(2,1)}, bf16[104,768]{1,0:T(8,128)(2,1)S(1)}, u32[]{:S(2)}, u32[]{:S(2)}) collective-permute-start(bf16[104,768]{1,0:T(8,128)(2,1)} %get-tuple-element.112), channel_id=1, source_target_pairs={{0,12},{4,0},{8,4},{12,8},{1,13},{5,1},{9,5},{13,9},{2,14},{6,2},{... | collective-permute-start | bytes 479240 | tf_op jit(solution)/shard_map/ppermute | solution.py:44
  198.2 28.8 %copy-start.3 = (bf16[128,768]{1,0:T(8,128)(2,1)}, bf16[128,768]{1,0:T(8,128)(2,1)S(1)}, u32[]{:S(2)}) copy-start(bf16[128,768]{1,0:T(8,128)(2,1)S(1)} %add_convert_fusion.own) | copy-start | bytes 589828
  208.4 18.5 %collective-permute-start.34 = (bf16[128,768]{1,0:T(8,128)(2,1)S(1)}, bf16[128,768]{1,0:T(8,128)(2,1)S(1)}, u32[]{:S(2)}, u32[]{:S(2)}) collective-permute-start(bf16[128,768]{1,0:T(8,128)(2,1)S(1)} %add_convert_fusion.own), channel_id=1, source_target_pairs={{0,1},{1,0},{2,3},{3,2},{4,5},{5,4},{6,7},{7,6},{8,9},{9,8},{10,11... | collective-permute-start | bytes 589832 | tf_op jit(solution)/shard_map/ppermute | solution.py:49
  208.4 14.9 %collective-permute-start.38 = (bf16[104,768]{1,0:T(8,128)(2,1)}, bf16[104,768]{1,0:T(8,128)(2,1)S(1)}, u32[]{:S(2)}, u32[]{:S(2)}) collective-permute-start(bf16[104,768]{1,0:T(8,128)(2,1)} %get-tuple-element.113), channel_id=1, source_target_pairs={{0,8},{4,12},{8,0},{12,4},{1,9},{5,13},{9,1},{13,5},{2,10},{6,14},... | collective-permute-start | bytes 479240 | tf_op jit(solution)/shard_map/ppermute | solution.py:44
  (36 other events, 225.0 us)
where the time goes:
time: 233 us
  waiting for transfers between devices  107 us (46%)
  starting transfers between devices  60.6 us (26%)
  Pallas kernels  51.7 us (22%)
  local copies, waits for them, and re-layouts  8.3 us (4%)
  other arithmetic  4.07 us (2%)
    ppermute x28, waiting for transfers between devices, ring(): lax.ppermute(value, axis, [(i, (i + step) % size) for i in range(size)])  89.6 us
    ppermute x28, starting transfers between devices, ring(): lax.ppermute(value, axis, [(i, (i + step) % size) for i in range(size)])  55.8 us
    pallas_call x13, Pallas kernels, pallas(): pl.pallas_call(kernel, out_shape=tuple((jax.ShapeDtypeStruct(s, t) for s,...  51.7 us
    ppermute x15, waiting for transfers between devices, flip(): return lax.ppermute(value, axis, [(i, i ^ bit) for i in range(size)])  17.4 us
    unnamed x82, local copies, waits for them, and re-layouts  8.3 us
    ppermute x15, starting transfers between devices, flip(): return lax.ppermute(value, axis, [(i, i ^ bit) for i in range(size)])  4.88 us
  transfers between devices with their start and end apart: 43, of which 22 were waited for; matrix products, arithmetic and copies ran while one was open for 1% of the time, Pallas kernels for 13%

commit v1 on v0

--- a/solution.py
+++ b/solution.py
@@ -13,6 +13,7 @@
 BF = jnp.bfloat16
 F32 = jnp.float32
 TAIL = 8
+SPARE = 8 << 20
 
 
 def norm_rows(hidden):
@@ -53,21 +54,24 @@
     return sorted(range(1, size), key=lambda k: min(k, size - k))
 
 
-def call(kernel, outs, args, smem=(), scratch=(), flops=0):
+def call(kernel, outs, args, smem=(), scratch=(), flops=0, spare=SPARE):
     size = sum(math.prod(s) * jnp.dtype(t).itemsize for s, t in outs)
     size += sum(a.size * a.dtype.itemsize for a in args)
     vmem = pl.BlockSpec(memory_space=pltpu.VMEM)
     table = pl.BlockSpec(memory_space=pltpu.SMEM)
-    return pallas(kernel, outs, args, smem, scratch, flops, size, vmem, table)
-
-
-def pallas(kernel, outs, args, smem, scratch, flops, size, vmem, table):
+    return pallas(kernel, outs, args, smem, scratch, flops, size, vmem, table, spare)
+
+
+def pallas(kernel, outs, args, smem, scratch, flops, size, vmem, table, spare):
+    held = sum(math.prod(s.shape) * jnp.dtype(s.dtype).itemsize for s in scratch)
+    room = size + held + spare
     return pl.pallas_call(
         kernel,
         out_shape=tuple(jax.ShapeDtypeStruct(s, t) for s, t in outs),
         in_specs=[table] * len(smem) + [vmem] * len(args),
         out_specs=tuple(vmem for _ in outs),
         scratch_shapes=list(scratch),
+        compiler_params=pltpu.CompilerParams(vmem_limit_bytes=room),
         cost_estimate=pl.CostEstimate(flops=flops, bytes_accessed=size, transcendentals=0),
     )(*smem, *args)
 
@@ -194,8 +198,8 @@
     meta, own, other, rows, small = refs[:5]
     count = z.blocks if z.direct else 1
     blocks, refs = refs[5 : 5 + count], refs[5 + count :]
-    up, down, normed_one, inverse_one, middle_b, slope, active, kept, sent = refs[:9]
-    work = refs[9]
+    up, down, normed_one, inverse_one, middle_b, slope, active, kept, sent, shown = refs[:10]
+    work = refs[10]
     row, col, lane = meta[0], meta[1], meta[2]
     if z.direct:
         for block, place in zip(blocks, block_places(z, order, row, col)):
@@ -214,13 +218,25 @@
     activated, gradient = gelu_parts(pre)
     slope[...] = gradient
     active[...] = activated.astype(BF)
+    show(z, row, middle_b, active, shown)
     work[...] = dot(active[...], down[...], 1, 1)
     split_halves(z, lane, work, kept, sent)
 
 
+def show(z, row, columns, whole, shown):
+    part = z.width // 2
+    shown[:, :part] = half_columns(z, 1 - row, columns)
+    shown[:, part:] = whole[...]
+
+
+def half_columns(z, which, columns):
+    part = z.width // 2
+    return jnp.where(which == 0, columns[:, :part], columns[:, part:])
+
+
 def middle_kernel(z, *refs):
     meta, own, other, normed_one, small, cotangent, up, down, slope = refs[:9]
-    output, d_two, d_two_b, d_pre_b, kept, sent, sums, work = refs[9:]
+    output, d_two, d_two_b, d_pre_b, kept, sent, sums, shown, work = refs[9:]
     lane = meta[2]
     place_halves(z, lane, own, other, work)
     middle = normed_one[...] * small[1:2, :] + small[2:3, :]
@@ -237,19 +253,25 @@
     d_pre = dot(d_two_b[...], down[...], 1, 0) * slope[...]
     sums[6:7, :] = jnp.sum(d_pre, axis=0, keepdims=True)
     d_pre_b[...] = d_pre.astype(BF)
+    show(z, meta[0], d_two_b, d_pre_b, shown)
     work[...] = dot(d_pre_b[...], up[...], 1, 1)
     split_halves(z, lane, work, kept, sent)
 
 
-def second_grad_kernel(z, *refs):
-    meta, middle_b, d_pre_b, d_two_b, active = refs[:5]
-    kept, sent, work = refs[5:]
-    pairs = ((middle_b, d_pre_b), (d_two_b, active))
-    for at, (left, right) in enumerate(pairs):
-        work[...] = dot(left[...], right[...], 0, 0).astype(BF)
-        part = z.width // 2
-        kept[at] = work[aligned(meta[0] * part, part), :]
-        sent[at] = work[aligned((1 - meta[0]) * part, part), :]
+def second_grad_kernel(z, order, *refs):
+    meta, middle_b, d_pre_b, d_two_b, active, acts, grads = refs[:7]
+    outs, work = refs[7:-1], refs[-1]
+    part = z.width // 2
+    total = dot(half_columns(z, meta[0], middle_b), d_pre_b[...], 0, 0)
+    total = total + dot(acts[:, :part], grads[:, part:], 0, 0)
+    work[0] = total.astype(BF)
+    total = dot(half_columns(z, meta[0], d_two_b), active[...], 0, 0)
+    total = total + dot(grads[:, :part], acts[:, part:], 0, 0)
+    work[1] = total.astype(BF)
+    for step, out in zip([0] + order, outs):
+        start = lax.rem(meta[1] + step, z.ctx) * z.shard
+        for at in range(2):
+            out[at] = work[at, aligned(start, z.shard), :]
 
 
 def second_grad_whole_kernel(*refs):
@@ -258,15 +280,14 @@
     out[1] = dot(d_two_b[...], active[...], 0, 0).astype(BF)
 
 
-def backward_kernel(z, order, *refs):
+def backward_kernel(z, *refs):
     (meta, own, other, d_two, normed_one, inverse_one, small, mixed, att, query, keys), refs = (
         refs[:11],
         refs[11:],
     )
     (probs, sums_in), refs = refs[:2], refs[2:]
-    d_one, d_one_b, d_query, d_keys, sums = refs[:5]
-    sends, refs = refs[5 : 4 + z.ctx], refs[4 + z.ctx :]
-    work, grads = refs
+    d_one, d_one_b, d_query, d_keys, sums, kept, sent = refs[:7]
+    work, grads, back = refs[7:]
     col, lane = meta[1], meta[2]
     place_halves(z, lane, own, other, work)
     d_middle = d_two[...] + work[...]
@@ -309,8 +330,12 @@
         for at in range(z.ctx):
             d_keys[at, span, :] = grads[at * z.local : (at + 1) * z.local, :].astype(BF)
     sums[7:8, : z.pair] = qv_sum
-    for step, send in zip(order, sends):
-        send[...] = d_keys[lax.rem(col + step, z.ctx)]
+    for at in range(z.ctx):
+        back[at] = dot(d_keys[at], mixed[:, z.pair :], 1, 1)
+    back[col] += dot(d_query[...], mixed[:, : z.pair], 1, 1)
+    parity = jnp.bitwise_and(lane, 1)
+    kept[...] = back[:, aligned(parity * z.half, z.half), :]
+    sent[...] = back[:, aligned((1 - parity) * z.half, z.half), :].astype(BF)
 
 
 def first_grad_kernel(z, *refs):
@@ -331,21 +356,28 @@
         out[part:, :] = sums[...].astype(BF)
 
 
-def back_kernel(z, *refs):
-    meta, d_keys, d_query, mixed = refs[:4]
-    got, refs = refs[4 : 3 + z.ctx], refs[3 + z.ctx :]
-    kept, sent, work = refs
-    total = d_keys[meta[1]].astype(F32)
-    for piece in got:
-        total = total + piece[...].astype(F32)
-    work[...] = dot(d_query[...], mixed[:, : z.pair], 1, 1)
-    work[...] += dot(total.astype(BF), mixed[:, z.pair :], 1, 1)
-    split_halves(z, meta[2], work, kept, sent)
-
-
-def token_kernel(z, meta, own, other, d_one, out, work):
-    place_halves(z, meta[2], own, other, work)
-    out[...] = (d_one[...] + work[...]).astype(BF)
+def cut_kernel(z, meta, kept, got, near, far):
+    chip = lax.shift_right_logical(meta[2], 1)
+    size = z.half // 2
+    for out, which in ((near, chip), (far, 1 - chip)):
+        span = aligned(which * size, size)
+        out[...] = (kept[:, span, :] + got[:, span, :].astype(F32)).astype(out.dtype)
+
+
+def spread_kernel(z, order, meta, kept, got, own, *sends):
+    for step, out in zip([0] + order, (own,) + sends):
+        at = lax.rem(meta[1] + step, z.ctx)
+        out[...] = (kept[at] + got[at].astype(F32)).astype(out.dtype)
+
+
+def token_kernel(z, masks, meta, *refs):
+    pieces, (d_one, out) = refs[:-2], refs[-2:]
+    size = z.rows // z.tp
+    for mask, piece in zip(masks, pieces):
+        lane = jnp.bitwise_xor(meta[2], mask)
+        start = jnp.bitwise_and(lane, 1) * z.half + lax.shift_right_logical(lane, 1) * size
+        span = aligned(start, size)
+        out[span, :] = (d_one[span, :] + piece[...].astype(F32)).astype(BF)
 
 
 def where_equal(shape, left, right):
@@ -470,12 +502,8 @@
     work[...] = (kept[...].astype(F32) + got[...].astype(F32)).astype(BF)
     for step, out in zip([0] + order, (own,) + tuple(sends)):
         start = lax.rem(meta[1] + step, z.ctx) * z.shard
-        if len(work.shape) == 3:
-            for at in range(work.shape[0]):
-                out[at] = work[at, aligned(start, z.shard), :]
-        else:
-            out[: z.shard, :] = work[aligned(start, z.shard), :]
-            out[z.shard :, :] = work[z.ctx * z.shard :, :]
+        out[: z.shard, :] = work[aligned(start, z.shard), :]
+        out[z.shard :, :] = work[z.ctx * z.shard :, :]
 
 
 def gather_blocks(order, shard):
@@ -500,8 +528,6 @@
 def reduce_shared(z, order, meta, kept, sent):
     got = ring(sent, "fsdp", 1)
     shape = kept.shape[:-2] + (kept.shape[-2] - (z.ctx - 1) * z.shard, kept.shape[-1])
-    if len(shape) == 3:
-        shape = (shape[0], z.shard, shape[2])
     pieces = call(
         functools.partial(share_kernel, z, order),
         [(shape, BF)] * z.ctx,
@@ -509,6 +535,10 @@
         smem=(meta,),
         scratch=[pltpu.VMEM(kept.shape, BF)],
     )
+    return send_pieces(order, pieces)
+
+
+def send_pieces(order, pieces):
     got = [ring(piece, "ctx", step) for step, piece in zip(order, pieces[1:])]
     return [pieces[0]] + got
 
@@ -554,6 +584,7 @@
                 *(vector.reshape(1, z.shard) for vector in vectors),
             ),
             smem=(meta,),
+            spare=58 << 20,
         )
     else:
         mixed_shard, tail = pack_plain(
@@ -600,7 +631,8 @@
         flops=4 * z.rows * z.ctx * z.width * z.pair,
     )
     own, other = sum_rows(z, kept, sent)
-    up, down, normed_one, inverse_one, middle_b, slope, active, kept, sent = call(
+    shown = ((z.rows, z.width // 2 + z.hidden), BF)
+    up, down, normed_one, inverse_one, middle_b, slope, active, kept, sent, acts = call(
         functools.partial(forward_kernel, z, order),
         [
             (square, BF),
@@ -612,6 +644,7 @@
             (full, BF),
             (half, F32),
             (half, BF),
+            shown,
         ],
         (own, other, rows, small, *second_blocks),
         smem=(meta,),
@@ -619,7 +652,7 @@
         flops=4 * z.rows * z.width * z.hidden,
     )
     own, other = sum_rows(z, kept, sent)
-    output, d_two, d_two_b, d_pre_b, kept, sent, sums = call(
+    output, d_two, d_two_b, d_pre_b, kept, sent, sums, grads = call(
         functools.partial(middle_kernel, z),
         [
             (full, BF),
@@ -629,6 +662,7 @@
             (half, F32),
             (half, BF),
             ((TAIL, z.width), F32),
+            shown,
         ],
         (own, other, normed_one, small, cotangent.reshape(full), up, down, slope),
         smem=(meta,),
@@ -638,15 +672,17 @@
     grad_args = (middle_b, d_pre_b, d_two_b, active)
     grad_flops = 4 * z.rows * z.width * z.hidden
     if z.direct:
-        part = (2, z.width // 2, z.hidden)
-        kept_two, sent_two = call(
-            functools.partial(second_grad_kernel, z),
-            [(part, BF), (part, BF)],
-            grad_args,
+        acts = ring(acts, "fsdp", 1)
+        grads = ring(grads, "fsdp", 1)
+        second = call(
+            functools.partial(second_grad_kernel, z, order),
+            [((2, z.shard, z.hidden), BF)] * z.ctx,
+            (*grad_args, acts, grads),
             smem=(meta,),
-            scratch=[pltpu.VMEM(square, BF)],
+            scratch=[pltpu.VMEM((2, z.width // 2, z.hidden), BF)],
             flops=grad_flops,
         )
+        second = send_pieces(order, second)
     else:
         (second_grads,) = call(
             second_grad_whole_kernel,
@@ -656,22 +692,46 @@
             flops=grad_flops,
         )
     own, other = sum_rows(z, kept, sent)
-    d_one, d_one_b, d_query, d_keys, sums, *sends = call(
-        functools.partial(backward_kernel, z, order),
+    terms_of = (z.ctx, z.half, z.width)
+    d_one, d_one_b, d_query, d_keys, sums, kept, sent = call(
+        functools.partial(backward_kernel, z),
         [
             (full, F32),
             (full, BF),
             ((z.rows, z.pair), BF),
             ((z.ctx, z.rows, z.pair), BF),
             ((TAIL, z.width), F32),
-        ]
-        + [((z.rows, z.pair), BF)] * (z.ctx - 1),
+            (terms_of, F32),
+            (terms_of, BF),
+        ],
         (own, other, d_two, normed_one, inverse_one, small, mixed, att, query, keys, probs, sums),
         smem=(meta,),
-        scratch=[pltpu.VMEM(full, F32), pltpu.VMEM((z.total, z.pair), F32)],
+        scratch=[
+            pltpu.VMEM(full, F32),
+            pltpu.VMEM((z.total, z.pair), F32),
+            pltpu.VMEM((z.ctx,) + full, F32),
+        ],
         flops=10 * z.rows * z.heads * z.total * z.pair,
     )
-    got = [ring(piece, "ctx", step) for step, piece in zip(order, sends)]
+    terms_of = (z.ctx, z.half // 2, z.width)
+    near, far = call(
+        functools.partial(cut_kernel, z),
+        [(terms_of, F32), (terms_of, BF)],
+        (kept, flip(sent, "tp", 1)),
+        smem=(meta,),
+    )
+    quarter = terms_of[1:]
+    total, *sends = call(
+        functools.partial(spread_kernel, z, order),
+        [(quarter, F32)] + [(quarter, BF)] * (z.ctx - 1),
+        (near, flip(far, "tp", 2)),
+        smem=(meta,),
+    )
+    for step, piece in zip(order, sends):
+        total = total + ring(piece, "ctx", step).astype(F32)
+    total = total.astype(BF)
+    backs = [total, flip(total, "tp", 2)]
+    backs += [flip(piece, "tp", 1) for piece in backs]
     if z.direct:
         part = (z.width // 2 + TAIL, z.width)
         grad_outs = [(part, BF), (part, BF)]
@@ -685,25 +745,14 @@
         scratch=[pltpu.VMEM(square, BF)],
         flops=2 * z.rows * (z.ctx + 2) * z.width * z.pair,
     )
-    kept, sent = call(
-        functools.partial(back_kernel, z),
-        [(half, F32), (half, BF)],
-        (d_keys, d_query, mixed, *got),
+    (token_grad,) = call(
+        functools.partial(token_kernel, z, [0, 2, 1, 3]),
+        [(full, BF)],
+        (*backs, d_one),
         smem=(meta,),
-        scratch=[pltpu.VMEM(full, F32)],
-        flops=4 * z.rows * z.width * z.pair,
-    )
-    own, other = sum_rows(z, kept, sent)
-    (token_grad,) = call(
-        functools.partial(token_kernel, z),
-        [(full, BF)],
-        (own, other, d_one),
-        smem=(meta,),
-        scratch=[pltpu.VMEM(full, F32)],
     )
 
     if z.direct:
-        second = reduce_shared(z, order, meta, kept_two, sent_two)
         first = reduce_shared(z, order, meta, *first_parts)
         g_up, g_down_t = call(
             functools.partial(finish_second_kernel, z),

time: 233 us -> 194 us (0.83)
  Pallas kernels: 51.7 us -> 28.9 us
  starting transfers between devices: 60.6 us -> 51.5 us
  local copies, waits for them, and re-layouts: 8.3 us -> 0.94 us
  other arithmetic: 4.07 us -> 0.97 us
  waiting for transfers between devices: 107 us -> 110 us
    pallas_call x13, Pallas kernels: 51.7 us -> 28.9 us  [pallas(): pl.pallas_call(kernel, out_shape=tuple((jax.ShapeDtypeStruct(s, t) for s,...]
    ppermute x28 -> x29, starting transfers between devices: 55.8 us -> 45.2 us  [ring(): lax.ppermute(value, axis, [(i, (i + step) % size) for i in range(size)])]
    ppermute x15 -> x17, waiting for transfers between devices: 17.4 us -> 25.5 us  [flip(): return lax.ppermute(value, axis, [(i, i ^ bit) for i in range(size)])]
    unnamed x82 -> x14, local copies, waits for them, and re-layouts: 8.3 us -> 0.94 us
    ppermute x28 -> x29, waiting for transfers between devices: 89.6 us -> 84.6 us  [ring(): lax.ppermute(value, axis, [(i, (i + step) % size) for i in range(size)])]
    convert_element_type x4 -> x3, other arithmetic: 3.14 us -> 0.12 us  [sum_rows(): mine = total.astype(BF)]
    ppermute x15 -> x17, starting transfers between devices: 4.88 us -> 6.32 us  [flip(): return lax.ppermute(value, axis, [(i, i ^ bit) for i in range(size)])]
  transfers between devices with their start and end apart: 43 -> 46, of which waited for: 22 -> 24; matrix products, arithmetic and copies ran while one was open for 1% -> 0% of each run, Pallas kernels for 13% -> 5%
where the time goes in v1:
time: 194 us; the launch traced here: 193 us
  waiting for transfers between devices  110 us (57%)
  starting transfers between devices  51.5 us (27%)
  Pallas kernels  28.9 us (15%)
    ppermute x29, waiting for transfers between devices, ring(): lax.ppermute(value, axis, [(i, (i + step) % size) for i in range(size)])  84.6 us
    ppermute x29, starting transfers between devices, ring(): lax.ppermute(value, axis, [(i, (i + step) % size) for i in range(size)])  45.2 us
    pallas_call x13, Pallas kernels, pallas(): pl.pallas_call(kernel, out_shape=tuple((jax.ShapeDtypeStruct(s, t) for s,...  28.9 us
    ppermute x17, waiting for transfers between devices, flip(): return lax.ppermute(value, axis, [(i, i ^ bit) for i in range(size)])  25.5 us
    ppermute x17, starting transfers between devices, flip(): return lax.ppermute(value, axis, [(i, i ^ bit) for i in range(size)])  6.32 us
  transfers between devices with their start and end apart: 46, of which 24 were waited for; matrix products, arithmetic and copies ran while one was open for 0% of the time, Pallas kernels for 5%

profile of v1, /device:TPU:0, one launch (start us, length us, event | category | flops | bytes accessed | tf_op | source)
XLA Modules:
  0.0 193.5 jit_solution(13914825161637490588)
XLA Ops:
  1.3 2.4 %shard_map.254 = (bf16[104,768]{1,0:T(8,128)(2,1)}, bf16[64,768]{1,0:T(8,128)(2,1)}) custom-call(s32[3]{0:T(128)} %pad_add_fusion.refs_0_.meta, bf16[3,96,192]{2,1,0:T(8,128)(2,1)} %refs_1_.2, bf16[192,96]{1,0:T(8,128)(2,1)} %refs_2_.1, bf16[8,12]{1,0:T(8,128)(2,1)} %bitcast.38, bf16[3,2,8]{2,1,0:T(2,128)(2,1)} %bitcast.39, bf16[256,768]{1,0:T(8,128)(2,1)} %bitcast.28, ...), custom_call_target="tpu_custom_call" | custom-call | bytes 800160 | tf_op jit(solution)/shard_map/pallas_call | solution.py:68
  3.6 3.1 %collective-permute-start.7 = (bf16[64,768]{1,0:T(8,128)(2,1)}, bf16[64,768]{1,0:T(8,128)(2,1)S(1)}, u32[]{:S(2)}, u32[]{:S(2)}) collective-permute-start(bf16[64,768]{1,0:T(8,128)(2,1)} %get-tuple-element.79), channel_id=1, source_target_pairs={{0,4},{4,8},{8,12},{12,0},{1,5},{5,9},{9,13},{13,1},{2,6},{6,10},{... | collective-permute-start | bytes 294920 | tf_op jit(solution)/shard_map/ppermute | solution.py:45
  6.7 2.1 %collective-permute-start.8 = (bf16[64,768]{1,0:T(8,128)(2,1)}, bf16[64,768]{1,0:T(8,128)(2,1)S(1)}, u32[]{:S(2)}, u32[]{:S(2)}) collective-permute-start(bf16[64,768]{1,0:T(8,128)(2,1)} %get-tuple-element.79), channel_id=1, source_target_pairs={{0,12},{4,0},{8,4},{12,8},{1,13},{5,1},{9,5},{13,9},{2,14},{6,2},{... | collective-permute-start | bytes 294920 | tf_op jit(solution)/shard_map/ppermute | solution.py:45
  9.7 2.6 %collective-permute-done.7 = bf16[64,768]{1,0:T(8,128)(2,1)S(1)} collective-permute-done((bf16[64,768]{1,0:T(8,128)(2,1)}, bf16[64,768]{1,0:T(8,128)(2,1)S(1)}, u32[]{:S(2)}, u32[]{:S(2)}) %collective-permute-start.7) | collective-permute-done | bytes 98336 | tf_op jit(solution)/shard_map/ppermute | solution.py:45
  13.3 4.8 %collective-permute-done.9 = bf16[64,768]{1,0:T(8,128)(2,1)S(1)} collective-permute-done((bf16[64,768]{1,0:T(8,128)(2,1)}, bf16[64,768]{1,0:T(8,128)(2,1)S(1)}, u32[]{:S(2)}, u32[]{:S(2)}) %collective-permute-start.9) | collective-permute-done | bytes 98336 | tf_op jit(solution)/shard_map/ppermute | solution.py:45
  18.1 1.6 collective-permute-start.10
  19.6 3.8 %collective-permute-start.3 = (bf16[104,768]{1,0:T(8,128)(2,1)}, bf16[104,768]{1,0:T(8,128)(2,1)S(1)}, u32[]{:S(2)}, u32[]{:S(2)}) collective-permute-start(bf16[104,768]{1,0:T(8,128)(2,1)} %get-tuple-element.78.refs_2_), channel_id=1, source_target_pairs={{0,12},{4,0},{8,4},{12,8},{1,13},{5,1},{9,5},{13,9},{2,14},{6,2},{... | collective-permute-start | bytes 479240 | tf_op jit(solution)/shard_map/ppermute | solution.py:45
  23.5 1.5 collective-permute-start
  25.0 3.6 %collective-permute-done.1.refs_4_ = bf16[104,768]{1,0:T(8,128)(2,1)S(1)} collective-permute-done((bf16[104,768]{1,0:T(8,128)(2,1)}, bf16[104,768]{1,0:T(8,128)(2,1)S(1)}, u32[]{:S(2)}, u32[]{:S(2)}) %collective-permute-start.1) | collective-permute-done | bytes 159776 | tf_op jit(solution)/shard_map/ppermute | solution.py:45
  29.5 1.5 collective-permute-start.2
  31.0 5.2 %collective-permute-done.5.refs_8_ = bf16[104,768]{1,0:T(8,128)(2,1)S(1)} collective-permute-done((bf16[104,768]{1,0:T(8,128)(2,1)}, bf16[104,768]{1,0:T(8,128)(2,1)S(1)}, u32[]{:S(2)}, u32[]{:S(2)}) %collective-permute-start.5) | collective-permute-done | bytes 159776 | tf_op jit(solution)/shard_map/ppermute | solution.py:45
  36.2 1.5 collective-permute-start.4
  38.3 4.7 %collective-permute-done.4.refs_7_ = bf16[104,768]{1,0:T(8,128)(2,1)S(1)} collective-permute-done((bf16[104,768]{1,0:T(8,128)(2,1)S(1)}, bf16[104,768]{1,0:T(8,128)(2,1)S(1)}, u32[]{:S(2)}, u32[]{:S(2)}) %collective-permute-start.4) | collective-permute-done | bytes 159776 | tf_op jit(solution)/shard_map/ppermute | solution.py:45
  42.9 1.7 collective-permute-done.6.refs_9_
  45.6 5.8 %shard_map.255 = (bf16[768,768]{1,0:T(8,128)(2,1)S(1)}, f32[8,768]{1,0:T(8,128)S(1)}, bf16[4,256,768]{2,1,0:T(8,128)(2,1)S(1)}, bf16[2,512,384]{2,1,0:T(8,128)(2...) custom-call(s32[3]{0:T(128)S(1)} %copy-done.2, ...), custom_call_target="tpu_custom_call" | custom-call | flops 1207959552 | bytes 8183808 | tf_op jit(solution)/shard_map/pallas_call | solution.py:68
  51.6 3.8 %collective-permute-start.19 = (bf16[192,768]{1,0:T(8,128)(2,1)S(1)}, bf16[192,768]{1,0:T(8,128)(2,1)S(1)}, u32[]{:S(2)}, u32[]{:S(2)}) collective-permute-start(bf16[192,768]{1,0:T(8,128)(2,1)S(1)} %pad_maximum_fusion.1.refs_5_), channel_id=1, source_target_pairs={{0,12},{4,0},{8,4},{12,8},{1,13},{5,1},{9,5},{13,9},{2,14},{6,2},{... | collective-permute-start | bytes 884744 | tf_op jit(solution)/shard_map/ppermute | solution.py:45
  56.0 1.5 collective-permute-start.16
  57.5 5.7 %collective-permute-done.17.refs_7_ = bf16[192,768]{1,0:T(8,128)(2,1)S(1)} collective-permute-done((bf16[192,768]{1,0:T(8,128)(2,1)S(1)}, bf16[192,768]{1,0:T(8,128)(2,1)S(1)}, u32[]{:S(2)}, u32[]{:S(2)}) %collective-permute-start.17) | collective-permute-done | bytes 294944 | tf_op jit(solution)/shard_map/ppermute | solution.py:45
  63.3 1.5 collective-permute-start.18
  64.8 4.7 %collective-permute-done.19.refs_9_ = bf16[192,768]{1,0:T(8,128)(2,1)S(1)} collective-permute-done((bf16[192,768]{1,0:T(8,128)(2,1)S(1)}, bf16[192,768]{1,0:T(8,128)(2,1)S(1)}, u32[]{:S(2)}, u32[]{:S(2)}) %collective-permute-start.19) | collective-permute-done | bytes 294944 | tf_op jit(solution)/shard_map/ppermute | solution.py:45
  69.4 1.5 collective-permute-start.20
  70.9 8.8 %collective-permute-done.21.refs_11_ = bf16[192,768]{1,0:T(8,128)(2,1)S(1)} collective-permute-done((bf16[192,768]{1,0:T(8,128)(2,1)S(1)}, bf16[192,768]{1,0:T(8,128)(2,1)S(1)}, u32[]{:S(2)}, u32[]{:S(2)}) %collective-permute-start.21) | collective-permute-done | bytes 294944 | tf_op jit(solution)/shard_map/ppermute | solution.py:45
  79.7 1.5 collective-permute-start.22
  81.4 6.6 %collective-permute-done.22.refs_12_ = bf16[192,768]{1,0:T(8,128)(2,1)S(1)} collective-permute-done((bf16[192,768]{1,0:T(8,128)(2,1)S(1)}, bf16[192,768]{1,0:T(8,128)(2,1)S(1)}, u32[]{:S(2)}, u32[]{:S(2)}) %collective-permute-start.22) | collective-permute-done | bytes 294944 | tf_op jit(solution)/shard_map/ppermute | solution.py:45
  88.0 2.2 %shard_map.256 = (bf16[768,768]{1,0:T(8,128)(2,1)S(1)}, bf16[768,768]{1,0:T(8,128)(2,1)S(1)}, f32[256,768]{1,0:T(8,128)S(1)}, f32[256,1]{1,0:T(8,128)S(1)}, bf16...) custom-call(s32[3]{0:T(128)S(1)} %copy-done.2, ...), custom_call_target="tpu_custom_call" | custom-call | flops 603979776 | bytes 9069568 | tf_op jit(solution)/shard_map/pallas_call | solution.py:68
  90.3 1.4 collective-permute-done.23
  92.3 6.4 %collective-permute-done.24 = bf16[128,768]{1,0:T(8,128)(2,1)S(1)} collective-permute-done((bf16[128,768]{1,0:T(8,128)(2,1)S(1)}, bf16[128,768]{1,0:T(8,128)(2,1)S(1)}, u32[]{:S(2)}, u32[]{:S(2)}) %collective-permute-start.24) | collective-permute-done | bytes 196640 | tf_op jit(solution)/shard_map/ppermute | solution.py:50
  98.9 1.4 collective-permute-done.25.refs_2_
  100.3 2.7 %shard_map.257 = (bf16[256,768]{1,0:T(8,128)(2,1)}, f32[256,768]{1,0:T(8,128)S(1)}, bf16[256,768]{1,0:T(8,128)(2,1)S(1)}, bf16[256,768]{1,0:T(8,128)(2,1)S(1)}, ...) custom-call(s32[3]{0:T(128)S(1)} %copy-done.2, ...), custom_call_target="tpu_custom_call" | custom-call | flops 603979776 | bytes 7913472 | tf_op jit(solution)/shard_map/pallas_call | solution.py:68
  103.2 1.3 collective-permute-done.26
  105.1 6.4 %collective-permute-done.27 = bf16[128,768]{1,0:T(8,128)(2,1)S(1)} collective-permute-done((bf16[128,768]{1,0:T(8,128)(2,1)S(1)}, bf16[128,768]{1,0:T(8,128)(2,1)S(1)}, u32[]{:S(2)}, u32[]{:S(2)}) %collective-permute-start.27) | collective-permute-done | bytes 196640 | tf_op jit(solution)/shard_map/ppermute | solution.py:50
  111.7 1.4 collective-permute-done.28.refs_2_
  113.1 5.6 %shard_map.258 = (f32[256,768]{1,0:T(8,128)S(1)}, bf16[256,768]{1,0:T(8,128)(2,1)S(1)}, bf16[256,384]{1,0:T(8,128)(2,1)S(1)}, bf16[4,256,384]{2,1,0:T(8,128)(2,1...) custom-call(s32[3]{0:T(128)S(1)} %copy-done.2, ...), custom_call_target="tpu_custom_call" | custom-call | flops 1509949440 | bytes 9708544 | tf_op jit(solution)/shard_map/pallas_call | solution.py:68
  118.9 1.5 collective-permute-start.41
  122.3 2.0 %shard_map.262 = (bf16[392,768]{1,0:T(8,128)(2,1)S(1)}, bf16[392,768]{1,0:T(8,128)(2,1)S(1)}) custom-call(s32[3]{0:T(128)S(1)} %copy-done.2, bf16[256,768]{1,0:T(8,128)(2,1)S(1)} %bitcast.31, bf16[4,256,768]{2,1,0:T(8,128)(2,1)S(1)} %get-tuple-element.109.refs_2_, bf16[256,384]{1,0:T(8,128)(2,1)S(1)} %get-tuple-element.110.refs_3_, ...), custom_call_target="tpu_custom_call" | custom-call | flops 905969664 | bytes 4767744 | tf_op jit(solution)/shard_map/pallas_call | solution.py:68
  124.4 1.6 collective-permute-start.37
  126.0 7.0 %collective-permute-done.30.got = bf16[4,64,768]{2,1,0:T(8,128)(2,1)S(1)} collective-permute-done((bf16[4,64,768]{2,1,0:T(8,128)(2,1)S(1)}, bf16[4,64,768]{2,1,0:T(8,128)(2,1)S(1)}, u32[]{:S(2)}, u32[]{:S(2)}) %collective-permute-start.30) | collective-permute-done | bytes 393248 | tf_op jit(solution)/shard_map/ppermute | solution.py:50
  133.7 3.8 %collective-permute-start.32 = (bf16[64,768]{1,0:T(8,128)(2,1)S(1)}, bf16[64,768]{1,0:T(8,128)(2,1)S(1)}, u32[]{:S(2)}, u32[]{:S(2)}) collective-permute-start(bf16[64,768]{1,0:T(8,128)(2,1)S(1)} %get-tuple-element.106), channel_id=1, source_target_pairs={{0,12},{4,0},{8,4},{12,8},{1,13},{5,1},{9,5},{13,9},{2,14},{6,2},{... | collective-permute-start | bytes 294920 | tf_op jit(solution)/shard_map/ppermute | solution.py:45
  137.5 10.3 %collective-permute-done.42.refs_6_ = bf16[256,1152]{1,0:T(8,128)(2,1)S(1)} collective-permute-done((bf16[256,1152]{1,0:T(8,128)(2,1)S(1)}, bf16[256,1152]{1,0:T(8,128)(2,1)S(1)}, u32[]{:S(2)}, u32[]{:S(2)}) %collective-permute-start.42) | collective-permute-done | bytes 589856 | tf_op jit(solution)/shard_map/ppermute | solution.py:45
  147.8 1.5 shard_map.265
  149.3 3.8 %collective-permute-start.44 = (bf16[2,96,768]{2,1,0:T(8,128)(2,1)S(1)}, bf16[2,96,768]{2,1,0:T(8,128)(2,1)S(1)}, u32[]{:S(2)}, u32[]{:S(2)}) collective-permute-start(bf16[2,96,768]{2,1,0:T(8,128)(2,1)S(1)} %get-tuple-element.134), channel_id=1, source_target_pairs={{0,12},{4,0},{8,4},{12,8},{1,13},{5,1},{9,5},{13,9},{2,14},{6,2},{... | collective-permute-start | bytes 884744 | tf_op jit(solution)/shard_map/ppermute | solution.py:45
  153.8 6.3 %collective-permute-done.37.refs_2_ = bf16[392,768]{1,0:T(8,128)(2,1)S(1)} collective-permute-done((bf16[392,768]{1,0:T(8,128)(2,1)S(1)}, bf16[392,768]{1,0:T(8,128)(2,1)S(1)}, u32[]{:S(2)}, u32[]{:S(2)}) %collective-permute-start.37) | collective-permute-done | bytes 602144 | tf_op jit(solution)/shard_map/ppermute | solution.py:45
  161.0 6.6 %collective-permute-start.39 = (bf16[104,768]{1,0:T(8,128)(2,1)S(1)}, bf16[104,768]{1,0:T(8,128)(2,1)S(1)}, u32[]{:S(2)}, u32[]{:S(2)}) collective-permute-start(bf16[104,768]{1,0:T(8,128)(2,1)S(1)} %get-tuple-element.118), channel_id=1, source_target_pairs={{0,12},{4,0},{8,4},{12,8},{1,13},{5,1},{9,5},{13,9},{2,14},{6,2},{... | collective-permute-start | bytes 479240 | tf_op jit(solution)/shard_map/ppermute | solution.py:45
  167.6 2.4 %collective-permute-start.40 = (bf16[104,768]{1,0:T(8,128)(2,1)S(1)}, bf16[104,768]{1,0:T(8,128)(2,1)S(1)}, u32[]{:S(2)}, u32[]{:S(2)}) collective-permute-start(bf16[104,768]{1,0:T(8,128)(2,1)S(1)} %get-tuple-element.119), channel_id=1, source_target_pairs={{0,8},{4,12},{8,0},{12,4},{1,9},{5,13},{9,1},{13,5},{2,10},{6,14},... | collective-permute-start | bytes 479240 | tf_op jit(solution)/shard_map/ppermute | solution.py:45
  170.0 14.8 %collective-permute-done.45.refs_3_ = bf16[2,96,768]{2,1,0:T(8,128)(2,1)S(1)} collective-permute-done((bf16[2,96,768]{2,1,0:T(8,128)(2,1)S(1)}, bf16[2,96,768]{2,1,0:T(8,128)(2,1)S(1)}, u32[]{:S(2)}, u32[]{:S(2)}) %collective-permute-start.45) | collective-permute-done | bytes 294944 | tf_op jit(solution)/shard_map/ppermute | solution.py:45
  186.2 3.6 %collective-permute-done.40.refs_3_ = bf16[104,768]{1,0:T(8,128)(2,1)S(1)} collective-permute-done((bf16[104,768]{1,0:T(8,128)(2,1)S(1)}, bf16[104,768]{1,0:T(8,128)(2,1)S(1)}, u32[]{:S(2)}, u32[]{:S(2)}) %collective-permute-start.40) | collective-permute-done | bytes 159776 | tf_op jit(solution)/shard_map/ppermute | solution.py:45
  189.8 2.3 %shard_map.264 = (f32[3,96,192]{2,1,0:T(8,128)}, f32[192,96]{1,0:T(8,128)}, f32[8,12]{1,0:T(8,128)}, f32[3,2,8]{2,1,0:T(2,128)}, f32[1,96]{1,0:T(1,128)}, /*inde...) custom-call(s32[3]{0:T(128)S(1)} %copy-done.2, ...), custom_call_target="tpu_custom_call" | custom-call | bytes 936768 | tf_op jit(solution)/shard_map/pallas_call | solution.py:68
  192.1 1.4 shard_map.261
  (81 shorter events, 13.4 us)
Async XLA Ops:
  0.6 44.0 %copy-start = (bf16[2,128,768]{2,1,0:T(8,128)(2,1)S(1)}, bf16[2,128,768]{2,1,0:T(8,128)(2,1)}, u32[]{:S(2)}) copy-start(bf16[2,128,768]{2,1,0:T(8,128)(2,1)} %param.15) | copy-start | bytes 1179652
  0.7 44.0 %copy-start.4 = (s32[2,6]{1,0:T(2,128)S(1)}, s32[2,6]{1,0:T(2,128)}, u32[]{:S(2)}) copy-start(s32[2,6]{1,0:T(2,128)} %refs_1_.3) | copy-start | bytes 148
  3.6 8.7 %collective-permute-start.7 = (bf16[64,768]{1,0:T(8,128)(2,1)}, bf16[64,768]{1,0:T(8,128)(2,1)S(1)}, u32[]{:S(2)}, u32[]{:S(2)}) collective-permute-start(bf16[64,768]{1,0:T(8,128)(2,1)} %get-tuple-element.79), channel_id=1, source_target_pairs={{0,4},{4,8},{8,12},{12,0},{1,5},{5,9},{9,13},{13,1},{2,6},{6,10},{... | collective-permute-start | bytes 294920 | tf_op jit(solution)/shard_map/ppermute | solution.py:45
  6.7 6.6 %collective-permute-start.8 = (bf16[64,768]{1,0:T(8,128)(2,1)}, bf16[64,768]{1,0:T(8,128)(2,1)S(1)}, u32[]{:S(2)}, u32[]{:S(2)}) collective-permute-start(bf16[64,768]{1,0:T(8,128)(2,1)} %get-tuple-element.79), channel_id=1, source_target_pairs={{0,12},{4,0},{8,4},{12,8},{1,13},{5,1},{9,5},{13,9},{2,14},{6,2},{... | collective-permute-start | bytes 294920 | tf_op jit(solution)/shard_map/ppermute | solution.py:45
  8.8 9.3 %collective-permute-start.9 = (bf16[64,768]{1,0:T(8,128)(2,1)}, bf16[64,768]{1,0:T(8,128)(2,1)S(1)}, u32[]{:S(2)}, u32[]{:S(2)}) collective-permute-start(bf16[64,768]{1,0:T(8,128)(2,1)} %get-tuple-element.79), channel_id=1, source_target_pairs={{0,8},{4,12},{8,0},{12,4},{1,9},{5,13},{9,1},{13,5},{2,10},{6,14},... | collective-permute-start | bytes 294920 | tf_op jit(solution)/shard_map/ppermute | solution.py:45
  18.1 10.6 %collective-permute-start.10 = (bf16[3,64,768]{2,1,0:T(8,128)(2,1)S(1)}, bf16[3,64,768]{2,1,0:T(8,128)(2,1)S(1)}, u32[]{:S(2)}, u32[]{:S(2)}) collective-permute-start(bf16[3,64,768]{2,1,0:T(8,128)(2,1)S(1)} %pad_maximum_fusion.refs_11_), channel_id=1, source_target_pairs={{0,2},{1,3},{2,0},{3,1},{4,6},{5,7},{6,4},{7,5},{8,10},{9,11},{10,... | collective-permute-start | bytes 884744 | tf_op jit(solution)/shard_map/ppermute | solution.py:50
  19.6 9.0 %collective-permute-start.1 = (bf16[104,768]{1,0:T(8,128)(2,1)}, bf16[104,768]{1,0:T(8,128)(2,1)S(1)}, u32[]{:S(2)}, u32[]{:S(2)}) collective-permute-start(bf16[104,768]{1,0:T(8,128)(2,1)} %get-tuple-element.78.refs_2_), channel_id=1, source_target_pairs={{0,4},{4,8},{8,12},{12,0},{1,5},{5,9},{9,13},{13,1},{2,6},{6,10},{... | collective-permute-start | bytes 479240 | tf_op jit(solution)/shard_map/ppermute | solution.py:45
  19.6 9.9 %collective-permute-start.3 = (bf16[104,768]{1,0:T(8,128)(2,1)}, bf16[104,768]{1,0:T(8,128)(2,1)S(1)}, u32[]{:S(2)}, u32[]{:S(2)}) collective-permute-start(bf16[104,768]{1,0:T(8,128)(2,1)} %get-tuple-element.78.refs_2_), channel_id=1, source_target_pairs={{0,12},{4,0},{8,4},{12,8},{1,13},{5,1},{9,5},{13,9},{2,14},{6,2},{... | collective-permute-start | bytes 479240 | tf_op jit(solution)/shard_map/ppermute | solution.py:45
  23.5 12.8 %collective-permute-start.5 = (bf16[104,768]{1,0:T(8,128)(2,1)}, bf16[104,768]{1,0:T(8,128)(2,1)S(1)}, u32[]{:S(2)}, u32[]{:S(2)}) collective-permute-start(bf16[104,768]{1,0:T(8,128)(2,1)} %get-tuple-element.78.refs_2_), channel_id=1, source_target_pairs={{0,8},{4,12},{8,0},{12,4},{1,9},{5,13},{9,1},{13,5},{2,10},{6,14},... | collective-permute-start | bytes 479240 | tf_op jit(solution)/shard_map/ppermute | solution.py:45
  23.5 14.3 %collective-permute-start = (bf16[104,768]{1,0:T(8,128)(2,1)}, bf16[104,768]{1,0:T(8,128)(2,1)S(1)}, u32[]{:S(2)}, u32[]{:S(2)}) collective-permute-start(bf16[104,768]{1,0:T(8,128)(2,1)} %get-tuple-element.78.refs_2_), channel_id=1, source_target_pairs={{0,16},{16,0},{1,17},{17,1},{2,18},{18,2},{3,19},{19,3},{4,20},{20... | collective-permute-start | bytes 479240 | tf_op jit(solution)/shard_map/ppermute | solution.py:45
  28.6 16.0 %collective-permute-start.11 = (bf16[3,64,768]{2,1,0:T(8,128)(2,1)S(1)}, bf16[3,64,768]{2,1,0:T(8,128)(2,1)S(1)}, u32[]{:S(2)}, u32[]{:S(2)}) collective-permute-start(bf16[3,64,768]{2,1,0:T(8,128)(2,1)S(1)} %pad_maximum_fusion.refs_11_), channel_id=1, source_target_pairs={{0,1},{1,0},{2,3},{3,2},{4,5},{5,4},{6,7},{7,6},{8,9},{9,8},{10,11... | collective-permute-start | bytes 884744 | tf_op jit(solution)/shard_map/ppermute | solution.py:50
  28.6 16.0 %collective-permute-start.12 = (bf16[3,64,768]{2,1,0:T(8,128)(2,1)S(1)}, bf16[3,64,768]{2,1,0:T(8,128)(2,1)S(1)}, u32[]{:S(2)}, u32[]{:S(2)}) collective-permute-start(bf16[3,64,768]{2,1,0:T(8,128)(2,1)S(1)} %collective-permute-done.10.refs_12_), channel_id=1, source_target_pairs={{0,1},{1,0},{2,3},{3,2},{4,5},{5,4},{6,7},{7,6},{8,9},{9,8},{10,11... | collective-permute-start | bytes 884744 | tf_op jit(solution)/shard_map/ppermute | solution.py:50
  29.5 8.7 %collective-permute-start.2 = (bf16[104,768]{1,0:T(8,128)(2,1)S(1)}, bf16[104,768]{1,0:T(8,128)(2,1)S(1)}, u32[]{:S(2)}, u32[]{:S(2)}) collective-permute-start(bf16[104,768]{1,0:T(8,128)(2,1)S(1)} %collective-permute-done.1.refs_4_), channel_id=1, source_target_pairs={{0,16},{16,0},{1,17},{17,1},{2,18},{18,2},{3,19},{19,3},{4,20},{20... | collective-permute-start | bytes 479240 | tf_op jit(solution)/shard_map/ppermute | solution.py:45
  36.2 6.7 %collective-permute-start.4 = (bf16[104,768]{1,0:T(8,128)(2,1)S(1)}, bf16[104,768]{1,0:T(8,128)(2,1)S(1)}, u32[]{:S(2)}, u32[]{:S(2)}) collective-permute-start(bf16[104,768]{1,0:T(8,128)(2,1)S(1)} %collective-permute-done.3.refs_6_), channel_id=1, source_target_pairs={{0,16},{16,0},{1,17},{17,1},{2,18},{18,2},{3,19},{19,3},{4,20},{20... | collective-permute-start | bytes 479240 | tf_op jit(solution)/shard_map/ppermute | solution.py:45
  37.7 6.9 %collective-permute-start.6 = (bf16[104,768]{1,0:T(8,128)(2,1)S(1)}, bf16[104,768]{1,0:T(8,128)(2,1)S(1)}, u32[]{:S(2)}, u32[]{:S(2)}) collective-permute-start(bf16[104,768]{1,0:T(8,128)(2,1)S(1)} %collective-permute-done.5.refs_8_), channel_id=1, source_target_pairs={{0,16},{16,0},{1,17},{17,1},{2,18},{18,2},{3,19},{19,3},{4,20},{20... | collective-permute-start | bytes 479240 | tf_op jit(solution)/shard_map/ppermute | solution.py:45
  51.4 4.0 %collective-permute-start.13 = (bf16[128,768]{1,0:T(8,128)(2,1)S(1)}, bf16[128,768]{1,0:T(8,128)(2,1)S(1)}, u32[]{:S(2)}, u32[]{:S(2)}) collective-permute-start(bf16[128,768]{1,0:T(8,128)(2,1)S(1)} %get-tuple-element.81), channel_id=1, source_target_pairs={{0,1},{1,0},{2,3},{3,2},{4,5},{5,4},{6,7},{7,6},{8,9},{9,8},{10,11... | collective-permute-start | bytes 589832 | tf_op jit(solution)/shard_map/ppermute | solution.py:50
  51.5 11.8 %collective-permute-start.17 = (bf16[192,768]{1,0:T(8,128)(2,1)S(1)}, bf16[192,768]{1,0:T(8,128)(2,1)S(1)}, u32[]{:S(2)}, u32[]{:S(2)}) collective-permute-start(bf16[192,768]{1,0:T(8,128)(2,1)S(1)} %pad_maximum_fusion.1.refs_5_), channel_id=1, source_target_pairs={{0,4},{4,8},{8,12},{12,0},{1,5},{5,9},{9,13},{13,1},{2,6},{6,10},{... | collective-permute-start | bytes 884744 | tf_op jit(solution)/shard_map/ppermute | solution.py:45
  51.6 17.9 %collective-permute-start.19 = (bf16[192,768]{1,0:T(8,128)(2,1)S(1)}, bf16[192,768]{1,0:T(8,128)(2,1)S(1)}, u32[]{:S(2)}, u32[]{:S(2)}) collective-permute-start(bf16[192,768]{1,0:T(8,128)(2,1)S(1)} %pad_maximum_fusion.1.refs_5_), channel_id=1, source_target_pairs={{0,12},{4,0},{8,4},{12,8},{1,13},{5,1},{9,5},{13,9},{2,14},{6,2},{... | collective-permute-start | bytes 884744 | tf_op jit(solution)/shard_map/ppermute | solution.py:45
  55.4 24.3 %collective-permute-start.21 = (bf16[192,768]{1,0:T(8,128)(2,1)S(1)}, bf16[192,768]{1,0:T(8,128)(2,1)S(1)}, u32[]{:S(2)}, u32[]{:S(2)}) collective-permute-start(bf16[192,768]{1,0:T(8,128)(2,1)S(1)} %pad_maximum_fusion.1.refs_5_), channel_id=1, source_target_pairs={{0,8},{4,12},{8,0},{12,4},{1,9},{5,13},{9,1},{13,5},{2,10},{6,14},... | collective-permute-start | bytes 884744 | tf_op jit(solution)/shard_map/ppermute | solution.py:45
  55.4 25.8 %collective-permute-start.14 = (bf16[128,768]{1,0:T(8,128)(2,1)S(1)}, bf16[128,768]{1,0:T(8,128)(2,1)S(1)}, u32[]{:S(2)}, u32[]{:S(2)}) collective-permute-start(bf16[128,768]{1,0:T(8,128)(2,1)S(1)} %add_convert_fusion.5), channel_id=1, source_target_pairs={{0,2},{1,3},{2,0},{3,1},{4,6},{5,7},{6,4},{7,5},{8,10},{9,11},{10,... | collective-permute-start | bytes 589832 | tf_op jit(solution)/shard_map/ppermute | solution.py:50
  56.0 25.4 %collective-permute-start.16 = (bf16[192,768]{1,0:T(8,128)(2,1)S(1)}, bf16[192,768]{1,0:T(8,128)(2,1)S(1)}, u32[]{:S(2)}, u32[]{:S(2)}) collective-permute-start(bf16[192,768]{1,0:T(8,128)(2,1)S(1)} %pad_maximum_fusion.1.refs_5_), channel_id=1, source_target_pairs={{0,16},{16,0},{1,17},{17,1},{2,18},{18,2},{3,19},{19,3},{4,20},{20... | collective-permute-start | bytes 884744 | tf_op jit(solution)/shard_map/ppermute | solution.py:45
  63.3 18.1 %collective-permute-start.18 = (bf16[192,768]{1,0:T(8,128)(2,1)S(1)}, bf16[192,768]{1,0:T(8,128)(2,1)S(1)}, u32[]{:S(2)}, u32[]{:S(2)}) collective-permute-start(bf16[192,768]{1,0:T(8,128)(2,1)S(1)} %collective-permute-done.17.refs_7_), channel_id=1, source_target_pairs={{0,16},{16,0},{1,17},{17,1},{2,18},{18,2},{3,19},{19,3},{4,20},{20... | collective-permute-start | bytes 884744 | tf_op jit(solution)/shard_map/ppermute | solution.py:45
  69.4 11.9 %collective-permute-start.20 = (bf16[192,768]{1,0:T(8,128)(2,1)S(1)}, bf16[192,768]{1,0:T(8,128)(2,1)S(1)}, u32[]{:S(2)}, u32[]{:S(2)}) collective-permute-start(bf16[192,768]{1,0:T(8,128)(2,1)S(1)} %collective-permute-done.19.refs_9_), channel_id=1, source_target_pairs={{0,16},{16,0},{1,17},{17,1},{2,18},{18,2},{3,19},{19,3},{4,20},{20... | collective-permute-start | bytes 884744 | tf_op jit(solution)/shard_map/ppermute | solution.py:45
  79.7 8.3 %collective-permute-start.22 = (bf16[192,768]{1,0:T(8,128)(2,1)S(1)}, bf16[192,768]{1,0:T(8,128)(2,1)S(1)}, u32[]{:S(2)}, u32[]{:S(2)}) collective-permute-start(bf16[192,768]{1,0:T(8,128)(2,1)S(1)} %collective-permute-done.21.refs_11_), channel_id=1, source_target_pairs={{0,16},{16,0},{1,17},{17,1},{2,18},{18,2},{3,19},{19,3},{4,20},{20... | collective-permute-start | bytes 884744 | tf_op jit(solution)/shard_map/ppermute | solution.py:45
  81.3 6.7 %collective-permute-start.15 = (bf16[128,768]{1,0:T(8,128)(2,1)S(1)}, bf16[128,768]{1,0:T(8,128)(2,1)S(1)}, u32[]{:S(2)}, u32[]{:S(2)}) collective-permute-start(bf16[128,768]{1,0:T(8,128)(2,1)S(1)} %add_convert_fusion.4.refs_1_), channel_id=1, source_target_pairs={{0,1},{1,0},{2,3},{3,2},{4,5},{5,4},{6,7},{7,6},{8,9},{9,8},{10,11... | collective-permute-start | bytes 589832 | tf_op jit(solution)/shard_map/ppermute | solution.py:50
  90.2 1.5 collective-permute-start.23
  91.7 7.0 %collective-permute-start.24 = (bf16[128,768]{1,0:T(8,128)(2,1)S(1)}, bf16[128,768]{1,0:T(8,128)(2,1)S(1)}, u32[]{:S(2)}, u32[]{:S(2)}) collective-permute-start(bf16[128,768]{1,0:T(8,128)(2,1)S(1)} %add_convert_fusion.3), channel_id=1, source_target_pairs={{0,2},{1,3},{2,0},{3,1},{4,6},{5,7},{6,4},{7,5},{8,10},{9,11},{10,... | collective-permute-start | bytes 589832 | tf_op jit(solution)/shard_map/ppermute | solution.py:50
  98.8 1.5 collective-permute-start.25
  103.0 1.4 collective-permute-start.26
  104.5 7.0 %collective-permute-start.27 = (bf16[128,768]{1,0:T(8,128)(2,1)S(1)}, bf16[128,768]{1,0:T(8,128)(2,1)S(1)}, u32[]{:S(2)}, u32[]{:S(2)}) collective-permute-start(bf16[128,768]{1,0:T(8,128)(2,1)S(1)} %add_convert_fusion.1), channel_id=1, source_target_pairs={{0,2},{1,3},{2,0},{3,1},{4,6},{5,7},{6,4},{7,5},{8,10},{9,11},{10,... | collective-permute-start | bytes 589832 | tf_op jit(solution)/shard_map/ppermute | solution.py:50
  111.6 1.5 collective-permute-start.28
  118.7 2.4 %collective-permute-start.29 = (bf16[4,128,768]{2,1,0:T(8,128)(2,1)S(1)}, bf16[4,128,768]{2,1,0:T(8,128)(2,1)S(1)}, u32[]{:S(2)}, u32[]{:S(2)}) collective-permute-start(bf16[4,128,768]{2,1,0:T(8,128)(2,1)S(1)} %get-tuple-element.101), channel_id=1, source_target_pairs={{0,1},{1,0},{2,3},{3,2},{4,5},{5,4},{6,7},{7,6},{8,9},{9,8},{10,11... | collective-permute-start | bytes 2359304 | tf_op jit(solution)/shard_map/ppermute | solution.py:50
  118.9 18.6 %collective-permute-start.41 = (bf16[256,1152]{1,0:T(8,128)(2,1)S(1)}, bf16[256,1152]{1,0:T(8,128)(2,1)S(1)}, u32[]{:S(2)}, u32[]{:S(2)}) collective-permute-start(bf16[256,1152]{1,0:T(8,128)(2,1)S(1)} %get-tuple-element.130), channel_id=1, source_target_pairs={{0,16},{16,0},{1,17},{17,1},{2,18},{18,2},{3,19},{19,3},{4,20},{20... | collective-permute-start | bytes 1769480 | tf_op jit(solution)/shard_map/ppermute | solution.py:45
  120.4 27.3 %collective-permute-start.42 = (bf16[256,1152]{1,0:T(8,128)(2,1)S(1)}, bf16[256,1152]{1,0:T(8,128)(2,1)S(1)}, u32[]{:S(2)}, u32[]{:S(2)}) collective-permute-start(bf16[256,1152]{1,0:T(8,128)(2,1)S(1)} %get-tuple-element.131), channel_id=1, source_target_pairs={{0,16},{16,0},{1,17},{17,1},{2,18},{18,2},{3,19},{19,3},{4,20},{20... | collective-permute-start | bytes 1769480 | tf_op jit(solution)/shard_map/ppermute | solution.py:45
  121.7 11.2 %collective-permute-start.30 = (bf16[4,64,768]{2,1,0:T(8,128)(2,1)S(1)}, bf16[4,64,768]{2,1,0:T(8,128)(2,1)S(1)}, u32[]{:S(2)}, u32[]{:S(2)}) collective-permute-start(bf16[4,64,768]{2,1,0:T(8,128)(2,1)S(1)} %get-tuple-element.103), channel_id=1, source_target_pairs={{0,2},{1,3},{2,0},{3,1},{4,6},{5,7},{6,4},{7,5},{8,10},{9,11},{10,... | collective-permute-start | bytes 1179656 | tf_op jit(solution)/shard_map/ppermute | solution.py:50
  124.4 35.7 %collective-permute-start.37 = (bf16[392,768]{1,0:T(8,128)(2,1)S(1)}, bf16[392,768]{1,0:T(8,128)(2,1)S(1)}, u32[]{:S(2)}, u32[]{:S(2)}) collective-permute-start(bf16[392,768]{1,0:T(8,128)(2,1)S(1)} %get-tuple-element.115), channel_id=1, source_target_pairs={{0,16},{16,0},{1,17},{17,1},{2,18},{18,2},{3,19},{19,3},{4,20},{20... | collective-permute-start | bytes 1806344 | tf_op jit(solution)/shard_map/ppermute | solution.py:45
  133.6 15.7 %collective-permute-start.31 = (bf16[64,768]{1,0:T(8,128)(2,1)S(1)}, bf16[64,768]{1,0:T(8,128)(2,1)S(1)}, u32[]{:S(2)}, u32[]{:S(2)}) collective-permute-start(bf16[64,768]{1,0:T(8,128)(2,1)S(1)} %get-tuple-element.105), channel_id=1, source_target_pairs={{0,4},{4,8},{8,12},{12,0},{1,5},{5,9},{9,13},{13,1},{2,6},{6,10},{... | collective-permute-start | bytes 294920 | tf_op jit(solution)/shard_map/ppermute | solution.py:45
  133.7 19.5 %collective-permute-start.32 = (bf16[64,768]{1,0:T(8,128)(2,1)S(1)}, bf16[64,768]{1,0:T(8,128)(2,1)S(1)}, u32[]{:S(2)}, u32[]{:S(2)}) collective-permute-start(bf16[64,768]{1,0:T(8,128)(2,1)S(1)} %get-tuple-element.106), channel_id=1, source_target_pairs={{0,12},{4,0},{8,4},{12,8},{1,13},{5,1},{9,5},{13,9},{2,14},{6,2},{... | collective-permute-start | bytes 294920 | tf_op jit(solution)/shard_map/ppermute | solution.py:45
  137.5 15.7 %collective-permute-start.33 = (bf16[64,768]{1,0:T(8,128)(2,1)S(1)}, bf16[64,768]{1,0:T(8,128)(2,1)S(1)}, u32[]{:S(2)}, u32[]{:S(2)}) collective-permute-start(bf16[64,768]{1,0:T(8,128)(2,1)S(1)} %get-tuple-element.107), channel_id=1, source_target_pairs={{0,8},{4,12},{8,0},{12,4},{1,9},{5,13},{9,1},{13,5},{2,10},{6,14},... | collective-permute-start | bytes 294920 | tf_op jit(solution)/shard_map/ppermute | solution.py:45
  149.2 11.8 %collective-permute-start.43 = (bf16[2,96,768]{2,1,0:T(8,128)(2,1)S(1)}, bf16[2,96,768]{2,1,0:T(8,128)(2,1)S(1)}, u32[]{:S(2)}, u32[]{:S(2)}) collective-permute-start(bf16[2,96,768]{2,1,0:T(8,128)(2,1)S(1)} %get-tuple-element.133), channel_id=1, source_target_pairs={{0,4},{4,8},{8,12},{12,0},{1,5},{5,9},{9,13},{13,1},{2,6},{6,10},{... | collective-permute-start | bytes 884744 | tf_op jit(solution)/shard_map/ppermute | solution.py:45
  149.3 18.3 %collective-permute-start.44 = (bf16[2,96,768]{2,1,0:T(8,128)(2,1)S(1)}, bf16[2,96,768]{2,1,0:T(8,128)(2,1)S(1)}, u32[]{:S(2)}, u32[]{:S(2)}) collective-permute-start(bf16[2,96,768]{2,1,0:T(8,128)(2,1)S(1)} %get-tuple-element.134), channel_id=1, source_target_pairs={{0,12},{4,0},{8,4},{12,8},{1,13},{5,1},{9,5},{13,9},{2,14},{6,2},{... | collective-permute-start | bytes 884744 | tf_op jit(solution)/shard_map/ppermute | solution.py:45
  153.1 31.7 %collective-permute-start.45 = (bf16[2,96,768]{2,1,0:T(8,128)(2,1)S(1)}, bf16[2,96,768]{2,1,0:T(8,128)(2,1)S(1)}, u32[]{:S(2)}, u32[]{:S(2)}) collective-permute-start(bf16[2,96,768]{2,1,0:T(8,128)(2,1)S(1)} %get-tuple-element.135), channel_id=1, source_target_pairs={{0,8},{4,12},{8,0},{12,4},{1,9},{5,13},{9,1},{13,5},{2,10},{6,14},... | collective-permute-start | bytes 884744 | tf_op jit(solution)/shard_map/ppermute | solution.py:45
  153.2 31.6 %collective-permute-start.34 = (bf16[64,768]{1,0:T(8,128)(2,1)S(1)}, bf16[64,768]{1,0:T(8,128)(2,1)S(1)}, u32[]{:S(2)}, u32[]{:S(2)}) collective-permute-start(bf16[64,768]{1,0:T(8,128)(2,1)S(1)} %add_convert_fusion.6.refs_0_), channel_id=1, source_target_pairs={{0,2},{1,3},{2,0},{3,1},{4,6},{5,7},{6,4},{7,5},{8,10},{9,11},{10,... | collective-permute-start | bytes 294920 | tf_op jit(solution)/shard_map/ppermute | solution.py:50
  161.0 25.2 %collective-permute-start.38 = (bf16[104,768]{1,0:T(8,128)(2,1)S(1)}, bf16[104,768]{1,0:T(8,128)(2,1)S(1)}, u32[]{:S(2)}, u32[]{:S(2)}) collective-permute-start(bf16[104,768]{1,0:T(8,128)(2,1)S(1)} %get-tuple-element.117), channel_id=1, source_target_pairs={{0,4},{4,8},{8,12},{12,0},{1,5},{5,9},{9,13},{13,1},{2,6},{6,10},{... | collective-permute-start | bytes 479240 | tf_op jit(solution)/shard_map/ppermute | solution.py:45
  161.0 25.2 %collective-permute-start.39 = (bf16[104,768]{1,0:T(8,128)(2,1)S(1)}, bf16[104,768]{1,0:T(8,128)(2,1)S(1)}, u32[]{:S(2)}, u32[]{:S(2)}) collective-permute-start(bf16[104,768]{1,0:T(8,128)(2,1)S(1)} %get-tuple-element.118), channel_id=1, source_target_pairs={{0,12},{4,0},{8,4},{12,8},{1,13},{5,1},{9,5},{13,9},{2,14},{6,2},{... | collective-permute-start | bytes 479240 | tf_op jit(solution)/shard_map/ppermute | solution.py:45
  167.6 22.2 %collective-permute-start.40 = (bf16[104,768]{1,0:T(8,128)(2,1)S(1)}, bf16[104,768]{1,0:T(8,128)(2,1)S(1)}, u32[]{:S(2)}, u32[]{:S(2)}) collective-permute-start(bf16[104,768]{1,0:T(8,128)(2,1)S(1)} %get-tuple-element.119), channel_id=1, source_target_pairs={{0,8},{4,12},{8,0},{12,4},{1,9},{5,13},{9,1},{13,5},{2,10},{6,14},... | collective-permute-start | bytes 479240 | tf_op jit(solution)/shard_map/ppermute | solution.py:45
  184.8 7.3 %collective-permute-start.35 = (bf16[64,768]{1,0:T(8,128)(2,1)S(1)}, bf16[64,768]{1,0:T(8,128)(2,1)S(1)}, u32[]{:S(2)}, u32[]{:S(2)}) collective-permute-start(bf16[64,768]{1,0:T(8,128)(2,1)S(1)} %add_convert_fusion.6.refs_0_), channel_id=1, source_target_pairs={{0,1},{1,0},{2,3},{3,2},{4,5},{5,4},{6,7},{7,6},{8,9},{9,8},{10,11... | collective-permute-start | bytes 294920 | tf_op jit(solution)/shard_map/ppermute | solution.py:50
  184.8 7.3 %collective-permute-start.36 = (bf16[64,768]{1,0:T(8,128)(2,1)S(1)}, bf16[64,768]{1,0:T(8,128)(2,1)S(1)}, u32[]{:S(2)}, u32[]{:S(2)}) collective-permute-start(bf16[64,768]{1,0:T(8,128)(2,1)S(1)} %collective-permute-done.34.refs_1_), channel_id=1, source_target_pairs={{0,1},{1,0},{2,3},{3,2},{4,5},{5,4},{6,7},{7,6},{8,9},{9,8},{10,11... | collective-permute-start | bytes 294920 | tf_op jit(solution)/shard_map/ppermute | solution.py:50
  (5 other events, 121.3 us)

commit v2 on v1

--- a/solution.py
+++ b/solution.py
@@ -100,6 +100,7 @@
         self.total = self.local * self.ctx
         self.half = self.rows // 2
         self.scale = 1.0 / math.sqrt(self.head)
+        self.folded = self.ctx == 4
         self.direct = self.fsdp == 2 and self.shard % 16 == 0
 
 
@@ -268,8 +269,7 @@
     total = dot(half_columns(z, meta[0], d_two_b), active[...], 0, 0)
     total = total + dot(grads[:, :part], acts[:, part:], 0, 0)
     work[1] = total.astype(BF)
-    for step, out in zip([0] + order, outs):
-        start = lax.rem(meta[1] + step, z.ctx) * z.shard
+    for start, out in zip(block_starts(z, order, meta[1]), outs):
         for at in range(2):
             out[at] = work[at, aligned(start, z.shard), :]
 
@@ -472,8 +472,9 @@
     place = meta[0] * z.ctx + meta[1]
     at = place * z.shard
     chosen = where_equal((z.width, z.shard), lambda r: r, lambda c: c + at)
+    found = exact_dot(small, chosen, 1, 0)
     for line, vector in enumerate(g_vectors):
-        vector[...] = exact_dot(small[line : line + 1], chosen, 1, 0)
+        vector[...] = found[line : line + 1]
     at = place * z.piece
     chosen = where_equal(
         (z.width, z.piece), lambda r: jnp.bitwise_and(r, z.head - 1), lambda c: c + at
@@ -481,9 +482,10 @@
     heads = g_up_bias.shape[1]
     wide = jnp.where(same_head(z, heads, z.width), small[6:7], 0.0)
     g_up_bias[...] = exact_dot(chosen, wide, 0, 1)
+    wide = [jnp.where(qv_lanes(z, head), small[7:8], 0.0) for head in range(z.heads)]
+    found = exact_dot(jnp.concatenate(wide, axis=0), chosen, 1, 0)
     for head in range(z.heads):
-        wide = jnp.where(qv_lanes(z, head), small[7:8], 0.0)
-        g_qv[head] = exact_dot(wide, chosen, 1, 0)
+        g_qv[head] = found[2 * head : 2 * head + 2]
 
 
 def finish_second_kernel(z, *refs):
@@ -498,10 +500,9 @@
 
 def share_kernel(z, order, *refs):
     meta, kept, got = refs[:3]
-    own, sends, work = refs[3], refs[4:-1], refs[-1]
+    outs, work = refs[3:-1], refs[-1]
     work[...] = (kept[...].astype(F32) + got[...].astype(F32)).astype(BF)
-    for step, out in zip([0] + order, (own,) + tuple(sends)):
-        start = lax.rem(meta[1] + step, z.ctx) * z.shard
+    for start, out in zip(block_starts(z, order, meta[1]), outs):
         out[: z.shard, :] = work[aligned(start, z.shard), :]
         out[z.shard :, :] = work[z.ctx * z.shard :, :]
 
@@ -530,17 +531,30 @@
     shape = kept.shape[:-2] + (kept.shape[-2] - (z.ctx - 1) * z.shard, kept.shape[-1])
     pieces = call(
         functools.partial(share_kernel, z, order),
-        [(shape, BF)] * z.ctx,
+        [(shape, BF)] * (z.ctx + z.folded),
         (kept, got),
         smem=(meta,),
         scratch=[pltpu.VMEM(kept.shape, BF)],
     )
-    return send_pieces(order, pieces)
-
-
-def send_pieces(order, pieces):
-    got = [ring(piece, "ctx", step) for step, piece in zip(order, pieces[1:])]
-    return [pieces[0]] + got
+    return send_pieces(z, order, pieces)
+
+
+def send_pieces(z, order, pieces):
+    if not z.folded:
+        return [pieces[0]] + [ring(piece, "ctx", step) for step, piece in zip(order, pieces[1:])]
+    own, right, left, far, fold = pieces
+    fold = lax.ppermute(fold, "ctx", ((0, 1), (3, 2)))
+    right = lax.ppermute(right, "ctx", ((0, 1), (1, 2), (2, 3)))
+    left = lax.ppermute(left, "ctx", ((1, 0), (2, 1), (3, 2)))
+    far = (far.astype(F32) + fold.astype(F32)).astype(BF)
+    return [own, right, left, ring(far, "ctx", 2)]
+
+
+def block_starts(z, order, col):
+    starts = [lax.rem(col + step, z.ctx) for step in [0] + order]
+    if z.folded:
+        starts.append(jnp.where(col == 0, z.ctx - 1, 0))
+    return [start * z.shard for start in starts]
 
 
 def body(
@@ -676,13 +690,13 @@
         grads = ring(grads, "fsdp", 1)
         second = call(
             functools.partial(second_grad_kernel, z, order),
-            [((2, z.shard, z.hidden), BF)] * z.ctx,
+            [((2, z.shard, z.hidden), BF)] * (z.ctx + z.folded),
             (*grad_args, acts, grads),
             smem=(meta,),
             scratch=[pltpu.VMEM((2, z.width // 2, z.hidden), BF)],
             flops=grad_flops,
         )
-        second = send_pieces(order, second)
+        second = send_pieces(z, order, second)
     else:
         (second_grads,) = call(
             second_grad_whole_kernel,

time: 194 us -> 197 us (1.015)
  starting transfers between devices: 51.5 us -> 54.6 us
    ppermute x0 -> x6, waiting for transfers between devices: none -> 11.7 us  [the longest x2 9.67 us: send_pieces(): fold = lax.ppermute(fold, 'ctx', ((0, 1), (3, 2)))]
    ppermute x0 -> x6, starting transfers between devices: none -> 8.74 us  [the longest x2 3.54 us: send_pieces(): fold = lax.ppermute(fold, 'ctx', ((0, 1), (3, 2)))]
    ppermute x17, waiting for transfers between devices: 25.5 us -> 18.5 us  [flip(): return lax.ppermute(value, axis, [(i, i ^ bit) for i in range(size)])]
    ppermute x29 -> x25, starting transfers between devices: 45.2 us -> 39.6 us  [ring(): lax.ppermute(value, axis, [(i, (i + step) % size) for i in range(size)])]
    ppermute x29 -> x25, waiting for transfers between devices: 84.6 us -> 80.8 us  [ring(): lax.ppermute(value, axis, [(i, (i + step) % size) for i in range(size)])]
  transfers between devices with their start and end apart: 46 -> 48, of which waited for: 24 -> 27; matrix products, arithmetic and copies ran while one was open for 0% -> 0% of each run, Pallas kernels for 5% -> 4%
where the time goes in v2:
time: 197 us
  waiting for transfers between devices  111 us (56%)
  starting transfers between devices  54.6 us (28%)
  Pallas kernels  28.4 us (14%)
    ppermute x25, waiting for transfers between devices, ring(): lax.ppermute(value, axis, [(i, (i + step) % size) for i in range(size)])  80.8 us
    ppermute x25, starting transfers between devices, ring(): lax.ppermute(value, axis, [(i, (i + step) % size) for i in range(size)])  39.6 us
    pallas_call x13, Pallas kernels, pallas(): pl.pallas_call(kernel, out_shape=tuple((jax.ShapeDtypeStruct(s, t) for s,...  28.4 us
    ppermute x17, waiting for transfers between devices, flip(): return lax.ppermute(value, axis, [(i, i ^ bit) for i in range(size)])  18.5 us
    ppermute x2, waiting for transfers between devices, send_pieces(): fold = lax.ppermute(fold, 'ctx', ((0, 1), (3, 2)))  9.67 us
    ppermute x17, starting transfers between devices, flip(): return lax.ppermute(value, axis, [(i, i ^ bit) for i in range(size)])  6.25 us
  transfers between devices with their start and end apart: 48, of which 27 were waited for; matrix products, arithmetic and copies ran while one was open for 0% of the time, Pallas kernels for 4%

profile of v2, /device:TPU:0, one launch (start us, length us, event | category | flops | bytes accessed | tf_op | source)
XLA Modules:
  0.0 197.1 jit_solution(1883751715969418206)
XLA Ops:
  1.3 2.4 %shard_map.254 = (bf16[104,768]{1,0:T(8,128)(2,1)}, bf16[64,768]{1,0:T(8,128)(2,1)}) custom-call(s32[3]{0:T(128)} %pad_add_fusion.refs_0_.meta, bf16[3,96,192]{2,1,0:T(8,128)(2,1)} %refs_1_.2, bf16[192,96]{1,0:T(8,128)(2,1)} %refs_2_.1, bf16[8,12]{1,0:T(8,128)(2,1)} %bitcast.38, bf16[3,2,8]{2,1,0:T(2,128)(2,1)} %bitcast.39, bf16[256,768]{1,0:T(8,128)(2,1)} %bitcast.28, ...), custom_call_target="tpu_custom_call" | custom-call | bytes 800160 | tf_op jit(solution)/shard_map/pallas_call | solution.py:68
  3.6 3.1 %collective-permute-start.7 = (bf16[64,768]{1,0:T(8,128)(2,1)}, bf16[64,768]{1,0:T(8,128)(2,1)S(1)}, u32[]{:S(2)}, u32[]{:S(2)}) collective-permute-start(bf16[64,768]{1,0:T(8,128)(2,1)} %get-tuple-element.81), channel_id=1, source_target_pairs={{0,4},{4,8},{8,12},{12,0},{1,5},{5,9},{9,13},{13,1},{2,6},{6,10},{... | collective-permute-start | bytes 294920 | tf_op jit(solution)/shard_map/ppermute | solution.py:45
  6.7 2.1 %collective-permute-start.8 = (bf16[64,768]{1,0:T(8,128)(2,1)}, bf16[64,768]{1,0:T(8,128)(2,1)S(1)}, u32[]{:S(2)}, u32[]{:S(2)}) collective-permute-start(bf16[64,768]{1,0:T(8,128)(2,1)} %get-tuple-element.81), channel_id=1, source_target_pairs={{0,12},{4,0},{8,4},{12,8},{1,13},{5,1},{9,5},{13,9},{2,14},{6,2},{... | collective-permute-start | bytes 294920 | tf_op jit(solution)/shard_map/ppermute | solution.py:45
  9.7 2.6 %collective-permute-done.7 = bf16[64,768]{1,0:T(8,128)(2,1)S(1)} collective-permute-done((bf16[64,768]{1,0:T(8,128)(2,1)}, bf16[64,768]{1,0:T(8,128)(2,1)S(1)}, u32[]{:S(2)}, u32[]{:S(2)}) %collective-permute-start.7) | collective-permute-done | bytes 98336 | tf_op jit(solution)/shard_map/ppermute | solution.py:45
  13.3 4.8 %collective-permute-done.9 = bf16[64,768]{1,0:T(8,128)(2,1)S(1)} collective-permute-done((bf16[64,768]{1,0:T(8,128)(2,1)}, bf16[64,768]{1,0:T(8,128)(2,1)S(1)}, u32[]{:S(2)}, u32[]{:S(2)}) %collective-permute-start.9) | collective-permute-done | bytes 98336 | tf_op jit(solution)/shard_map/ppermute | solution.py:45
  18.1 1.6 collective-permute-start.10
  19.6 3.8 %collective-permute-start.3 = (bf16[104,768]{1,0:T(8,128)(2,1)}, bf16[104,768]{1,0:T(8,128)(2,1)S(1)}, u32[]{:S(2)}, u32[]{:S(2)}) collective-permute-start(bf16[104,768]{1,0:T(8,128)(2,1)} %get-tuple-element.80.refs_2_), channel_id=1, source_target_pairs={{0,12},{4,0},{8,4},{12,8},{1,13},{5,1},{9,5},{13,9},{2,14},{6,2},{... | collective-permute-start | bytes 479240 | tf_op jit(solution)/shard_map/ppermute | solution.py:45
  23.5 1.5 collective-permute-start
  25.0 3.6 %collective-permute-done.1.refs_4_ = bf16[104,768]{1,0:T(8,128)(2,1)S(1)} collective-permute-done((bf16[104,768]{1,0:T(8,128)(2,1)}, bf16[104,768]{1,0:T(8,128)(2,1)S(1)}, u32[]{:S(2)}, u32[]{:S(2)}) %collective-permute-start.1) | collective-permute-done | bytes 159776 | tf_op jit(solution)/shard_map/ppermute | solution.py:45
  29.5 1.5 collective-permute-start.2
  31.0 5.2 %collective-permute-done.5.refs_8_ = bf16[104,768]{1,0:T(8,128)(2,1)S(1)} collective-permute-done((bf16[104,768]{1,0:T(8,128)(2,1)}, bf16[104,768]{1,0:T(8,128)(2,1)S(1)}, u32[]{:S(2)}, u32[]{:S(2)}) %collective-permute-start.5) | collective-permute-done | bytes 159776 | tf_op jit(solution)/shard_map/ppermute | solution.py:45
  36.2 1.5 collective-permute-start.4
  38.3 4.7 %collective-permute-done.4.refs_7_ = bf16[104,768]{1,0:T(8,128)(2,1)S(1)} collective-permute-done((bf16[104,768]{1,0:T(8,128)(2,1)S(1)}, bf16[104,768]{1,0:T(8,128)(2,1)S(1)}, u32[]{:S(2)}, u32[]{:S(2)}) %collective-permute-start.4) | collective-permute-done | bytes 159776 | tf_op jit(solution)/shard_map/ppermute | solution.py:45
  42.9 1.7 collective-permute-done.6.refs_9_
  45.6 5.8 %shard_map.255 = (bf16[768,768]{1,0:T(8,128)(2,1)S(1)}, f32[8,768]{1,0:T(8,128)S(1)}, bf16[4,256,768]{2,1,0:T(8,128)(2,1)S(1)}, bf16[2,512,384]{2,1,0:T(8,128)(2...) custom-call(s32[3]{0:T(128)S(1)} %copy-done.2, ...), custom_call_target="tpu_custom_call" | custom-call | flops 1207959552 | bytes 8183808 | tf_op jit(solution)/shard_map/pallas_call | solution.py:68
  51.6 3.8 %collective-permute-start.19 = (bf16[192,768]{1,0:T(8,128)(2,1)S(1)}, bf16[192,768]{1,0:T(8,128)(2,1)S(1)}, u32[]{:S(2)}, u32[]{:S(2)}) collective-permute-start(bf16[192,768]{1,0:T(8,128)(2,1)S(1)} %pad_maximum_fusion.1.refs_5_), channel_id=1, source_target_pairs={{0,12},{4,0},{8,4},{12,8},{1,13},{5,1},{9,5},{13,9},{2,14},{6,2},{... | collective-permute-start | bytes 884744 | tf_op jit(solution)/shard_map/ppermute | solution.py:45
  56.0 1.5 collective-permute-start.16
  57.5 5.7 %collective-permute-done.17.refs_7_ = bf16[192,768]{1,0:T(8,128)(2,1)S(1)} collective-permute-done((bf16[192,768]{1,0:T(8,128)(2,1)S(1)}, bf16[192,768]{1,0:T(8,128)(2,1)S(1)}, u32[]{:S(2)}, u32[]{:S(2)}) %collective-permute-start.17) | collective-permute-done | bytes 294944 | tf_op jit(solution)/shard_map/ppermute | solution.py:45
  63.3 1.5 collective-permute-start.18
  64.8 4.7 %collective-permute-done.19.refs_9_ = bf16[192,768]{1,0:T(8,128)(2,1)S(1)} collective-permute-done((bf16[192,768]{1,0:T(8,128)(2,1)S(1)}, bf16[192,768]{1,0:T(8,128)(2,1)S(1)}, u32[]{:S(2)}, u32[]{:S(2)}) %collective-permute-start.19) | collective-permute-done | bytes 294944 | tf_op jit(solution)/shard_map/ppermute | solution.py:45
  69.4 1.5 collective-permute-start.20
  70.9 8.8 %collective-permute-done.21.refs_11_ = bf16[192,768]{1,0:T(8,128)(2,1)S(1)} collective-permute-done((bf16[192,768]{1,0:T(8,128)(2,1)S(1)}, bf16[192,768]{1,0:T(8,128)(2,1)S(1)}, u32[]{:S(2)}, u32[]{:S(2)}) %collective-permute-start.21) | collective-permute-done | bytes 294944 | tf_op jit(solution)/shard_map/ppermute | solution.py:45
  79.7 1.5 collective-permute-start.22
  81.4 6.6 %collective-permute-done.22.refs_12_ = bf16[192,768]{1,0:T(8,128)(2,1)S(1)} collective-permute-done((bf16[192,768]{1,0:T(8,128)(2,1)S(1)}, bf16[192,768]{1,0:T(8,128)(2,1)S(1)}, u32[]{:S(2)}, u32[]{:S(2)}) %collective-permute-start.22) | collective-permute-done | bytes 294944 | tf_op jit(solution)/shard_map/ppermute | solution.py:45
  88.0 2.2 %shard_map.256 = (bf16[768,768]{1,0:T(8,128)(2,1)S(1)}, bf16[768,768]{1,0:T(8,128)(2,1)S(1)}, f32[256,768]{1,0:T(8,128)S(1)}, f32[256,1]{1,0:T(8,128)S(1)}, bf16...) custom-call(s32[3]{0:T(128)S(1)} %copy-done.2, ...), custom_call_target="tpu_custom_call" | custom-call | flops 603979776 | bytes 9069568 | tf_op jit(solution)/shard_map/pallas_call | solution.py:68
  90.3 1.4 collective-permute-done.23
  92.3 6.4 %collective-permute-done.24 = bf16[128,768]{1,0:T(8,128)(2,1)S(1)} collective-permute-done((bf16[128,768]{1,0:T(8,128)(2,1)S(1)}, bf16[128,768]{1,0:T(8,128)(2,1)S(1)}, u32[]{:S(2)}, u32[]{:S(2)}) %collective-permute-start.24) | collective-permute-done | bytes 196640 | tf_op jit(solution)/shard_map/ppermute | solution.py:50
  98.9 1.4 collective-permute-done.25.refs_2_
  100.3 2.7 %shard_map.257 = (bf16[256,768]{1,0:T(8,128)(2,1)}, f32[256,768]{1,0:T(8,128)S(1)}, bf16[256,768]{1,0:T(8,128)(2,1)S(1)}, bf16[256,768]{1,0:T(8,128)(2,1)S(1)}, ...) custom-call(s32[3]{0:T(128)S(1)} %copy-done.2, ...), custom_call_target="tpu_custom_call" | custom-call | flops 603979776 | bytes 7913472 | tf_op jit(solution)/shard_map/pallas_call | solution.py:68
  105.2 6.4 %collective-permute-done.27 = bf16[128,768]{1,0:T(8,128)(2,1)S(1)} collective-permute-done((bf16[128,768]{1,0:T(8,128)(2,1)S(1)}, bf16[128,768]{1,0:T(8,128)(2,1)S(1)}, u32[]{:S(2)}, u32[]{:S(2)}) %collective-permute-start.27) | collective-permute-done | bytes 196640 | tf_op jit(solution)/shard_map/ppermute | solution.py:50
  113.1 5.6 %shard_map.258 = (f32[256,768]{1,0:T(8,128)S(1)}, bf16[256,768]{1,0:T(8,128)(2,1)S(1)}, bf16[256,384]{1,0:T(8,128)(2,1)S(1)}, bf16[4,256,384]{2,1,0:T(8,128)(2,1...) custom-call(s32[3]{0:T(128)S(1)} %copy-done.2, ...), custom_call_target="tpu_custom_call" | custom-call | flops 1509949440 | bytes 9708544 | tf_op jit(solution)/shard_map/pallas_call | solution.py:68
  118.9 1.5 collective-permute-start.42
  122.4 2.0 %shard_map.262 = (bf16[392,768]{1,0:T(8,128)(2,1)S(1)}, bf16[392,768]{1,0:T(8,128)(2,1)S(1)}) custom-call(s32[3]{0:T(128)S(1)} %copy-done.2, bf16[256,768]{1,0:T(8,128)(2,1)S(1)} %bitcast.31, bf16[4,256,768]{2,1,0:T(8,128)(2,1)S(1)} %get-tuple-element.111.refs_2_, bf16[256,384]{1,0:T(8,128)(2,1)S(1)} %get-tuple-element.112.refs_3_, ...), custom_call_target="tpu_custom_call" | custom-call | flops 905969664 | bytes 4767744 | tf_op jit(solution)/shard_map/pallas_call | solution.py:68
  124.4 1.6 collective-permute-start.37
  126.0 9.2 %collective-permute-done.42.refs_5_ = bf16[256,1152]{1,0:T(8,128)(2,1)S(1)} collective-permute-done((bf16[256,1152]{1,0:T(8,128)(2,1)S(1)}, bf16[256,1152]{1,0:T(8,128)(2,1)S(1)}, u32[]{:S(2)}, u32[]{:S(2)}) %collective-permute-start.42) | collective-permute-done | bytes 589856 | tf_op jit(solution)/shard_map/ppermute | solution.py:45
  135.1 12.6 %collective-permute-done.43.refs_6_ = bf16[256,1152]{1,0:T(8,128)(2,1)S(1)} collective-permute-done((bf16[256,1152]{1,0:T(8,128)(2,1)S(1)}, bf16[256,1152]{1,0:T(8,128)(2,1)S(1)}, u32[]{:S(2)}, u32[]{:S(2)}) %collective-permute-start.43) | collective-permute-done | bytes 589856 | tf_op jit(solution)/shard_map/ppermute | solution.py:45
  147.8 1.5 shard_map.265
  153.3 3.1 %collective-permute-start.32 = (bf16[64,768]{1,0:T(8,128)(2,1)S(1)}, bf16[64,768]{1,0:T(8,128)(2,1)S(1)}, u32[]{:S(2)}, u32[]{:S(2)}) collective-permute-start(bf16[64,768]{1,0:T(8,128)(2,1)S(1)} %get-tuple-element.108), channel_id=1, source_target_pairs={{0,12},{4,0},{8,4},{12,8},{1,13},{5,1},{9,5},{13,9},{2,14},{6,2},{... | collective-permute-start | bytes 294920 | tf_op jit(solution)/shard_map/ppermute | solution.py:45
  156.4 1.5 collective-permute-done.46
  158.0 2.6 %collective-permute-start.33 = (bf16[64,768]{1,0:T(8,128)(2,1)S(1)}, bf16[64,768]{1,0:T(8,128)(2,1)S(1)}, u32[]{:S(2)}, u32[]{:S(2)}) collective-permute-start(bf16[64,768]{1,0:T(8,128)(2,1)S(1)} %get-tuple-element.109), channel_id=1, source_target_pairs={{0,8},{4,12},{8,0},{12,4},{1,9},{5,13},{9,1},{13,5},{2,10},{6,14},... | collective-permute-start | bytes 294920 | tf_op jit(solution)/shard_map/ppermute | solution.py:45
  162.9 3.5 %collective-permute-done.31 = bf16[64,768]{1,0:T(8,128)(2,1)S(1)} collective-permute-done((bf16[64,768]{1,0:T(8,128)(2,1)S(1)}, bf16[64,768]{1,0:T(8,128)(2,1)S(1)}, u32[]{:S(2)}, u32[]{:S(2)}) %collective-permute-start.31) | collective-permute-done | bytes 98336 | tf_op jit(solution)/shard_map/ppermute | solution.py:45
  166.4 2.2 %collective-permute-done.32 = bf16[64,768]{1,0:T(8,128)(2,1)S(1)} collective-permute-done((bf16[64,768]{1,0:T(8,128)(2,1)S(1)}, bf16[64,768]{1,0:T(8,128)(2,1)S(1)}, u32[]{:S(2)}, u32[]{:S(2)}) %collective-permute-start.32) | collective-permute-done | bytes 98336 | tf_op jit(solution)/shard_map/ppermute | solution.py:45
  168.5 2.2 %collective-permute-start.40 = (bf16[104,768]{1,0:T(8,128)(2,1)S(1)}, bf16[104,768]{1,0:T(8,128)(2,1)S(1)}, u32[]{:S(2)}, u32[]{:S(2)}) collective-permute-start(bf16[104,768]{1,0:T(8,128)(2,1)S(1)} %get-tuple-element.122), channel_id=1, source_target_pairs={{0,4},{12,8},{1,5},{13,9},{2,6},{14,10},{3,7},{15,11},{16,20},{28,... | collective-permute-start | bytes 479240 | tf_op jit(solution)/shard_map/ppermute | solution.py:546
  172.2 8.2 %collective-permute-done.40 = bf16[104,768]{1,0:T(8,128)(2,1)S(1)} collective-permute-done((bf16[104,768]{1,0:T(8,128)(2,1)S(1)}, bf16[104,768]{1,0:T(8,128)(2,1)S(1)}, u32[]{:S(2)}, u32[]{:S(2)}) %collective-permute-start.40) | collective-permute-done | bytes 159776 | tf_op jit(solution)/shard_map/ppermute | solution.py:546
  182.2 4.6 %collective-permute-start.41 = (bf16[104,768]{1,0:T(8,128)(2,1)S(1)}, bf16[104,768]{1,0:T(8,128)(2,1)S(1)}, u32[]{:S(2)}, u32[]{:S(2)}) collective-permute-start(bf16[104,768]{1,0:T(8,128)(2,1)S(1)} %add_convert_fusion.7), channel_id=1, source_target_pairs={{0,8},{4,12},{8,0},{12,4},{1,9},{5,13},{9,1},{13,5},{2,10},{6,14},... | collective-permute-start | bytes 479240 | tf_op jit(solution)/shard_map/ppermute | solution.py:45
  188.2 2.0 %collective-permute-done.39.refs_2_ = bf16[104,768]{1,0:T(8,128)(2,1)S(1)} collective-permute-done((bf16[104,768]{1,0:T(8,128)(2,1)S(1)}, bf16[104,768]{1,0:T(8,128)(2,1)S(1)}, u32[]{:S(2)}, u32[]{:S(2)}) %collective-permute-start.39) | collective-permute-done | bytes 159776 | tf_op jit(solution)/shard_map/ppermute | solution.py:548
  190.3 3.7 %collective-permute-done.41.refs_3_ = bf16[104,768]{1,0:T(8,128)(2,1)S(1)} collective-permute-done((bf16[104,768]{1,0:T(8,128)(2,1)S(1)}, bf16[104,768]{1,0:T(8,128)(2,1)S(1)}, u32[]{:S(2)}, u32[]{:S(2)}) %collective-permute-start.41) | collective-permute-done | bytes 159776 | tf_op jit(solution)/shard_map/ppermute | solution.py:45
  194.0 1.7 shard_map.264
  (87 shorter events, 24.6 us)
Async XLA Ops:
  3.6 8.7 %collective-permute-start.7 = (bf16[64,768]{1,0:T(8,128)(2,1)}, bf16[64,768]{1,0:T(8,128)(2,1)S(1)}, u32[]{:S(2)}, u32[]{:S(2)}) collective-permute-start(bf16[64,768]{1,0:T(8,128)(2,1)} %get-tuple-element.81), channel_id=1, source_target_pairs={{0,4},{4,8},{8,12},{12,0},{1,5},{5,9},{9,13},{13,1},{2,6},{6,10},{... | collective-permute-start | bytes 294920 | tf_op jit(solution)/shard_map/ppermute | solution.py:45
  6.7 6.6 %collective-permute-start.8 = (bf16[64,768]{1,0:T(8,128)(2,1)}, bf16[64,768]{1,0:T(8,128)(2,1)S(1)}, u32[]{:S(2)}, u32[]{:S(2)}) collective-permute-start(bf16[64,768]{1,0:T(8,128)(2,1)} %get-tuple-element.81), channel_id=1, source_target_pairs={{0,12},{4,0},{8,4},{12,8},{1,13},{5,1},{9,5},{13,9},{2,14},{6,2},{... | collective-permute-start | bytes 294920 | tf_op jit(solution)/shard_map/ppermute | solution.py:45
  8.8 9.3 %collective-permute-start.9 = (bf16[64,768]{1,0:T(8,128)(2,1)}, bf16[64,768]{1,0:T(8,128)(2,1)S(1)}, u32[]{:S(2)}, u32[]{:S(2)}) collective-permute-start(bf16[64,768]{1,0:T(8,128)(2,1)} %get-tuple-element.81), channel_id=1, source_target_pairs={{0,8},{4,12},{8,0},{12,4},{1,9},{5,13},{9,1},{13,5},{2,10},{6,14},... | collective-permute-start | bytes 294920 | tf_op jit(solution)/shard_map/ppermute | solution.py:45
  18.1 10.6 %collective-permute-start.10 = (bf16[3,64,768]{2,1,0:T(8,128)(2,1)S(1)}, bf16[3,64,768]{2,1,0:T(8,128)(2,1)S(1)}, u32[]{:S(2)}, u32[]{:S(2)}) collective-permute-start(bf16[3,64,768]{2,1,0:T(8,128)(2,1)S(1)} %pad_maximum_fusion.refs_11_), channel_id=1, source_target_pairs={{0,2},{1,3},{2,0},{3,1},{4,6},{5,7},{6,4},{7,5},{8,10},{9,11},{10,... | collective-permute-start | bytes 884744 | tf_op jit(solution)/shard_map/ppermute | solution.py:50
  19.6 9.0 %collective-permute-start.1 = (bf16[104,768]{1,0:T(8,128)(2,1)}, bf16[104,768]{1,0:T(8,128)(2,1)S(1)}, u32[]{:S(2)}, u32[]{:S(2)}) collective-permute-start(bf16[104,768]{1,0:T(8,128)(2,1)} %get-tuple-element.80.refs_2_), channel_id=1, source_target_pairs={{0,4},{4,8},{8,12},{12,0},{1,5},{5,9},{9,13},{13,1},{2,6},{6,10},{... | collective-permute-start | bytes 479240 | tf_op jit(solution)/shard_map/ppermute | solution.py:45
  19.6 9.9 %collective-permute-start.3 = (bf16[104,768]{1,0:T(8,128)(2,1)}, bf16[104,768]{1,0:T(8,128)(2,1)S(1)}, u32[]{:S(2)}, u32[]{:S(2)}) collective-permute-start(bf16[104,768]{1,0:T(8,128)(2,1)} %get-tuple-element.80.refs_2_), channel_id=1, source_target_pairs={{0,12},{4,0},{8,4},{12,8},{1,13},{5,1},{9,5},{13,9},{2,14},{6,2},{... | collective-permute-start | bytes 479240 | tf_op jit(solution)/shard_map/ppermute | solution.py:45
  23.5 12.8 %collective-permute-start.5 = (bf16[104,768]{1,0:T(8,128)(2,1)}, bf16[104,768]{1,0:T(8,128)(2,1)S(1)}, u32[]{:S(2)}, u32[]{:S(2)}) collective-permute-start(bf16[104,768]{1,0:T(8,128)(2,1)} %get-tuple-element.80.refs_2_), channel_id=1, source_target_pairs={{0,8},{4,12},{8,0},{12,4},{1,9},{5,13},{9,1},{13,5},{2,10},{6,14},... | collective-permute-start | bytes 479240 | tf_op jit(solution)/shard_map/ppermute | solution.py:45
  23.5 14.3 %collective-permute-start = (bf16[104,768]{1,0:T(8,128)(2,1)}, bf16[104,768]{1,0:T(8,128)(2,1)S(1)}, u32[]{:S(2)}, u32[]{:S(2)}) collective-permute-start(bf16[104,768]{1,0:T(8,128)(2,1)} %get-tuple-element.80.refs_2_), channel_id=1, source_target_pairs={{0,16},{16,0},{1,17},{17,1},{2,18},{18,2},{3,19},{19,3},{4,20},{20... | collective-permute-start | bytes 479240 | tf_op jit(solution)/shard_map/ppermute | solution.py:45
  28.6 16.0 %collective-permute-start.11 = (bf16[3,64,768]{2,1,0:T(8,128)(2,1)S(1)}, bf16[3,64,768]{2,1,0:T(8,128)(2,1)S(1)}, u32[]{:S(2)}, u32[]{:S(2)}) collective-permute-start(bf16[3,64,768]{2,1,0:T(8,128)(2,1)S(1)} %pad_maximum_fusion.refs_11_), channel_id=1, source_target_pairs={{0,1},{1,0},{2,3},{3,2},{4,5},{5,4},{6,7},{7,6},{8,9},{9,8},{10,11... | collective-permute-start | bytes 884744 | tf_op jit(solution)/shard_map/ppermute | solution.py:50
  28.6 16.0 %collective-permute-start.12 = (bf16[3,64,768]{2,1,0:T(8,128)(2,1)S(1)}, bf16[3,64,768]{2,1,0:T(8,128)(2,1)S(1)}, u32[]{:S(2)}, u32[]{:S(2)}) collective-permute-start(bf16[3,64,768]{2,1,0:T(8,128)(2,1)S(1)} %collective-permute-done.10.refs_12_), channel_id=1, source_target_pairs={{0,1},{1,0},{2,3},{3,2},{4,5},{5,4},{6,7},{7,6},{8,9},{9,8},{10,11... | collective-permute-start | bytes 884744 | tf_op jit(solution)/shard_map/ppermute | solution.py:50
  29.5 8.7 %collective-permute-start.2 = (bf16[104,768]{1,0:T(8,128)(2,1)S(1)}, bf16[104,768]{1,0:T(8,128)(2,1)S(1)}, u32[]{:S(2)}, u32[]{:S(2)}) collective-permute-start(bf16[104,768]{1,0:T(8,128)(2,1)S(1)} %collective-permute-done.1.refs_4_), channel_id=1, source_target_pairs={{0,16},{16,0},{1,17},{17,1},{2,18},{18,2},{3,19},{19,3},{4,20},{20... | collective-permute-start | bytes 479240 | tf_op jit(solution)/shard_map/ppermute | solution.py:45
  36.2 6.7 %collective-permute-start.4 = (bf16[104,768]{1,0:T(8,128)(2,1)S(1)}, bf16[104,768]{1,0:T(8,128)(2,1)S(1)}, u32[]{:S(2)}, u32[]{:S(2)}) collective-permute-start(bf16[104,768]{1,0:T(8,128)(2,1)S(1)} %collective-permute-done.3.refs_6_), channel_id=1, source_target_pairs={{0,16},{16,0},{1,17},{17,1},{2,18},{18,2},{3,19},{19,3},{4,20},{20... | collective-permute-start | bytes 479240 | tf_op jit(solution)/shard_map/ppermute | solution.py:45
  37.7 6.9 %collective-permute-start.6 = (bf16[104,768]{1,0:T(8,128)(2,1)S(1)}, bf16[104,768]{1,0:T(8,128)(2,1)S(1)}, u32[]{:S(2)}, u32[]{:S(2)}) collective-permute-start(bf16[104,768]{1,0:T(8,128)(2,1)S(1)} %collective-permute-done.5.refs_8_), channel_id=1, source_target_pairs={{0,16},{16,0},{1,17},{17,1},{2,18},{18,2},{3,19},{19,3},{4,20},{20... | collective-permute-start | bytes 479240 | tf_op jit(solution)/shard_map/ppermute | solution.py:45
  51.4 4.0 %collective-permute-start.13 = (bf16[128,768]{1,0:T(8,128)(2,1)S(1)}, bf16[128,768]{1,0:T(8,128)(2,1)S(1)}, u32[]{:S(2)}, u32[]{:S(2)}) collective-permute-start(bf16[128,768]{1,0:T(8,128)(2,1)S(1)} %get-tuple-element.83), channel_id=1, source_target_pairs={{0,1},{1,0},{2,3},{3,2},{4,5},{5,4},{6,7},{7,6},{8,9},{9,8},{10,11... | collective-permute-start | bytes 589832 | tf_op jit(solution)/shard_map/ppermute | solution.py:50
  51.5 11.8 %collective-permute-start.17 = (bf16[192,768]{1,0:T(8,128)(2,1)S(1)}, bf16[192,768]{1,0:T(8,128)(2,1)S(1)}, u32[]{:S(2)}, u32[]{:S(2)}) collective-permute-start(bf16[192,768]{1,0:T(8,128)(2,1)S(1)} %pad_maximum_fusion.1.refs_5_), channel_id=1, source_target_pairs={{0,4},{4,8},{8,12},{12,0},{1,5},{5,9},{9,13},{13,1},{2,6},{6,10},{... | collective-permute-start | bytes 884744 | tf_op jit(solution)/shard_map/ppermute | solution.py:45
  51.6 17.9 %collective-permute-start.19 = (bf16[192,768]{1,0:T(8,128)(2,1)S(1)}, bf16[192,768]{1,0:T(8,128)(2,1)S(1)}, u32[]{:S(2)}, u32[]{:S(2)}) collective-permute-start(bf16[192,768]{1,0:T(8,128)(2,1)S(1)} %pad_maximum_fusion.1.refs_5_), channel_id=1, source_target_pairs={{0,12},{4,0},{8,4},{12,8},{1,13},{5,1},{9,5},{13,9},{2,14},{6,2},{... | collective-permute-start | bytes 884744 | tf_op jit(solution)/shard_map/ppermute | solution.py:45
  55.4 24.3 %collective-permute-start.21 = (bf16[192,768]{1,0:T(8,128)(2,1)S(1)}, bf16[192,768]{1,0:T(8,128)(2,1)S(1)}, u32[]{:S(2)}, u32[]{:S(2)}) collective-permute-start(bf16[192,768]{1,0:T(8,128)(2,1)S(1)} %pad_maximum_fusion.1.refs_5_), channel_id=1, source_target_pairs={{0,8},{4,12},{8,0},{12,4},{1,9},{5,13},{9,1},{13,5},{2,10},{6,14},... | collective-permute-start | bytes 884744 | tf_op jit(solution)/shard_map/ppermute | solution.py:45
  55.4 25.8 %collective-permute-start.14 = (bf16[128,768]{1,0:T(8,128)(2,1)S(1)}, bf16[128,768]{1,0:T(8,128)(2,1)S(1)}, u32[]{:S(2)}, u32[]{:S(2)}) collective-permute-start(bf16[128,768]{1,0:T(8,128)(2,1)S(1)} %add_convert_fusion.6), channel_id=1, source_target_pairs={{0,2},{1,3},{2,0},{3,1},{4,6},{5,7},{6,4},{7,5},{8,10},{9,11},{10,... | collective-permute-start | bytes 589832 | tf_op jit(solution)/shard_map/ppermute | solution.py:50
  56.0 25.4 %collective-permute-start.16 = (bf16[192,768]{1,0:T(8,128)(2,1)S(1)}, bf16[192,768]{1,0:T(8,128)(2,1)S(1)}, u32[]{:S(2)}, u32[]{:S(2)}) collective-permute-start(bf16[192,768]{1,0:T(8,128)(2,1)S(1)} %pad_maximum_fusion.1.refs_5_), channel_id=1, source_target_pairs={{0,16},{16,0},{1,17},{17,1},{2,18},{18,2},{3,19},{19,3},{4,20},{20... | collective-permute-start | bytes 884744 | tf_op jit(solution)/shard_map/ppermute | solution.py:45
  63.3 18.1 %collective-permute-start.18 = (bf16[192,768]{1,0:T(8,128)(2,1)S(1)}, bf16[192,768]{1,0:T(8,128)(2,1)S(1)}, u32[]{:S(2)}, u32[]{:S(2)}) collective-permute-start(bf16[192,768]{1,0:T(8,128)(2,1)S(1)} %collective-permute-done.17.refs_7_), channel_id=1, source_target_pairs={{0,16},{16,0},{1,17},{17,1},{2,18},{18,2},{3,19},{19,3},{4,20},{20... | collective-permute-start | bytes 884744 | tf_op jit(solution)/shard_map/ppermute | solution.py:45
  69.4 11.9 %collective-permute-start.20 = (bf16[192,768]{1,0:T(8,128)(2,1)S(1)}, bf16[192,768]{1,0:T(8,128)(2,1)S(1)}, u32[]{:S(2)}, u32[]{:S(2)}) collective-permute-start(bf16[192,768]{1,0:T(8,128)(2,1)S(1)} %collective-permute-done.19.refs_9_), channel_id=1, source_target_pairs={{0,16},{16,0},{1,17},{17,1},{2,18},{18,2},{3,19},{19,3},{4,20},{20... | collective-permute-start | bytes 884744 | tf_op jit(solution)/shard_map/ppermute | solution.py:45
  79.7 8.3 %collective-permute-start.22 = (bf16[192,768]{1,0:T(8,128)(2,1)S(1)}, bf16[192,768]{1,0:T(8,128)(2,1)S(1)}, u32[]{:S(2)}, u32[]{:S(2)}) collective-permute-start(bf16[192,768]{1,0:T(8,128)(2,1)S(1)} %collective-permute-done.21.refs_11_), channel_id=1, source_target_pairs={{0,16},{16,0},{1,17},{17,1},{2,18},{18,2},{3,19},{19,3},{4,20},{20... | collective-permute-start | bytes 884744 | tf_op jit(solution)/shard_map/ppermute | solution.py:45
  81.3 6.7 %collective-permute-start.15 = (bf16[128,768]{1,0:T(8,128)(2,1)S(1)}, bf16[128,768]{1,0:T(8,128)(2,1)S(1)}, u32[]{:S(2)}, u32[]{:S(2)}) collective-permute-start(bf16[128,768]{1,0:T(8,128)(2,1)S(1)} %add_convert_fusion.5.refs_1_), channel_id=1, source_target_pairs={{0,1},{1,0},{2,3},{3,2},{4,5},{5,4},{6,7},{7,6},{8,9},{9,8},{10,11... | collective-permute-start | bytes 589832 | tf_op jit(solution)/shard_map/ppermute | solution.py:50
  90.2 1.5 collective-permute-start.23
  91.7 7.0 %collective-permute-start.24 = (bf16[128,768]{1,0:T(8,128)(2,1)S(1)}, bf16[128,768]{1,0:T(8,128)(2,1)S(1)}, u32[]{:S(2)}, u32[]{:S(2)}) collective-permute-start(bf16[128,768]{1,0:T(8,128)(2,1)S(1)} %add_convert_fusion.4), channel_id=1, source_target_pairs={{0,2},{1,3},{2,0},{3,1},{4,6},{5,7},{6,4},{7,5},{8,10},{9,11},{10,... | collective-permute-start | bytes 589832 | tf_op jit(solution)/shard_map/ppermute | solution.py:50
  98.8 1.5 collective-permute-start.25
  103.1 1.4 collective-permute-start.26
  104.5 7.0 %collective-permute-start.27 = (bf16[128,768]{1,0:T(8,128)(2,1)S(1)}, bf16[128,768]{1,0:T(8,128)(2,1)S(1)}, u32[]{:S(2)}, u32[]{:S(2)}) collective-permute-start(bf16[128,768]{1,0:T(8,128)(2,1)S(1)} %add_convert_fusion.2), channel_id=1, source_target_pairs={{0,2},{1,3},{2,0},{3,1},{4,6},{5,7},{6,4},{7,5},{8,10},{9,11},{10,... | collective-permute-start | bytes 589832 | tf_op jit(solution)/shard_map/ppermute | solution.py:50
  111.6 1.5 collective-permute-start.28
  118.7 2.4 %collective-permute-start.29 = (bf16[4,128,768]{2,1,0:T(8,128)(2,1)S(1)}, bf16[4,128,768]{2,1,0:T(8,128)(2,1)S(1)}, u32[]{:S(2)}, u32[]{:S(2)}) collective-permute-start(bf16[4,128,768]{2,1,0:T(8,128)(2,1)S(1)} %get-tuple-element.103), channel_id=1, source_target_pairs={{0,1},{1,0},{2,3},{3,2},{4,5},{5,4},{6,7},{7,6},{8,9},{9,8},{10,11... | collective-permute-start | bytes 2359304 | tf_op jit(solution)/shard_map/ppermute | solution.py:50
  118.9 16.2 %collective-permute-start.42 = (bf16[256,1152]{1,0:T(8,128)(2,1)S(1)}, bf16[256,1152]{1,0:T(8,128)(2,1)S(1)}, u32[]{:S(2)}, u32[]{:S(2)}) collective-permute-start(bf16[256,1152]{1,0:T(8,128)(2,1)S(1)} %get-tuple-element.133), channel_id=1, source_target_pairs={{0,16},{16,0},{1,17},{17,1},{2,18},{18,2},{3,19},{19,3},{4,20},{20... | collective-permute-start | bytes 1769480 | tf_op jit(solution)/shard_map/ppermute | solution.py:45
  120.5 27.3 %collective-permute-start.43 = (bf16[256,1152]{1,0:T(8,128)(2,1)S(1)}, bf16[256,1152]{1,0:T(8,128)(2,1)S(1)}, u32[]{:S(2)}, u32[]{:S(2)}) collective-permute-start(bf16[256,1152]{1,0:T(8,128)(2,1)S(1)} %get-tuple-element.134), channel_id=1, source_target_pairs={{0,16},{16,0},{1,17},{17,1},{2,18},{18,2},{3,19},{19,3},{4,20},{20... | collective-permute-start | bytes 1769480 | tf_op jit(solution)/shard_map/ppermute | solution.py:45
  121.8 30.2 %collective-permute-start.30 = (bf16[4,64,768]{2,1,0:T(8,128)(2,1)S(1)}, bf16[4,64,768]{2,1,0:T(8,128)(2,1)S(1)}, u32[]{:S(2)}, u32[]{:S(2)}) collective-permute-start(bf16[4,64,768]{2,1,0:T(8,128)(2,1)S(1)} %get-tuple-element.105), channel_id=1, source_target_pairs={{0,2},{1,3},{2,0},{3,1},{4,6},{5,7},{6,4},{7,5},{8,10},{9,11},{10,... | collective-permute-start | bytes 1179656 | tf_op jit(solution)/shard_map/ppermute | solution.py:50
  124.4 36.3 %collective-permute-start.37 = (bf16[392,768]{1,0:T(8,128)(2,1)S(1)}, bf16[392,768]{1,0:T(8,128)(2,1)S(1)}, u32[]{:S(2)}, u32[]{:S(2)}) collective-permute-start(bf16[392,768]{1,0:T(8,128)(2,1)S(1)} %get-tuple-element.117), channel_id=1, source_target_pairs={{0,16},{16,0},{1,17},{17,1},{2,18},{18,2},{3,19},{19,3},{4,20},{20... | collective-permute-start | bytes 1806344 | tf_op jit(solution)/shard_map/ppermute | solution.py:45
  149.3 8.7 %collective-permute-start.46 = (bf16[2,96,768]{2,1,0:T(8,128)(2,1)S(1)}, bf16[2,96,768]{2,1,0:T(8,128)(2,1)S(1)}, u32[]{:S(2)}, u32[]{:S(2)}) collective-permute-start(bf16[2,96,768]{2,1,0:T(8,128)(2,1)S(1)} %get-tuple-element.139), channel_id=1, source_target_pairs={{0,4},{12,8},{1,5},{13,9},{2,6},{14,10},{3,7},{15,11},{16,20},{28,... | collective-permute-start | bytes 884744 | tf_op jit(solution)/shard_map/ppermute | solution.py:546
  150.6 30.3 %collective-permute-start.44 = (bf16[2,96,768]{2,1,0:T(8,128)(2,1)S(1)}, bf16[2,96,768]{2,1,0:T(8,128)(2,1)S(1)}, u32[]{:S(2)}, u32[]{:S(2)}) collective-permute-start(bf16[2,96,768]{2,1,0:T(8,128)(2,1)S(1)} %get-tuple-element.136), channel_id=1, source_target_pairs={{0,4},{4,8},{8,12},{1,5},{5,9},{9,13},{2,6},{6,10},{10,14},{3,7},{... | collective-permute-start | bytes 884744 | tf_op jit(solution)/shard_map/ppermute | solution.py:547
  152.6 13.8 %collective-permute-start.31 = (bf16[64,768]{1,0:T(8,128)(2,1)S(1)}, bf16[64,768]{1,0:T(8,128)(2,1)S(1)}, u32[]{:S(2)}, u32[]{:S(2)}) collective-permute-start(bf16[64,768]{1,0:T(8,128)(2,1)S(1)} %get-tuple-element.107), channel_id=1, source_target_pairs={{0,4},{4,8},{8,12},{12,0},{1,5},{5,9},{9,13},{13,1},{2,6},{6,10},{... | collective-permute-start | bytes 294920 | tf_op jit(solution)/shard_map/ppermute | solution.py:45
  153.3 15.2 %collective-permute-start.32 = (bf16[64,768]{1,0:T(8,128)(2,1)S(1)}, bf16[64,768]{1,0:T(8,128)(2,1)S(1)}, u32[]{:S(2)}, u32[]{:S(2)}) collective-permute-start(bf16[64,768]{1,0:T(8,128)(2,1)S(1)} %get-tuple-element.108), channel_id=1, source_target_pairs={{0,12},{4,0},{8,4},{12,8},{1,13},{5,1},{9,5},{13,9},{2,14},{6,2},{... | collective-permute-start | bytes 294920 | tf_op jit(solution)/shard_map/ppermute | solution.py:45
  158.0 12.8 %collective-permute-start.33 = (bf16[64,768]{1,0:T(8,128)(2,1)S(1)}, bf16[64,768]{1,0:T(8,128)(2,1)S(1)}, u32[]{:S(2)}, u32[]{:S(2)}) collective-permute-start(bf16[64,768]{1,0:T(8,128)(2,1)S(1)} %get-tuple-element.109), channel_id=1, source_target_pairs={{0,8},{4,12},{8,0},{12,4},{1,9},{5,13},{9,1},{13,5},{2,10},{6,14},... | collective-permute-start | bytes 294920 | tf_op jit(solution)/shard_map/ppermute | solution.py:45
  160.7 21.5 %collective-permute-start.45 = (bf16[2,96,768]{2,1,0:T(8,128)(2,1)S(1)}, bf16[2,96,768]{2,1,0:T(8,128)(2,1)S(1)}, u32[]{:S(2)}, u32[]{:S(2)}) collective-permute-start(bf16[2,96,768]{2,1,0:T(8,128)(2,1)S(1)} %get-tuple-element.137), channel_id=1, source_target_pairs={{4,0},{8,4},{12,8},{5,1},{9,5},{13,9},{6,2},{10,6},{14,10},{7,3},{... | collective-permute-start | bytes 884744 | tf_op jit(solution)/shard_map/ppermute | solution.py:548
  166.4 20.5 %collective-permute-start.47 = (bf16[2,96,768]{2,1,0:T(8,128)(2,1)S(1)}, bf16[2,96,768]{2,1,0:T(8,128)(2,1)S(1)}, u32[]{:S(2)}, u32[]{:S(2)}) collective-permute-start(bf16[2,96,768]{2,1,0:T(8,128)(2,1)S(1)} %add_convert_fusion), channel_id=1, source_target_pairs={{0,8},{4,12},{8,0},{12,4},{1,9},{5,13},{9,1},{13,5},{2,10},{6,14},... | collective-permute-start | bytes 884744 | tf_op jit(solution)/shard_map/ppermute | solution.py:45
  168.5 11.8 %collective-permute-start.40 = (bf16[104,768]{1,0:T(8,128)(2,1)S(1)}, bf16[104,768]{1,0:T(8,128)(2,1)S(1)}, u32[]{:S(2)}, u32[]{:S(2)}) collective-permute-start(bf16[104,768]{1,0:T(8,128)(2,1)S(1)} %get-tuple-element.122), channel_id=1, source_target_pairs={{0,4},{12,8},{1,5},{13,9},{2,6},{14,10},{3,7},{15,11},{16,20},{28,... | collective-permute-start | bytes 479240 | tf_op jit(solution)/shard_map/ppermute | solution.py:546
  170.8 17.4 %collective-permute-start.38 = (bf16[104,768]{1,0:T(8,128)(2,1)S(1)}, bf16[104,768]{1,0:T(8,128)(2,1)S(1)}, u32[]{:S(2)}, u32[]{:S(2)}) collective-permute-start(bf16[104,768]{1,0:T(8,128)(2,1)S(1)} %get-tuple-element.119), channel_id=1, source_target_pairs={{0,4},{4,8},{8,12},{1,5},{5,9},{9,13},{2,6},{6,10},{10,14},{3,7},{... | collective-permute-start | bytes 479240 | tf_op jit(solution)/shard_map/ppermute | solution.py:547
  180.3 6.5 %collective-permute-start.34 = (bf16[64,768]{1,0:T(8,128)(2,1)S(1)}, bf16[64,768]{1,0:T(8,128)(2,1)S(1)}, u32[]{:S(2)}, u32[]{:S(2)}) collective-permute-start(bf16[64,768]{1,0:T(8,128)(2,1)S(1)} %add_convert_fusion.8.refs_0_), channel_id=1, source_target_pairs={{0,2},{1,3},{2,0},{3,1},{4,6},{5,7},{6,4},{7,5},{8,10},{9,11},{10,... | collective-permute-start | bytes 294920 | tf_op jit(solution)/shard_map/ppermute | solution.py:50
  180.9 9.3 %collective-permute-start.39 = (bf16[104,768]{1,0:T(8,128)(2,1)S(1)}, bf16[104,768]{1,0:T(8,128)(2,1)S(1)}, u32[]{:S(2)}, u32[]{:S(2)}) collective-permute-start(bf16[104,768]{1,0:T(8,128)(2,1)S(1)} %get-tuple-element.120), channel_id=1, source_target_pairs={{4,0},{8,4},{12,8},{5,1},{9,5},{13,9},{6,2},{10,6},{14,10},{7,3},{... | collective-permute-start | bytes 479240 | tf_op jit(solution)/shard_map/ppermute | solution.py:548
  182.2 11.7 %collective-permute-start.41 = (bf16[104,768]{1,0:T(8,128)(2,1)S(1)}, bf16[104,768]{1,0:T(8,128)(2,1)S(1)}, u32[]{:S(2)}, u32[]{:S(2)}) collective-permute-start(bf16[104,768]{1,0:T(8,128)(2,1)S(1)} %add_convert_fusion.7), channel_id=1, source_target_pairs={{0,8},{4,12},{8,0},{12,4},{1,9},{5,13},{9,1},{13,5},{2,10},{6,14},... | collective-permute-start | bytes 479240 | tf_op jit(solution)/shard_map/ppermute | solution.py:45
  186.8 8.8 %collective-permute-start.35 = (bf16[64,768]{1,0:T(8,128)(2,1)S(1)}, bf16[64,768]{1,0:T(8,128)(2,1)S(1)}, u32[]{:S(2)}, u32[]{:S(2)}) collective-permute-start(bf16[64,768]{1,0:T(8,128)(2,1)S(1)} %add_convert_fusion.8.refs_0_), channel_id=1, source_target_pairs={{0,1},{1,0},{2,3},{3,2},{4,5},{5,4},{6,7},{7,6},{8,9},{9,8},{10,11... | collective-permute-start | bytes 294920 | tf_op jit(solution)/shard_map/ppermute | solution.py:50
  186.9 8.8 %collective-permute-start.36 = (bf16[64,768]{1,0:T(8,128)(2,1)S(1)}, bf16[64,768]{1,0:T(8,128)(2,1)S(1)}, u32[]{:S(2)}, u32[]{:S(2)}) collective-permute-start(bf16[64,768]{1,0:T(8,128)(2,1)S(1)} %collective-permute-done.34.refs_1_), channel_id=1, source_target_pairs={{0,1},{1,0},{2,3},{3,2},{4,5},{5,4},{6,7},{7,6},{8,9},{9,8},{10,11... | collective-permute-start | bytes 294920 | tf_op jit(solution)/shard_map/ppermute | solution.py:50
  (7 other events, 209.2 us)

commit v3 on v2

--- a/solution.py
+++ b/solution.py
@@ -399,8 +399,8 @@
 
 
 def pack_kernel(z, *refs):
-    meta, qkv, out, up_bias, qv_bias, rows = refs[:6]
-    vectors, (pack, share) = refs[6:-2], refs[-2:]
+    meta, qkv, out, up_bias, qv_bias = refs[:5]
+    vectors, pack = refs[5:-1], refs[-1]
     place = meta[0] * z.ctx + meta[1]
     inner = z.inner
 
@@ -426,8 +426,6 @@
         line = line + jnp.sum(wide, axis=0, keepdims=True)
     lines.append(line)
     pack[z.shard :, :] = jnp.concatenate(lines, axis=0).astype(BF)
-    size = z.rows // z.tp
-    share[...] = rows[aligned(meta[2] * size, size), :]
 
 
 def pack_plain(z, place, qkv_weight, out_weight, vectors, up_bias, qv_bias):
@@ -586,15 +584,14 @@
 
     vectors = (out_bias, norm1_gain, norm1_bias, down_bias, norm2_gain, norm2_bias)
     if z.direct:
-        first_pack, token_share = call(
+        (first_pack,) = call(
             functools.partial(pack_kernel, z),
-            [((z.shard + TAIL, z.width), BF), ((z.rows // z.tp, z.width), BF)],
+            [((z.shard + TAIL, z.width), BF)],
             (
                 qkv_weight,
                 out_weight,
                 up_bias.T,
                 qv_bias.transpose(1, 0, 2),
-                rows,
                 *(vector.reshape(1, z.shard) for vector in vectors),
             ),
             smem=(meta,),
@@ -604,8 +601,8 @@
         mixed_shard, tail = pack_plain(
             z, place, qkv_weight, out_weight, jnp.stack(vectors), up_bias, qv_bias
         )
-        share = z.rows // z.tp
-        token_share = lax.dynamic_slice_in_dim(rows, lane * share, share, 0)
+    share = z.rows // z.tp
+    token_share = lax.dynamic_slice_in_dim(rows, lane * share, share, 0)
     got = jnp.stack([ring(token_share, "ctx", step) for step in order])
     pieces, masks = [got], [0]
     bit = z.tp // 2

time: 197 us -> 199 us (1.010)
  transfers between devices with their start and end apart: 48 -> 48, of which waited for: 27 -> 27; matrix products, arithmetic and copies ran while one was open for 0% -> 0% of each run, Pallas kernels for 4% -> 5%
where the time goes in v3:
time: 199 us; the launch traced here: 198 us
  waiting for transfers between devices  111 us (56%)
  starting transfers between devices  54.5 us (27%)
  Pallas kernels  28.1 us (14%)
  local copies, waits for them, and re-layouts  2.54 us (1%)
    ppermute x25, waiting for transfers between devices, ring(): lax.ppermute(value, axis, [(i, (i + step) % size) for i in range(size)])  80.7 us
    ppermute x25, starting transfers between devices, ring(): lax.ppermute(value, axis, [(i, (i + step) % size) for i in range(size)])  39.5 us
    pallas_call x13, Pallas kernels, pallas(): pl.pallas_call(kernel, out_shape=tuple((jax.ShapeDtypeStruct(s, t) for s,...  28.1 us
    ppermute x17, waiting for transfers between devices, flip(): return lax.ppermute(value, axis, [(i, i ^ bit) for i in range(size)])  18.6 us
    ppermute x2, waiting for transfers between devices, send_pieces(): fold = lax.ppermute(fold, 'ctx', ((0, 1), (3, 2)))  9.71 us
    ppermute x17, starting transfers between devices, flip(): return lax.ppermute(value, axis, [(i, i ^ bit) for i in range(size)])  6.21 us
  transfers between devices with their start and end apart: 48, of which 27 were waited for; matrix products, arithmetic and copies ran while one was open for 0% of the time, Pallas kernels for 5%

profile of v3, /device:TPU:0, one launch (start us, length us, event | category | flops | bytes accessed | tf_op | source)
XLA Modules:
  0.0 198.2 jit_solution(5111756662422518501)
XLA Ops:
  1.6 3.1 %collective-permute-start.7 = (bf16[64,768]{1,0:T(8,128)(2,1)S(1)}, bf16[64,768]{1,0:T(8,128)(2,1)S(1)}, u32[]{:S(2)}, u32[]{:S(2)}) collective-permute-start(bf16[64,768]{1,0:T(8,128)(2,1)S(1)} %constant_dynamic-slice_fusion), channel_id=1, source_target_pairs={{0,4},{4,8},{8,12},{12,0},{1,5},{5,9},{9,13},{13,1},{2,6},{6,10},{... | collective-permute-start | bytes 294920 | tf_op jit(solution)/shard_map/ppermute | solution.py:45
  4.7 2.1 %collective-permute-start.8 = (bf16[64,768]{1,0:T(8,128)(2,1)S(1)}, bf16[64,768]{1,0:T(8,128)(2,1)S(1)}, u32[]{:S(2)}, u32[]{:S(2)}) collective-permute-start(bf16[64,768]{1,0:T(8,128)(2,1)S(1)} %constant_dynamic-slice_fusion), channel_id=1, source_target_pairs={{0,12},{4,0},{8,4},{12,8},{1,13},{5,1},{9,5},{13,9},{2,14},{6,2},{... | collective-permute-start | bytes 294920 | tf_op jit(solution)/shard_map/ppermute | solution.py:45
  7.7 2.4 %collective-permute-done.7 = bf16[64,768]{1,0:T(8,128)(2,1)S(1)} collective-permute-done((bf16[64,768]{1,0:T(8,128)(2,1)S(1)}, bf16[64,768]{1,0:T(8,128)(2,1)S(1)}, u32[]{:S(2)}, u32[]{:S(2)}) %collective-permute-start.7) | collective-permute-done | bytes 98336 | tf_op jit(solution)/shard_map/ppermute | solution.py:45
  11.0 4.8 %collective-permute-done.9 = bf16[64,768]{1,0:T(8,128)(2,1)S(1)} collective-permute-done((bf16[64,768]{1,0:T(8,128)(2,1)S(1)}, bf16[64,768]{1,0:T(8,128)(2,1)S(1)}, u32[]{:S(2)}, u32[]{:S(2)}) %collective-permute-start.9) | collective-permute-done | bytes 98336 | tf_op jit(solution)/shard_map/ppermute | solution.py:45
  15.8 1.6 collective-permute-start.10
  18.0 2.2 %shard_map.254.refs_2_ = bf16[104,768]{1,0:T(8,128)(2,1)} custom-call(s32[3]{0:T(128)} %pad_add_fusion.refs_0_.meta, bf16[3,96,192]{2,1,0:T(8,128)(2,1)} %refs_1_.2, bf16[192,96]{1,0:T(8,128)(2,1)} %refs_2_.1, bf16[8,12]{1,0:T(8,128)(2,1)} %bitcast.38, bf16[3,2,8]{2,1,0:T(2,128)(2,1)} %bitcast.39, bf16[1,96]{1,0:T(2,128)(2,1)} %bitcast.40, ...), custom_call_target="tpu_custom_call" | custom-call | bytes 308640 | tf_op jit(solution)/shard_map/pallas_call | solution.py:68
  20.2 3.8 %collective-permute-start.3 = (bf16[104,768]{1,0:T(8,128)(2,1)}, bf16[104,768]{1,0:T(8,128)(2,1)S(1)}, u32[]{:S(2)}, u32[]{:S(2)}) collective-permute-start(bf16[104,768]{1,0:T(8,128)(2,1)} %shard_map.254.refs_2_), channel_id=1, source_target_pairs={{0,12},{4,0},{8,4},{12,8},{1,13},{5,1},{9,5},{13,9},{2,14},{6,2},{... | collective-permute-start | bytes 479240 | tf_op jit(solution)/shard_map/ppermute | solution.py:45
  24.0 1.5 collective-permute-start
  25.6 3.6 %collective-permute-done.1.refs_4_ = bf16[104,768]{1,0:T(8,128)(2,1)S(1)} collective-permute-done((bf16[104,768]{1,0:T(8,128)(2,1)}, bf16[104,768]{1,0:T(8,128)(2,1)S(1)}, u32[]{:S(2)}, u32[]{:S(2)}) %collective-permute-start.1) | collective-permute-done | bytes 159776 | tf_op jit(solution)/shard_map/ppermute | solution.py:45
  30.1 1.5 collective-permute-start.2
  31.6 5.2 %collective-permute-done.5.refs_8_ = bf16[104,768]{1,0:T(8,128)(2,1)S(1)} collective-permute-done((bf16[104,768]{1,0:T(8,128)(2,1)}, bf16[104,768]{1,0:T(8,128)(2,1)S(1)}, u32[]{:S(2)}, u32[]{:S(2)}) %collective-permute-start.5) | collective-permute-done | bytes 159776 | tf_op jit(solution)/shard_map/ppermute | solution.py:45
  36.8 1.5 collective-permute-start.4
  38.8 4.7 %collective-permute-done.4.refs_7_ = bf16[104,768]{1,0:T(8,128)(2,1)S(1)} collective-permute-done((bf16[104,768]{1,0:T(8,128)(2,1)S(1)}, bf16[104,768]{1,0:T(8,128)(2,1)S(1)}, u32[]{:S(2)}, u32[]{:S(2)}) %collective-permute-start.4) | collective-permute-done | bytes 159776 | tf_op jit(solution)/shard_map/ppermute | solution.py:45
  43.5 1.7 collective-permute-done.6.refs_9_
  46.8 5.8 %shard_map.255 = (bf16[768,768]{1,0:T(8,128)(2,1)S(1)}, f32[8,768]{1,0:T(8,128)S(1)}, bf16[4,256,768]{2,1,0:T(8,128)(2,1)S(1)}, bf16[2,512,384]{2,1,0:T(8,128)(2...) custom-call(s32[3]{0:T(128)S(1)} %copy-done.3, ...), custom_call_target="tpu_custom_call" | custom-call | flops 1207959552 | bytes 8183808 | tf_op jit(solution)/shard_map/pallas_call | solution.py:68
  52.8 3.8 %collective-permute-start.19 = (bf16[192,768]{1,0:T(8,128)(2,1)S(1)}, bf16[192,768]{1,0:T(8,128)(2,1)S(1)}, u32[]{:S(2)}, u32[]{:S(2)}) collective-permute-start(bf16[192,768]{1,0:T(8,128)(2,1)S(1)} %pad_maximum_fusion.1.refs_5_), channel_id=1, source_target_pairs={{0,12},{4,0},{8,4},{12,8},{1,13},{5,1},{9,5},{13,9},{2,14},{6,2},{... | collective-permute-start | bytes 884744 | tf_op jit(solution)/shard_map/ppermute | solution.py:45
  57.2 1.5 collective-permute-start.16
  58.8 5.7 %collective-permute-done.17.refs_7_ = bf16[192,768]{1,0:T(8,128)(2,1)S(1)} collective-permute-done((bf16[192,768]{1,0:T(8,128)(2,1)S(1)}, bf16[192,768]{1,0:T(8,128)(2,1)S(1)}, u32[]{:S(2)}, u32[]{:S(2)}) %collective-permute-start.17) | collective-permute-done | bytes 294944 | tf_op jit(solution)/shard_map/ppermute | solution.py:45
  64.5 1.5 collective-permute-start.18
  66.0 4.7 %collective-permute-done.19.refs_9_ = bf16[192,768]{1,0:T(8,128)(2,1)S(1)} collective-permute-done((bf16[192,768]{1,0:T(8,128)(2,1)S(1)}, bf16[192,768]{1,0:T(8,128)(2,1)S(1)}, u32[]{:S(2)}, u32[]{:S(2)}) %collective-permute-start.19) | collective-permute-done | bytes 294944 | tf_op jit(solution)/shard_map/ppermute | solution.py:45
  70.7 1.4 collective-permute-start.20
  72.1 8.8 %collective-permute-done.21.refs_11_ = bf16[192,768]{1,0:T(8,128)(2,1)S(1)} collective-permute-done((bf16[192,768]{1,0:T(8,128)(2,1)S(1)}, bf16[192,768]{1,0:T(8,128)(2,1)S(1)}, u32[]{:S(2)}, u32[]{:S(2)}) %collective-permute-start.21) | collective-permute-done | bytes 294944 | tf_op jit(solution)/shard_map/ppermute | solution.py:45
  80.9 1.5 collective-permute-start.22
  82.6 6.6 %collective-permute-done.22.refs_12_ = bf16[192,768]{1,0:T(8,128)(2,1)S(1)} collective-permute-done((bf16[192,768]{1,0:T(8,128)(2,1)S(1)}, bf16[192,768]{1,0:T(8,128)(2,1)S(1)}, u32[]{:S(2)}, u32[]{:S(2)}) %collective-permute-start.22) | collective-permute-done | bytes 294944 | tf_op jit(solution)/shard_map/ppermute | solution.py:45
  89.2 2.2 %shard_map.256 = (bf16[768,768]{1,0:T(8,128)(2,1)S(1)}, bf16[768,768]{1,0:T(8,128)(2,1)S(1)}, f32[256,768]{1,0:T(8,128)S(1)}, f32[256,1]{1,0:T(8,128)S(1)}, bf16...) custom-call(s32[3]{0:T(128)S(1)} %copy-done.4, ...), custom_call_target="tpu_custom_call" | custom-call | flops 603979776 | bytes 9069568 | tf_op jit(solution)/shard_map/pallas_call | solution.py:68
  91.5 1.4 collective-permute-done.23
  93.6 6.4 %collective-permute-done.24 = bf16[128,768]{1,0:T(8,128)(2,1)S(1)} collective-permute-done((bf16[128,768]{1,0:T(8,128)(2,1)S(1)}, bf16[128,768]{1,0:T(8,128)(2,1)S(1)}, u32[]{:S(2)}, u32[]{:S(2)}) %collective-permute-start.24) | collective-permute-done | bytes 196640 | tf_op jit(solution)/shard_map/ppermute | solution.py:50
  100.1 1.4 collective-permute-done.25.refs_2_
  101.5 2.7 %shard_map.257 = (bf16[256,768]{1,0:T(8,128)(2,1)}, f32[256,768]{1,0:T(8,128)S(1)}, bf16[256,768]{1,0:T(8,128)(2,1)S(1)}, bf16[256,768]{1,0:T(8,128)(2,1)S(1)}, ...) custom-call(s32[3]{0:T(128)S(1)} %copy-done.4, ...), custom_call_target="tpu_custom_call" | custom-call | flops 603979776 | bytes 7913472 | tf_op jit(solution)/shard_map/pallas_call | solution.py:68
  106.3 6.4 %collective-permute-done.27 = bf16[128,768]{1,0:T(8,128)(2,1)S(1)} collective-permute-done((bf16[128,768]{1,0:T(8,128)(2,1)S(1)}, bf16[128,768]{1,0:T(8,128)(2,1)S(1)}, u32[]{:S(2)}, u32[]{:S(2)}) %collective-permute-start.27) | collective-permute-done | bytes 196640 | tf_op jit(solution)/shard_map/ppermute | solution.py:50
  114.3 5.5 %shard_map.258 = (f32[256,768]{1,0:T(8,128)S(1)}, bf16[256,768]{1,0:T(8,128)(2,1)S(1)}, bf16[256,384]{1,0:T(8,128)(2,1)S(1)}, bf16[4,256,384]{2,1,0:T(8,128)(2,1...) custom-call(s32[3]{0:T(128)S(1)} %copy-done.4, ...), custom_call_target="tpu_custom_call" | custom-call | flops 1509949440 | bytes 9708544 | tf_op jit(solution)/shard_map/pallas_call | solution.py:68
  120.1 1.5 collective-permute-start.42
  123.5 2.0 %shard_map.262 = (bf16[392,768]{1,0:T(8,128)(2,1)S(1)}, bf16[392,768]{1,0:T(8,128)(2,1)S(1)}) custom-call(s32[3]{0:T(128)S(1)} %copy-done.4, bf16[256,768]{1,0:T(8,128)(2,1)S(1)} %bitcast.31, bf16[4,256,768]{2,1,0:T(8,128)(2,1)S(1)} %get-tuple-element.107.refs_2_, bf16[256,384]{1,0:T(8,128)(2,1)S(1)} %get-tuple-element.108.refs_3_, ...), custom_call_target="tpu_custom_call" | custom-call | flops 905969664 | bytes 4767744 | tf_op jit(solution)/shard_map/pallas_call | solution.py:68
  125.5 1.6 collective-permute-start.37
  127.1 9.2 %collective-permute-done.42.refs_5_ = bf16[256,1152]{1,0:T(8,128)(2,1)S(1)} collective-permute-done((bf16[256,1152]{1,0:T(8,128)(2,1)S(1)}, bf16[256,1152]{1,0:T(8,128)(2,1)S(1)}, u32[]{:S(2)}, u32[]{:S(2)}) %collective-permute-start.42) | collective-permute-done | bytes 589856 | tf_op jit(solution)/shard_map/ppermute | solution.py:45
  136.3 12.6 %collective-permute-done.43.refs_6_ = bf16[256,1152]{1,0:T(8,128)(2,1)S(1)} collective-permute-done((bf16[256,1152]{1,0:T(8,128)(2,1)S(1)}, bf16[256,1152]{1,0:T(8,128)(2,1)S(1)}, u32[]{:S(2)}, u32[]{:S(2)}) %collective-permute-start.43) | collective-permute-done | bytes 589856 | tf_op jit(solution)/shard_map/ppermute | solution.py:45
  148.9 1.5 shard_map.265
  154.4 3.1 %collective-permute-start.32 = (bf16[64,768]{1,0:T(8,128)(2,1)S(1)}, bf16[64,768]{1,0:T(8,128)(2,1)S(1)}, u32[]{:S(2)}, u32[]{:S(2)}) collective-permute-start(bf16[64,768]{1,0:T(8,128)(2,1)S(1)} %get-tuple-element.104), channel_id=1, source_target_pairs={{0,12},{4,0},{8,4},{12,8},{1,13},{5,1},{9,5},{13,9},{2,14},{6,2},{... | collective-permute-start | bytes 294920 | tf_op jit(solution)/shard_map/ppermute | solution.py:45
  157.6 1.5 collective-permute-done.46
  159.1 2.6 %collective-permute-start.33 = (bf16[64,768]{1,0:T(8,128)(2,1)S(1)}, bf16[64,768]{1,0:T(8,128)(2,1)S(1)}, u32[]{:S(2)}, u32[]{:S(2)}) collective-permute-start(bf16[64,768]{1,0:T(8,128)(2,1)S(1)} %get-tuple-element.105), channel_id=1, source_target_pairs={{0,8},{4,12},{8,0},{12,4},{1,9},{5,13},{9,1},{13,5},{2,10},{6,14},... | collective-permute-start | bytes 294920 | tf_op jit(solution)/shard_map/ppermute | solution.py:45
  164.0 3.5 %collective-permute-done.31 = bf16[64,768]{1,0:T(8,128)(2,1)S(1)} collective-permute-done((bf16[64,768]{1,0:T(8,128)(2,1)S(1)}, bf16[64,768]{1,0:T(8,128)(2,1)S(1)}, u32[]{:S(2)}, u32[]{:S(2)}) %collective-permute-start.31) | collective-permute-done | bytes 98336 | tf_op jit(solution)/shard_map/ppermute | solution.py:45
  167.5 2.2 %collective-permute-done.32 = bf16[64,768]{1,0:T(8,128)(2,1)S(1)} collective-permute-done((bf16[64,768]{1,0:T(8,128)(2,1)S(1)}, bf16[64,768]{1,0:T(8,128)(2,1)S(1)}, u32[]{:S(2)}, u32[]{:S(2)}) %collective-permute-start.32) | collective-permute-done | bytes 98336 | tf_op jit(solution)/shard_map/ppermute | solution.py:45
  169.7 2.2 %collective-permute-start.40 = (bf16[104,768]{1,0:T(8,128)(2,1)S(1)}, bf16[104,768]{1,0:T(8,128)(2,1)S(1)}, u32[]{:S(2)}, u32[]{:S(2)}) collective-permute-start(bf16[104,768]{1,0:T(8,128)(2,1)S(1)} %get-tuple-element.118), channel_id=1, source_target_pairs={{0,4},{12,8},{1,5},{13,9},{2,6},{14,10},{3,7},{15,11},{16,20},{28,... | collective-permute-start | bytes 479240 | tf_op jit(solution)/shard_map/ppermute | solution.py:544
  173.3 8.2 %collective-permute-done.40 = bf16[104,768]{1,0:T(8,128)(2,1)S(1)} collective-permute-done((bf16[104,768]{1,0:T(8,128)(2,1)S(1)}, bf16[104,768]{1,0:T(8,128)(2,1)S(1)}, u32[]{:S(2)}, u32[]{:S(2)}) %collective-permute-start.40) | collective-permute-done | bytes 159776 | tf_op jit(solution)/shard_map/ppermute | solution.py:544
  183.4 4.6 %collective-permute-start.41 = (bf16[104,768]{1,0:T(8,128)(2,1)S(1)}, bf16[104,768]{1,0:T(8,128)(2,1)S(1)}, u32[]{:S(2)}, u32[]{:S(2)}) collective-permute-start(bf16[104,768]{1,0:T(8,128)(2,1)S(1)} %add_convert_fusion.7), channel_id=1, source_target_pairs={{0,8},{4,12},{8,0},{12,4},{1,9},{5,13},{9,1},{13,5},{2,10},{6,14},... | collective-permute-start | bytes 479240 | tf_op jit(solution)/shard_map/ppermute | solution.py:45
  189.4 2.0 %collective-permute-done.39.refs_2_ = bf16[104,768]{1,0:T(8,128)(2,1)S(1)} collective-permute-done((bf16[104,768]{1,0:T(8,128)(2,1)S(1)}, bf16[104,768]{1,0:T(8,128)(2,1)S(1)}, u32[]{:S(2)}, u32[]{:S(2)}) %collective-permute-start.39) | collective-permute-done | bytes 159776 | tf_op jit(solution)/shard_map/ppermute | solution.py:546
  191.4 3.7 %collective-permute-done.41.refs_3_ = bf16[104,768]{1,0:T(8,128)(2,1)S(1)} collective-permute-done((bf16[104,768]{1,0:T(8,128)(2,1)S(1)}, bf16[104,768]{1,0:T(8,128)(2,1)S(1)}, u32[]{:S(2)}, u32[]{:S(2)}) %collective-permute-start.41) | collective-permute-done | bytes 159776 | tf_op jit(solution)/shard_map/ppermute | solution.py:45
  195.1 1.7 shard_map.264
  (90 shorter events, 26.1 us)
Async XLA Ops:
  1.6 8.5 %collective-permute-start.7 = (bf16[64,768]{1,0:T(8,128)(2,1)S(1)}, bf16[64,768]{1,0:T(8,128)(2,1)S(1)}, u32[]{:S(2)}, u32[]{:S(2)}) collective-permute-start(bf16[64,768]{1,0:T(8,128)(2,1)S(1)} %constant_dynamic-slice_fusion), channel_id=1, source_target_pairs={{0,4},{4,8},{8,12},{12,0},{1,5},{5,9},{9,13},{13,1},{2,6},{6,10},{... | collective-permute-start | bytes 294920 | tf_op jit(solution)/shard_map/ppermute | solution.py:45
  4.7 6.4 %collective-permute-start.8 = (bf16[64,768]{1,0:T(8,128)(2,1)S(1)}, bf16[64,768]{1,0:T(8,128)(2,1)S(1)}, u32[]{:S(2)}, u32[]{:S(2)}) collective-permute-start(bf16[64,768]{1,0:T(8,128)(2,1)S(1)} %constant_dynamic-slice_fusion), channel_id=1, source_target_pairs={{0,12},{4,0},{8,4},{12,8},{1,13},{5,1},{9,5},{13,9},{2,14},{6,2},{... | collective-permute-start | bytes 294920 | tf_op jit(solution)/shard_map/ppermute | solution.py:45
  6.8 9.0 %collective-permute-start.9 = (bf16[64,768]{1,0:T(8,128)(2,1)S(1)}, bf16[64,768]{1,0:T(8,128)(2,1)S(1)}, u32[]{:S(2)}, u32[]{:S(2)}) collective-permute-start(bf16[64,768]{1,0:T(8,128)(2,1)S(1)} %constant_dynamic-slice_fusion), channel_id=1, source_target_pairs={{0,8},{4,12},{8,0},{12,4},{1,9},{5,13},{9,1},{13,5},{2,10},{6,14},... | collective-permute-start | bytes 294920 | tf_op jit(solution)/shard_map/ppermute | solution.py:45
  15.8 13.4 %collective-permute-start.10 = (bf16[3,64,768]{2,1,0:T(8,128)(2,1)S(1)}, bf16[3,64,768]{2,1,0:T(8,128)(2,1)S(1)}, u32[]{:S(2)}, u32[]{:S(2)}) collective-permute-start(bf16[3,64,768]{2,1,0:T(8,128)(2,1)S(1)} %pad_maximum_fusion.refs_11_), channel_id=1, source_target_pairs={{0,2},{1,3},{2,0},{3,1},{4,6},{5,7},{6,4},{7,5},{8,10},{9,11},{10,... | collective-permute-start | bytes 884744 | tf_op jit(solution)/shard_map/ppermute | solution.py:50
  20.2 9.0 %collective-permute-start.1 = (bf16[104,768]{1,0:T(8,128)(2,1)}, bf16[104,768]{1,0:T(8,128)(2,1)S(1)}, u32[]{:S(2)}, u32[]{:S(2)}) collective-permute-start(bf16[104,768]{1,0:T(8,128)(2,1)} %shard_map.254.refs_2_), channel_id=1, source_target_pairs={{0,4},{4,8},{8,12},{12,0},{1,5},{5,9},{9,13},{13,1},{2,6},{6,10},{... | collective-permute-start | bytes 479240 | tf_op jit(solution)/shard_map/ppermute | solution.py:45
  20.2 9.9 %collective-permute-start.3 = (bf16[104,768]{1,0:T(8,128)(2,1)}, bf16[104,768]{1,0:T(8,128)(2,1)S(1)}, u32[]{:S(2)}, u32[]{:S(2)}) collective-permute-start(bf16[104,768]{1,0:T(8,128)(2,1)} %shard_map.254.refs_2_), channel_id=1, source_target_pairs={{0,12},{4,0},{8,4},{12,8},{1,13},{5,1},{9,5},{13,9},{2,14},{6,2},{... | collective-permute-start | bytes 479240 | tf_op jit(solution)/shard_map/ppermute | solution.py:45
  24.0 12.8 %collective-permute-start.5 = (bf16[104,768]{1,0:T(8,128)(2,1)}, bf16[104,768]{1,0:T(8,128)(2,1)S(1)}, u32[]{:S(2)}, u32[]{:S(2)}) collective-permute-start(bf16[104,768]{1,0:T(8,128)(2,1)} %shard_map.254.refs_2_), channel_id=1, source_target_pairs={{0,8},{4,12},{8,0},{12,4},{1,9},{5,13},{9,1},{13,5},{2,10},{6,14},... | collective-permute-start | bytes 479240 | tf_op jit(solution)/shard_map/ppermute | solution.py:45
  24.0 14.3 %collective-permute-start = (bf16[104,768]{1,0:T(8,128)(2,1)}, bf16[104,768]{1,0:T(8,128)(2,1)S(1)}, u32[]{:S(2)}, u32[]{:S(2)}) collective-permute-start(bf16[104,768]{1,0:T(8,128)(2,1)} %shard_map.254.refs_2_), channel_id=1, source_target_pairs={{0,16},{16,0},{1,17},{17,1},{2,18},{18,2},{3,19},{19,3},{4,20},{20... | collective-permute-start | bytes 479240 | tf_op jit(solution)/shard_map/ppermute | solution.py:45
  29.2 16.0 %collective-permute-start.11 = (bf16[3,64,768]{2,1,0:T(8,128)(2,1)S(1)}, bf16[3,64,768]{2,1,0:T(8,128)(2,1)S(1)}, u32[]{:S(2)}, u32[]{:S(2)}) collective-permute-start(bf16[3,64,768]{2,1,0:T(8,128)(2,1)S(1)} %pad_maximum_fusion.refs_11_), channel_id=1, source_target_pairs={{0,1},{1,0},{2,3},{3,2},{4,5},{5,4},{6,7},{7,6},{8,9},{9,8},{10,11... | collective-permute-start | bytes 884744 | tf_op jit(solution)/shard_map/ppermute | solution.py:50
  29.2 16.0 %collective-permute-start.12 = (bf16[3,64,768]{2,1,0:T(8,128)(2,1)S(1)}, bf16[3,64,768]{2,1,0:T(8,128)(2,1)S(1)}, u32[]{:S(2)}, u32[]{:S(2)}) collective-permute-start(bf16[3,64,768]{2,1,0:T(8,128)(2,1)S(1)} %collective-permute-done.10.refs_12_), channel_id=1, source_target_pairs={{0,1},{1,0},{2,3},{3,2},{4,5},{5,4},{6,7},{7,6},{8,9},{9,8},{10,11... | collective-permute-start | bytes 884744 | tf_op jit(solution)/shard_map/ppermute | solution.py:50
  30.1 8.8 %collective-permute-start.2 = (bf16[104,768]{1,0:T(8,128)(2,1)S(1)}, bf16[104,768]{1,0:T(8,128)(2,1)S(1)}, u32[]{:S(2)}, u32[]{:S(2)}) collective-permute-start(bf16[104,768]{1,0:T(8,128)(2,1)S(1)} %collective-permute-done.1.refs_4_), channel_id=1, source_target_pairs={{0,16},{16,0},{1,17},{17,1},{2,18},{18,2},{3,19},{19,3},{4,20},{20... | collective-permute-start | bytes 479240 | tf_op jit(solution)/shard_map/ppermute | solution.py:45
  36.8 6.7 %collective-permute-start.4 = (bf16[104,768]{1,0:T(8,128)(2,1)S(1)}, bf16[104,768]{1,0:T(8,128)(2,1)S(1)}, u32[]{:S(2)}, u32[]{:S(2)}) collective-permute-start(bf16[104,768]{1,0:T(8,128)(2,1)S(1)} %collective-permute-done.3.refs_6_), channel_id=1, source_target_pairs={{0,16},{16,0},{1,17},{17,1},{2,18},{18,2},{3,19},{19,3},{4,20},{20... | collective-permute-start | bytes 479240 | tf_op jit(solution)/shard_map/ppermute | solution.py:45
  38.3 6.9 %collective-permute-start.6 = (bf16[104,768]{1,0:T(8,128)(2,1)S(1)}, bf16[104,768]{1,0:T(8,128)(2,1)S(1)}, u32[]{:S(2)}, u32[]{:S(2)}) collective-permute-start(bf16[104,768]{1,0:T(8,128)(2,1)S(1)} %collective-permute-done.5.refs_8_), channel_id=1, source_target_pairs={{0,16},{16,0},{1,17},{17,1},{2,18},{18,2},{3,19},{19,3},{4,20},{20... | collective-permute-start | bytes 479240 | tf_op jit(solution)/shard_map/ppermute | solution.py:45
  52.6 4.0 %collective-permute-start.13 = (bf16[128,768]{1,0:T(8,128)(2,1)S(1)}, bf16[128,768]{1,0:T(8,128)(2,1)S(1)}, u32[]{:S(2)}, u32[]{:S(2)}) collective-permute-start(bf16[128,768]{1,0:T(8,128)(2,1)S(1)} %get-tuple-element.79), channel_id=1, source_target_pairs={{0,1},{1,0},{2,3},{3,2},{4,5},{5,4},{6,7},{7,6},{8,9},{9,8},{10,11... | collective-permute-start | bytes 589832 | tf_op jit(solution)/shard_map/ppermute | solution.py:50
  52.7 11.8 %collective-permute-start.17 = (bf16[192,768]{1,0:T(8,128)(2,1)S(1)}, bf16[192,768]{1,0:T(8,128)(2,1)S(1)}, u32[]{:S(2)}, u32[]{:S(2)}) collective-permute-start(bf16[192,768]{1,0:T(8,128)(2,1)S(1)} %pad_maximum_fusion.1.refs_5_), channel_id=1, source_target_pairs={{0,4},{4,8},{8,12},{12,0},{1,5},{5,9},{9,13},{13,1},{2,6},{6,10},{... | collective-permute-start | bytes 884744 | tf_op jit(solution)/shard_map/ppermute | solution.py:45
  52.8 17.9 %collective-permute-start.19 = (bf16[192,768]{1,0:T(8,128)(2,1)S(1)}, bf16[192,768]{1,0:T(8,128)(2,1)S(1)}, u32[]{:S(2)}, u32[]{:S(2)}) collective-permute-start(bf16[192,768]{1,0:T(8,128)(2,1)S(1)} %pad_maximum_fusion.1.refs_5_), channel_id=1, source_target_pairs={{0,12},{4,0},{8,4},{12,8},{1,13},{5,1},{9,5},{13,9},{2,14},{6,2},{... | collective-permute-start | bytes 884744 | tf_op jit(solution)/shard_map/ppermute | solution.py:45
  56.6 24.3 %collective-permute-start.21 = (bf16[192,768]{1,0:T(8,128)(2,1)S(1)}, bf16[192,768]{1,0:T(8,128)(2,1)S(1)}, u32[]{:S(2)}, u32[]{:S(2)}) collective-permute-start(bf16[192,768]{1,0:T(8,128)(2,1)S(1)} %pad_maximum_fusion.1.refs_5_), channel_id=1, source_target_pairs={{0,8},{4,12},{8,0},{12,4},{1,9},{5,13},{9,1},{13,5},{2,10},{6,14},... | collective-permute-start | bytes 884744 | tf_op jit(solution)/shard_map/ppermute | solution.py:45
  56.7 25.8 %collective-permute-start.14 = (bf16[128,768]{1,0:T(8,128)(2,1)S(1)}, bf16[128,768]{1,0:T(8,128)(2,1)S(1)}, u32[]{:S(2)}, u32[]{:S(2)}) collective-permute-start(bf16[128,768]{1,0:T(8,128)(2,1)S(1)} %add_convert_fusion.6), channel_id=1, source_target_pairs={{0,2},{1,3},{2,0},{3,1},{4,6},{5,7},{6,4},{7,5},{8,10},{9,11},{10,... | collective-permute-start | bytes 589832 | tf_op jit(solution)/shard_map/ppermute | solution.py:50
  57.2 25.4 %collective-permute-start.16 = (bf16[192,768]{1,0:T(8,128)(2,1)S(1)}, bf16[192,768]{1,0:T(8,128)(2,1)S(1)}, u32[]{:S(2)}, u32[]{:S(2)}) collective-permute-start(bf16[192,768]{1,0:T(8,128)(2,1)S(1)} %pad_maximum_fusion.1.refs_5_), channel_id=1, source_target_pairs={{0,16},{16,0},{1,17},{17,1},{2,18},{18,2},{3,19},{19,3},{4,20},{20... | collective-permute-start | bytes 884744 | tf_op jit(solution)/shard_map/ppermute | solution.py:45
  64.5 18.1 %collective-permute-start.18 = (bf16[192,768]{1,0:T(8,128)(2,1)S(1)}, bf16[192,768]{1,0:T(8,128)(2,1)S(1)}, u32[]{:S(2)}, u32[]{:S(2)}) collective-permute-start(bf16[192,768]{1,0:T(8,128)(2,1)S(1)} %collective-permute-done.17.refs_7_), channel_id=1, source_target_pairs={{0,16},{16,0},{1,17},{17,1},{2,18},{18,2},{3,19},{19,3},{4,20},{20... | collective-permute-start | bytes 884744 | tf_op jit(solution)/shard_map/ppermute | solution.py:45
  70.7 11.9 %collective-permute-start.20 = (bf16[192,768]{1,0:T(8,128)(2,1)S(1)}, bf16[192,768]{1,0:T(8,128)(2,1)S(1)}, u32[]{:S(2)}, u32[]{:S(2)}) collective-permute-start(bf16[192,768]{1,0:T(8,128)(2,1)S(1)} %collective-permute-done.19.refs_9_), channel_id=1, source_target_pairs={{0,16},{16,0},{1,17},{17,1},{2,18},{18,2},{3,19},{19,3},{4,20},{20... | collective-permute-start | bytes 884744 | tf_op jit(solution)/shard_map/ppermute | solution.py:45
  80.9 8.3 %collective-permute-start.22 = (bf16[192,768]{1,0:T(8,128)(2,1)S(1)}, bf16[192,768]{1,0:T(8,128)(2,1)S(1)}, u32[]{:S(2)}, u32[]{:S(2)}) collective-permute-start(bf16[192,768]{1,0:T(8,128)(2,1)S(1)} %collective-permute-done.21.refs_11_), channel_id=1, source_target_pairs={{0,16},{16,0},{1,17},{17,1},{2,18},{18,2},{3,19},{19,3},{4,20},{20... | collective-permute-start | bytes 884744 | tf_op jit(solution)/shard_map/ppermute | solution.py:45
  82.5 6.7 %collective-permute-start.15 = (bf16[128,768]{1,0:T(8,128)(2,1)S(1)}, bf16[128,768]{1,0:T(8,128)(2,1)S(1)}, u32[]{:S(2)}, u32[]{:S(2)}) collective-permute-start(bf16[128,768]{1,0:T(8,128)(2,1)S(1)} %add_convert_fusion.5.refs_1_), channel_id=1, source_target_pairs={{0,1},{1,0},{2,3},{3,2},{4,5},{5,4},{6,7},{7,6},{8,9},{9,8},{10,11... | collective-permute-start | bytes 589832 | tf_op jit(solution)/shard_map/ppermute | solution.py:50
  91.4 1.5 collective-permute-start.23
  93.0 7.0 %collective-permute-start.24 = (bf16[128,768]{1,0:T(8,128)(2,1)S(1)}, bf16[128,768]{1,0:T(8,128)(2,1)S(1)}, u32[]{:S(2)}, u32[]{:S(2)}) collective-permute-start(bf16[128,768]{1,0:T(8,128)(2,1)S(1)} %add_convert_fusion.4), channel_id=1, source_target_pairs={{0,2},{1,3},{2,0},{3,1},{4,6},{5,7},{6,4},{7,5},{8,10},{9,11},{10,... | collective-permute-start | bytes 589832 | tf_op jit(solution)/shard_map/ppermute | solution.py:50
  100.0 1.5 collective-permute-start.25
  104.3 1.4 collective-permute-start.26
  105.7 7.0 %collective-permute-start.27 = (bf16[128,768]{1,0:T(8,128)(2,1)S(1)}, bf16[128,768]{1,0:T(8,128)(2,1)S(1)}, u32[]{:S(2)}, u32[]{:S(2)}) collective-permute-start(bf16[128,768]{1,0:T(8,128)(2,1)S(1)} %add_convert_fusion.2), channel_id=1, source_target_pairs={{0,2},{1,3},{2,0},{3,1},{4,6},{5,7},{6,4},{7,5},{8,10},{9,11},{10,... | collective-permute-start | bytes 589832 | tf_op jit(solution)/shard_map/ppermute | solution.py:50
  112.8 1.5 collective-permute-start.28
  119.9 2.4 %collective-permute-start.29 = (bf16[4,128,768]{2,1,0:T(8,128)(2,1)S(1)}, bf16[4,128,768]{2,1,0:T(8,128)(2,1)S(1)}, u32[]{:S(2)}, u32[]{:S(2)}) collective-permute-start(bf16[4,128,768]{2,1,0:T(8,128)(2,1)S(1)} %get-tuple-element.99), channel_id=1, source_target_pairs={{0,1},{1,0},{2,3},{3,2},{4,5},{5,4},{6,7},{7,6},{8,9},{9,8},{10,11... | collective-permute-start | bytes 2359304 | tf_op jit(solution)/shard_map/ppermute | solution.py:50
  120.1 16.2 %collective-permute-start.42 = (bf16[256,1152]{1,0:T(8,128)(2,1)S(1)}, bf16[256,1152]{1,0:T(8,128)(2,1)S(1)}, u32[]{:S(2)}, u32[]{:S(2)}) collective-permute-start(bf16[256,1152]{1,0:T(8,128)(2,1)S(1)} %get-tuple-element.129), channel_id=1, source_target_pairs={{0,16},{16,0},{1,17},{17,1},{2,18},{18,2},{3,19},{19,3},{4,20},{20... | collective-permute-start | bytes 1769480 | tf_op jit(solution)/shard_map/ppermute | solution.py:45
  121.6 27.3 %collective-permute-start.43 = (bf16[256,1152]{1,0:T(8,128)(2,1)S(1)}, bf16[256,1152]{1,0:T(8,128)(2,1)S(1)}, u32[]{:S(2)}, u32[]{:S(2)}) collective-permute-start(bf16[256,1152]{1,0:T(8,128)(2,1)S(1)} %get-tuple-element.130), channel_id=1, source_target_pairs={{0,16},{16,0},{1,17},{17,1},{2,18},{18,2},{3,19},{19,3},{4,20},{20... | collective-permute-start | bytes 1769480 | tf_op jit(solution)/shard_map/ppermute | solution.py:45
  122.9 30.2 %collective-permute-start.30 = (bf16[4,64,768]{2,1,0:T(8,128)(2,1)S(1)}, bf16[4,64,768]{2,1,0:T(8,128)(2,1)S(1)}, u32[]{:S(2)}, u32[]{:S(2)}) collective-permute-start(bf16[4,64,768]{2,1,0:T(8,128)(2,1)S(1)} %get-tuple-element.101), channel_id=1, source_target_pairs={{0,2},{1,3},{2,0},{3,1},{4,6},{5,7},{6,4},{7,5},{8,10},{9,11},{10,... | collective-permute-start | bytes 1179656 | tf_op jit(solution)/shard_map/ppermute | solution.py:50
  125.5 36.3 %collective-permute-start.37 = (bf16[392,768]{1,0:T(8,128)(2,1)S(1)}, bf16[392,768]{1,0:T(8,128)(2,1)S(1)}, u32[]{:S(2)}, u32[]{:S(2)}) collective-permute-start(bf16[392,768]{1,0:T(8,128)(2,1)S(1)} %get-tuple-element.113), channel_id=1, source_target_pairs={{0,16},{16,0},{1,17},{17,1},{2,18},{18,2},{3,19},{19,3},{4,20},{20... | collective-permute-start | bytes 1806344 | tf_op jit(solution)/shard_map/ppermute | solution.py:45
  150.4 8.7 %collective-permute-start.46 = (bf16[2,96,768]{2,1,0:T(8,128)(2,1)S(1)}, bf16[2,96,768]{2,1,0:T(8,128)(2,1)S(1)}, u32[]{:S(2)}, u32[]{:S(2)}) collective-permute-start(bf16[2,96,768]{2,1,0:T(8,128)(2,1)S(1)} %get-tuple-element.135), channel_id=1, source_target_pairs={{0,4},{12,8},{1,5},{13,9},{2,6},{14,10},{3,7},{15,11},{16,20},{28,... | collective-permute-start | bytes 884744 | tf_op jit(solution)/shard_map/ppermute | solution.py:544
  151.7 30.3 %collective-permute-start.44 = (bf16[2,96,768]{2,1,0:T(8,128)(2,1)S(1)}, bf16[2,96,768]{2,1,0:T(8,128)(2,1)S(1)}, u32[]{:S(2)}, u32[]{:S(2)}) collective-permute-start(bf16[2,96,768]{2,1,0:T(8,128)(2,1)S(1)} %get-tuple-element.132), channel_id=1, source_target_pairs={{0,4},{4,8},{8,12},{1,5},{5,9},{9,13},{2,6},{6,10},{10,14},{3,7},{... | collective-permute-start | bytes 884744 | tf_op jit(solution)/shard_map/ppermute | solution.py:545
  153.7 13.8 %collective-permute-start.31 = (bf16[64,768]{1,0:T(8,128)(2,1)S(1)}, bf16[64,768]{1,0:T(8,128)(2,1)S(1)}, u32[]{:S(2)}, u32[]{:S(2)}) collective-permute-start(bf16[64,768]{1,0:T(8,128)(2,1)S(1)} %get-tuple-element.103), channel_id=1, source_target_pairs={{0,4},{4,8},{8,12},{12,0},{1,5},{5,9},{9,13},{13,1},{2,6},{6,10},{... | collective-permute-start | bytes 294920 | tf_op jit(solution)/shard_map/ppermute | solution.py:45
  154.4 15.2 %collective-permute-start.32 = (bf16[64,768]{1,0:T(8,128)(2,1)S(1)}, bf16[64,768]{1,0:T(8,128)(2,1)S(1)}, u32[]{:S(2)}, u32[]{:S(2)}) collective-permute-start(bf16[64,768]{1,0:T(8,128)(2,1)S(1)} %get-tuple-element.104), channel_id=1, source_target_pairs={{0,12},{4,0},{8,4},{12,8},{1,13},{5,1},{9,5},{13,9},{2,14},{6,2},{... | collective-permute-start | bytes 294920 | tf_op jit(solution)/shard_map/ppermute | solution.py:45
  159.1 12.8 %collective-permute-start.33 = (bf16[64,768]{1,0:T(8,128)(2,1)S(1)}, bf16[64,768]{1,0:T(8,128)(2,1)S(1)}, u32[]{:S(2)}, u32[]{:S(2)}) collective-permute-start(bf16[64,768]{1,0:T(8,128)(2,1)S(1)} %get-tuple-element.105), channel_id=1, source_target_pairs={{0,8},{4,12},{8,0},{12,4},{1,9},{5,13},{9,1},{13,5},{2,10},{6,14},... | collective-permute-start | bytes 294920 | tf_op jit(solution)/shard_map/ppermute | solution.py:45
  161.8 21.5 %collective-permute-start.45 = (bf16[2,96,768]{2,1,0:T(8,128)(2,1)S(1)}, bf16[2,96,768]{2,1,0:T(8,128)(2,1)S(1)}, u32[]{:S(2)}, u32[]{:S(2)}) collective-permute-start(bf16[2,96,768]{2,1,0:T(8,128)(2,1)S(1)} %get-tuple-element.133), channel_id=1, source_target_pairs={{4,0},{8,4},{12,8},{5,1},{9,5},{13,9},{6,2},{10,6},{14,10},{7,3},{... | collective-permute-start | bytes 884744 | tf_op jit(solution)/shard_map/ppermute | solution.py:546
  167.5 20.5 %collective-permute-start.47 = (bf16[2,96,768]{2,1,0:T(8,128)(2,1)S(1)}, bf16[2,96,768]{2,1,0:T(8,128)(2,1)S(1)}, u32[]{:S(2)}, u32[]{:S(2)}) collective-permute-start(bf16[2,96,768]{2,1,0:T(8,128)(2,1)S(1)} %add_convert_fusion), channel_id=1, source_target_pairs={{0,8},{4,12},{8,0},{12,4},{1,9},{5,13},{9,1},{13,5},{2,10},{6,14},... | collective-permute-start | bytes 884744 | tf_op jit(solution)/shard_map/ppermute | solution.py:45
  169.7 11.8 %collective-permute-start.40 = (bf16[104,768]{1,0:T(8,128)(2,1)S(1)}, bf16[104,768]{1,0:T(8,128)(2,1)S(1)}, u32[]{:S(2)}, u32[]{:S(2)}) collective-permute-start(bf16[104,768]{1,0:T(8,128)(2,1)S(1)} %get-tuple-element.118), channel_id=1, source_target_pairs={{0,4},{12,8},{1,5},{13,9},{2,6},{14,10},{3,7},{15,11},{16,20},{28,... | collective-permute-start | bytes 479240 | tf_op jit(solution)/shard_map/ppermute | solution.py:544
  171.9 17.4 %collective-permute-start.38 = (bf16[104,768]{1,0:T(8,128)(2,1)S(1)}, bf16[104,768]{1,0:T(8,128)(2,1)S(1)}, u32[]{:S(2)}, u32[]{:S(2)}) collective-permute-start(bf16[104,768]{1,0:T(8,128)(2,1)S(1)} %get-tuple-element.115), channel_id=1, source_target_pairs={{0,4},{4,8},{8,12},{1,5},{5,9},{9,13},{2,6},{6,10},{10,14},{3,7},{... | collective-permute-start | bytes 479240 | tf_op jit(solution)/shard_map/ppermute | solution.py:545
  181.5 6.5 %collective-permute-start.34 = (bf16[64,768]{1,0:T(8,128)(2,1)S(1)}, bf16[64,768]{1,0:T(8,128)(2,1)S(1)}, u32[]{:S(2)}, u32[]{:S(2)}) collective-permute-start(bf16[64,768]{1,0:T(8,128)(2,1)S(1)} %add_convert_fusion.8.refs_0_), channel_id=1, source_target_pairs={{0,2},{1,3},{2,0},{3,1},{4,6},{5,7},{6,4},{7,5},{8,10},{9,11},{10,... | collective-permute-start | bytes 294920 | tf_op jit(solution)/shard_map/ppermute | solution.py:50
  182.1 9.3 %collective-permute-start.39 = (bf16[104,768]{1,0:T(8,128)(2,1)S(1)}, bf16[104,768]{1,0:T(8,128)(2,1)S(1)}, u32[]{:S(2)}, u32[]{:S(2)}) collective-permute-start(bf16[104,768]{1,0:T(8,128)(2,1)S(1)} %get-tuple-element.116), channel_id=1, source_target_pairs={{4,0},{8,4},{12,8},{5,1},{9,5},{13,9},{6,2},{10,6},{14,10},{7,3},{... | collective-permute-start | bytes 479240 | tf_op jit(solution)/shard_map/ppermute | solution.py:546
  183.4 11.7 %collective-permute-start.41 = (bf16[104,768]{1,0:T(8,128)(2,1)S(1)}, bf16[104,768]{1,0:T(8,128)(2,1)S(1)}, u32[]{:S(2)}, u32[]{:S(2)}) collective-permute-start(bf16[104,768]{1,0:T(8,128)(2,1)S(1)} %add_convert_fusion.7), channel_id=1, source_target_pairs={{0,8},{4,12},{8,0},{12,4},{1,9},{5,13},{9,1},{13,5},{2,10},{6,14},... | collective-permute-start | bytes 479240 | tf_op jit(solution)/shard_map/ppermute | solution.py:45
  188.0 8.8 %collective-permute-start.35 = (bf16[64,768]{1,0:T(8,128)(2,1)S(1)}, bf16[64,768]{1,0:T(8,128)(2,1)S(1)}, u32[]{:S(2)}, u32[]{:S(2)}) collective-permute-start(bf16[64,768]{1,0:T(8,128)(2,1)S(1)} %add_convert_fusion.8.refs_0_), channel_id=1, source_target_pairs={{0,1},{1,0},{2,3},{3,2},{4,5},{5,4},{6,7},{7,6},{8,9},{9,8},{10,11... | collective-permute-start | bytes 294920 | tf_op jit(solution)/shard_map/ppermute | solution.py:50
  188.0 8.8 %collective-permute-start.36 = (bf16[64,768]{1,0:T(8,128)(2,1)S(1)}, bf16[64,768]{1,0:T(8,128)(2,1)S(1)}, u32[]{:S(2)}, u32[]{:S(2)}) collective-permute-start(bf16[64,768]{1,0:T(8,128)(2,1)S(1)} %collective-permute-done.34.refs_1_), channel_id=1, source_target_pairs={{0,1},{1,0},{2,3},{3,2},{4,5},{5,4},{6,7},{7,6},{8,9},{9,8},{10,11... | collective-permute-start | bytes 294920 | tf_op jit(solution)/shard_map/ppermute | solution.py:50
  (8 other events, 206.9 us)
